TPU v7x, 512 devices: a whole 4x8x8 slice. The times are simulated.
512 devices in a mesh: dp: 16 (over z, x_lo), mp: 32 (over x_hi, y, core).
Axes of the slice: x: 4 (x_hi: 2, x_lo: 2; x = x_hi * 2 + x_lo), y: 8, z: 8, core: 2. Of those that a mesh axis runs over, the one named last changes fastest.
Arguments:
- inputs: bfloat16 [197, 196608], P(None, ('dp', 'mp')), may hold values from -6 to 6
- cotangent: bfloat16 [197, 196608], P(None, ('dp', 'mp')), may hold values from -1.1953125 to 1.1953125
- w_in: bfloat16 [768, 3072], P('dp', 'mp'), may hold values from -0.21875 to 0.21875
- w_out: bfloat16 [3072, 768], P('mp', 'dp'), may hold values from -0.109375 to 0.109375
- prec_in: float32 [768, 3072], P('dp', 'mp'), may hold values from 0.1 to 2
- prec_out: float32 [3072, 768], P('mp', 'dp'), may hold values from 0.1 to 2
Outputs:
- new_prec_in: float32 [768, 3072], P('dp', 'mp')
- new_prec_out: float32 [3072, 768], P('mp', 'dp')
- new_w_in: float32 [768, 3072], P('dp', 'mp')
- new_w_out: float32 [3072, 768], P('mp', 'dp')
All inputs are finite; a program needn't handle non-finite values.
Results may differ from a plain program's by a relative error of at most 0.0028.
Values may be sent and summed in bfloat16 or wider, within the bound.
No kernel may reach another device: no remote copies, remote signals or barrier semaphores. Data moves between devices by JAX's collectives and lax.ppermute only.
A program may use at most 64 MiB of HBM per device.

v0:
```python
import jax
import jax.numpy as jnp
from jax import lax
from jax.sharding import Mesh
from jax.sharding import PartitionSpec as P

D = 768
SEQ = 197
MP = ("mp_0", "mp_1", "mp_2")
DP_MP = ("dp", "mp_0", "mp_1", "mp_2")


def rows_first(arrays, axis, dims):
    turned = [jnp.moveaxis(a, dim, 0) for a, dim in zip(arrays, dims)]
    both = jnp.concatenate([t.reshape(len(t), -1) for t in turned], axis=1)
    out, at, outs = (lax.all_gather(both, axis, axis=0, tiled=True), 0, [])
    for t, dim in zip(turned, dims):
        slab = out[:, at : at + t[0].size].reshape(-1, *t.shape[1:])
        outs.append(jnp.moveaxis(slab, 0, dim))
        at += t[0].size
    return tuple(outs)


def in_order(pieces, dim):
    pieces = jnp.moveaxis(pieces, 0, dim)
    lengths = pieces.shape
    return pieces.reshape(*lengths[:dim], lengths[dim] * lengths[dim + 1], *lengths[dim + 2 :])


def gather_in_order(array, axes, turns):
    pieces = array
    for k in turns:
        pieces = lax.all_gather(pieces, axes[k])
    done = turns[::-1]
    back = [done.index(k) for k in range(len(axes))]
    pieces = pieces.transpose(*back, *range(len(axes), pieces.ndim))
    return pieces.reshape(-1, *array.shape)


def whole_of(array, axes, turns, dim):
    return in_order(gather_in_order(array, axes, turns), dim)


def split_up(array, dim, size):
    before, after = (array.shape[:dim], array.shape[dim + 1 :])
    return jnp.moveaxis(array.reshape(*before, size, -1, *after), dim, 0)


def sum_at_owner(array, axis, dim):
    size = lax.axis_size(axis)
    pieces = lax.all_to_all(split_up(array, dim, size), axis, 0, 0, tiled=True)
    return jnp.sum(pieces, axis=0)


def sent_together(arrays, axis, dim, along):
    ends, at = ([], 0)
    for a in arrays[:-1]:
        at += a.shape[along]
        ends.append(at)
    both = jnp.concatenate(arrays, axis=along)
    return tuple(jnp.split(sum_at_owner(both, axis, dim), ends, axis=along))


def gelu_tanh(v):
    return jax.nn.gelu(v, approximate=True)


def per_device(inputs, cotangent, w_in, w_out, prec_in, prec_out):
    w_in_full, w_out_full = rows_first((w_in, w_out), "dp", (0, 1))
    whole = whole_of(inputs, MP, (0, 1, 2), 1)
    rows3 = whole.reshape(SEQ, -1, D)
    images = rows3.shape[1]
    pre = jnp.einsum("snd,dh->snh", rows3, w_in_full, preferred_element_type=jnp.float32)
    act = gelu_tanh(pre).astype(jnp.bfloat16)
    cot_whole = whole_of(cotangent, MP, (0, 1, 2), 1)
    cot3 = cot_whole.reshape(SEQ, images, D)
    back = jnp.einsum("snd,hd->snh", cot3, w_out_full, preferred_element_type=jnp.float32)
    per_out = jnp.einsum("snh,snd->nhd", act, cot3, preferred_element_type=jnp.float32)
    sum_out = jnp.sum(per_out, 0)
    sq_out = jnp.sum(per_out * per_out, 0)
    delta = jax.vjp(gelu_tanh, pre)[1](back)[0].astype(jnp.bfloat16)
    per_in = jnp.einsum("snd,snh->ndh", rows3, delta, preferred_element_type=jnp.float32)
    sum_in = jnp.sum(per_in, 0)
    sq_in = jnp.sum(per_in * per_in, 0)
    sum_in, sq_in = sent_together((sum_in, sq_in), "dp", 0, 1)
    sum_out, sq_out = sent_together((sum_out, sq_out), "dp", 1, 0)
    scale = 1.0 / (images * lax.axis_size("dp"))
    new_prec_in = 0.6 * prec_in + 0.4 * sq_in * scale
    new_prec_out = 0.6 * prec_out + 0.4 * sq_out * scale
    w_in_own = w_in.astype(jnp.float32)
    w_out_own = w_out.astype(jnp.float32)
    new_w_in = w_in_own - 1.0 * (sum_in * scale + 0.1 * w_in_own) / (new_prec_in + 0.1)
    new_w_out = w_out_own - 1.0 * (sum_out * scale + 0.1 * w_out_own) / (new_prec_out + 0.1)
    return (new_prec_in, new_prec_out, new_w_in, new_w_out)


def solution(mesh):
    torus = Mesh(mesh.devices.reshape(mesh.shape["dp"], 2, 8, 2), ("dp", "mp_0", "mp_1", "mp_2"))
    in_specs = (P(None, DP_MP), P(None, DP_MP), P("dp", MP), P(MP, "dp"), P("dp", MP), P(MP, "dp"))
    out_specs = (P("dp", MP), P(MP, "dp"), P("dp", MP), P(MP, "dp"))
    return jax.shard_map(
        per_device, mesh=torus, in_specs=in_specs, out_specs=out_specs, check_vma=False
    )
```

profile of v0, /device:TPU:56, one launch (start us, length us, event | category | flops | bytes accessed | tf_op | source)
XLA Modules:
  0.0 251.4 jit_solution(193393904579016392)
XLA Ops:
  7.2 0.0 all-gather.17.cloned.1.call-start
  7.2 10.2 %all-gather.7 = bf16[2,197,384]{2,1,0:T(8,128)(2,1)} all-gather(bf16[1,197,384]{2,1,0:T(8,128)(2,1)} %bitcast.85), channel_id=5, replica_groups=mesh['dp'=16,'mp_0'=2,'mp_1'=8,'mp_2'=2] {'mp_0'}, dimensions={0}, use_global_device_ids=true | all-gather | bytes 453888 | tf_op jit(solution)/shard_map/all_gather | solution.py:33
  17.4 0.0 all-gather.17.cloned.1.call-update
  17.4 0.0 all-gather.13.cloned.1.call-start
  17.4 7.7 %all-gather.6 = bf16[2,197,384]{2,1,0:T(8,128)(2,1)} all-gather(bf16[1,197,384]{2,1,0:T(8,128)(2,1)} %bitcast.86), channel_id=2, replica_groups=mesh['dp'=16,'mp_0'=2,'mp_1'=8,'mp_2'=2] {'mp_0'}, dimensions={0}, use_global_device_ids=true | all-gather | bytes 453888 | tf_op jit(solution)/shard_map/all_gather | solution.py:33
  25.1 0.0 all-gather.13.cloned.1.call-update
  25.2 0.0 all-gather.19.cloned.1.call-start
  25.2 38.4 %all-gather.17.cloned.1.call-done = bf16[16,197,384]{2,1,0:T(8,128)(2,1)} async-done(((bf16[2,197,384]{2,1,0:T(8,128)(2,1)}), bf16[16,197,384]{2,1,0:T(8,128)(2,1)}) %all-gather.17.cloned.1.call-update) | async-done | bytes 2420752 | tf_op jit(solution)/shard_map/all_gather | solution.py:33
  63.6 5.1 %copy.64 = bf16[8,2,197,384]{3,1,2,0:T(2,128)(2,1)} copy(bf16[8,2,197,384]{3,2,1,0:T(8,128)(2,1)} %bitcast.84) | data formatting | bytes 4841472 | tf_op jit(solution)/shard_map/all_gather | solution.py:33
  68.7 0.0 all-gather.19.cloned.1.call-update
  68.7 0.0 all-gather.15.cloned.1.call-start
  68.8 40.3 %all-gather.13.cloned.1.call-done = bf16[16,197,384]{2,1,0:T(8,128)(2,1)} async-done(((bf16[2,197,384]{2,1,0:T(8,128)(2,1)}), bf16[16,197,384]{2,1,0:T(8,128)(2,1)}) %all-gather.13.cloned.1.call-update) | async-done | bytes 2420752 | tf_op jit(solution)/shard_map/all_gather | solution.py:33
  109.1 5.0 %copy.58 = bf16[8,2,197,384]{3,1,2,0:T(2,128)(2,1)} copy(bf16[8,2,197,384]{3,2,1,0:T(8,128)(2,1)} %bitcast.83) | data formatting | bytes 4841472 | tf_op jit(solution)/shard_map/all_gather | solution.py:33
  114.1 0.0 copy-start
  114.1 0.0 copy-start.1
  114.1 0.0 all-gather.15.cloned.1.call-update
  114.1 0.7 copy-done
  114.8 0.0 copy-done.1
  114.8 0.1 pad_maximum_fusion.2
  114.9 36.9 %all_gather.39 = bf16[768,192]{1,0:T(8,128)(2,1)S(1)} all-gather(bf16[48,192]{1,0:T(8,128)(2,1)S(1)} %pad_maximum_fusion.2), channel_id=1, replica_groups=mesh['dp'=16,'mp_0'=2,'mp_1'=8,'mp_2'=2] {'dp'}, dimensions={0}, use_global_device_ids=true | all-gather | bytes 313344 | tf_op jit(solution)/shard_map/all_gather | solution.py:16
  151.8 0.0 all-gather.19.cloned.1.call-done
  151.8 3.7 %copy.95 = bf16[16,2,197,384]{3,0,2,1:T(8,128)(2,1)S(1)} copy(bf16[16,2,197,384]{3,1,2,0:T(2,128)(2,1)} %all-gather.19.cloned.1.call-done) | data formatting | bytes 9682944 | tf_op jit(solution)/shard_map/all_gather | solution.py:33
  155.5 1.1 copy.66
  156.6 2.8 %copy.67 = bf16[197,32,384]{2,1,0:T(8,128)(2,1)} copy(bf16[197,32,384]{2,0,1:T(8,128)(2,1)S(1)} %bitcast.79) | data formatting | bytes 9682944 | tf_op jit(solution)/shard_map/transpose | solution.py:25
  159.4 8.2 %reshape_reshape.7 = bf16[197,16,768]{2,1,0:T(8,128)(2,1)} reshape(bf16[197,32,384]{2,1,0:T(8,128)(2,1)} %copy.67) | data formatting | bytes 9682944 | tf_op jit(solution)/shard_map/reshape;reshape | solution.py:71
  167.6 0.0 all-gather.15.cloned.1.call-done
  167.6 3.0 %copy.96 = bf16[16,2,197,384]{3,0,2,1:T(8,128)(2,1)S(1)} copy(bf16[16,2,197,384]{3,1,2,0:T(2,128)(2,1)} %all-gather.15.cloned.1.call-done) | data formatting | bytes 9682944 | tf_op jit(solution)/shard_map/all_gather | solution.py:33
  170.6 1.1 copy.60
  171.7 2.8 %copy.61 = bf16[197,32,384]{2,1,0:T(8,128)(2,1)} copy(bf16[197,32,384]{2,0,1:T(8,128)(2,1)S(1)} %bitcast.80) | data formatting | bytes 9682944 | tf_op jit(solution)/shard_map/transpose | solution.py:25
  174.5 8.2 %reshape_reshape.6 = bf16[197,16,768]{2,1,0:T(8,128)(2,1)} reshape(bf16[197,32,384]{2,1,0:T(8,128)(2,1)} %copy.61) | data formatting | bytes 9682944 | tf_op jit(solution)/shard_map/reshape;reshape | solution.py:76
  182.7 4.4 %fusion.3 = f32[96,197,16]{1,0,2:T(8,128)S(1)} fusion(bf16[197,16,768]{2,1,0:T(8,128)(2,1)} %reshape_reshape.7, bf16[768,192]{1,0:T(8,128)(2,1)S(1)} %all_gather.39), kind=kOutput, calls=%fused_computation.8 | convolution fusion | flops 464781312 | bytes 6248448 | tf_op jit(solution)/shard_map/snd,dh->snh/dot_general | solution.py:73
  187.0 10.4 %bitcast_reduce_fusion = (f32[768,96]{0,1:T(8,128)S(1)}, f32[768,96]{0,1:T(8,128)S(1)}) fusion(bf16[197,16,768]{2,1,0:T(8,128)(2,1)} %reshape_reshape.7, f32[96,197,16]{1,0,2:T(8,128)S(1)} %fusion.3, bf16[197,16,768]{2,1,0:T(8,128)(2,1)} %reshape_reshape.6, bf16[768,192]{1,0:T(8,128)(2,1)S(1)} %all_gather.39), kind=kOutput, calls=%fused_computation.3 | convolution fusion | flops 939005952 | bytes 12042240 | tf_op jit(solution)/shard_map/snd,snh->ndh/dot_general | solution.py:82
  197.5 1.2 copy.70
  198.7 3.8 %all-to-all-start = ((f32[16,48,192]{2,1,0:T(8,128)}), f32[16,48,192]{2,1,0:T(8,128)S(1)}, u32[]{:S(2)}, u32[]{:S(2)}) async-start(f32[16,48,192]{2,1,0:T(8,128)} %bitcast.18), calls=%async_computation | async-start | bytes 1572864 | tf_op jit(solution)/shard_map/all_to_all | solution.py:51
  202.5 6.2 %fusion.52 = (f32[96,768]{1,0:T(8,128)S(1)}, f32[96,768]{1,0:T(8,128)S(1)}) fusion(bf16[197,16,768]{2,1,0:T(8,128)(2,1)} %reshape_reshape.6, f32[96,197,16]{1,0,2:T(8,128)S(1)} %fusion.3), kind=kOutput, calls=%fused_computation.69 | convolution fusion | flops 470896128 | bytes 6641664 | tf_op jit(solution)/shard_map/snh,snd->nhd/dot_general | solution.py:78
  208.8 0.0 copy-start.2
  208.8 1.2 copy.72
  209.9 11.8 %all-to-all-done = f32[16,48,192]{2,1,0:T(8,128)S(1)} async-done(((f32[16,48,192]{2,1,0:T(8,128)}), f32[16,48,192]{2,1,0:T(8,128)S(1)}, u32[]{:S(2)}, u32[]{:S(2)}) %all-to-all-start) | async-done | bytes 589856 | tf_op jit(solution)/shard_map/all_to_all | solution.py:51
  221.7 0.0 copy-start.3
  221.7 3.7 %all-to-all-start.1 = ((f32[16,192,48]{1,2,0:T(8,128)}), f32[16,192,48]{1,2,0:T(8,128)S(1)}, u32[]{:S(2)}, u32[]{:S(2)}) async-start(f32[16,192,48]{1,2,0:T(8,128)} %bitcast.20), calls=%async_computation.1 | async-start | bytes 1572864 | tf_op jit(solution)/shard_map/all_to_all | solution.py:51
  225.5 0.1 reduce_sum.56
  225.5 0.0 copy-done.2
  225.5 0.7 convert_subtract_fusion.1
  226.2 17.9 %all-to-all-done.1 = f32[16,192,48]{1,2,0:T(8,128)S(1)} async-done(((f32[16,192,48]{1,2,0:T(8,128)}), f32[16,192,48]{1,2,0:T(8,128)S(1)}, u32[]{:S(2)}, u32[]{:S(2)}) %all-to-all-start.1) | async-done | bytes 589856 | tf_op jit(solution)/shard_map/all_to_all | solution.py:51
  244.1 0.1 reduce_sum.59
  244.2 0.0 copy-done.3
  244.2 0.7 convert_subtract_fusion
  (2 shorter events, 0.1 us)
Async XLA Ops:
  7.2 56.5 %all-gather.17.cloned.1.call-start = ((), (), s32[]{:S(2)}) async-start(), calls=%async_computation.4 | async-start | bytes 2764800 | tf_op jit(solution)/shard_map/all_gather | solution.py:33
  17.4 91.7 %all-gather.13.cloned.1.call-start = ((), (), s32[]{:S(2)}) async-start(), calls=%async_computation.2 | async-start | bytes 2764800 | tf_op jit(solution)/shard_map/all_gather | solution.py:33
  25.2 126.6 %all-gather.19.cloned.1.call-start = ((), (), s32[]{:S(2)}) async-start(), calls=%async_computation.5 | async-start | bytes 7262208 | tf_op jit(solution)/shard_map/all_gather | solution.py:33
  68.7 98.9 %all-gather.15.cloned.1.call-start = ((), (), s32[]{:S(2)}) async-start(), calls=%async_computation.3 | async-start | bytes 7262208 | tf_op jit(solution)/shard_map/all_gather | solution.py:33
  114.1 0.7 copy-start
  114.1 0.7 copy-start.1
  198.7 23.0 %all-to-all-start = ((f32[16,48,192]{2,1,0:T(8,128)}), f32[16,48,192]{2,1,0:T(8,128)S(1)}, u32[]{:S(2)}, u32[]{:S(2)}) async-start(f32[16,48,192]{2,1,0:T(8,128)} %bitcast.18), calls=%async_computation | async-start | bytes 1572864 | tf_op jit(solution)/shard_map/all_to_all | solution.py:51
  208.8 16.8 %copy-start.2 = (f32[48,96]{1,0:T(8,128)S(1)}, f32[48,96]{1,0:T(8,128)}, u32[]{:S(2)}) copy-start(f32[48,96]{1,0:T(8,128)} %param.10) | copy-start | bytes 55300
  221.7 22.5 %copy-start.3 = (f32[96,48]{0,1:T(8,128)S(1)}, f32[96,48]{0,1:T(8,128)}, u32[]{:S(2)}) copy-start(f32[96,48]{0,1:T(8,128)} %param.11) | copy-start | bytes 55300
  221.7 22.4 %all-to-all-start.1 = ((f32[16,192,48]{1,2,0:T(8,128)}), f32[16,192,48]{1,2,0:T(8,128)S(1)}, u32[]{:S(2)}, u32[]{:S(2)}) async-start(f32[16,192,48]{1,2,0:T(8,128)} %bitcast.20), calls=%async_computation.1 | async-start | bytes 1572864 | tf_op jit(solution)/shard_map/all_to_all | solution.py:51
Sparse Core Ops, SparseCore 0:
  17.5 46.0 all-gather.16
  65.7 43.2 all-gather.12
  111.2 22.1 all-gather.18
  135.3 24.0 all-gather.14
where the time goes:
time: 256 us; the launch traced here: 251 us
  waiting for transfers between devices  108 us (42%)
  blocking collectives  54.8 us (21%)
  local copies, waits for them, and re-layouts  44 us (17%)
  matrix products  21 us (8%)
  between operations  13.9 us (5%)
  starting transfers between devices  7.74 us (3%)
    all_gather x4, waiting for transfers between devices, gather_in_order(): pieces = lax.all_gather(pieces, axes[k])  78.7 us
    all_gather x1, blocking collectives, rows_first(): out, at, outs = (lax.all_gather(both, axis, axis=0, tiled=True), 0, [])  36.9 us
    all_to_all x2, waiting for transfers between devices, sum_at_owner(): pieces = lax.all_to_all(split_up(array, dim, size), axis, 0, 0, tiled=True)  29.6 us
    all_gather x2, blocking collectives, gather_in_order(): pieces = lax.all_gather(pieces, axes[k])  17.9 us
    all_gather x4, local copies, waits for them, and re-layouts, gather_in_order(): pieces = lax.all_gather(pieces, axes[k])  16.8 us
    dot_general x1, matrix products, per_device(): jnp.einsum('snd,snh->ndh', rows3, delta, preferred_element_type=jnp.float32)  10.4 us
    another operation x1, local copies, waits for them, and re-layouts, per_device(): rows3 = whole.reshape(SEQ, -1, D)  8.19 us
    another operation x1, local copies, waits for them, and re-layouts, per_device(): cot3 = cot_whole.reshape(SEQ, images, D)  8.17 us
  transfers between devices with their start and end apart: 6, of which 4 were waited for; matrix products, arithmetic and copies ran while one was open for 14% of the time, Pallas kernels for 0%

commit v1 on v0

v1 whole, which is shorter than its diff:
```python
import functools
import math
import jax
import jax.numpy as jnp
from jax import lax
from jax.experimental import pallas as pl
from jax.experimental.pallas import tpu as pltpu
from jax.sharding import Mesh
from jax.sharding import PartitionSpec as P

AXES = ("z", "xlo", "xhi", "y", "core")
DP = ("z", "xlo")
MP = ("xhi", "y", "core")
GROUP = ("y", "core")
OWNERS = ("xhi", "z", "xlo")
BF16 = jnp.bfloat16
F32 = jnp.float32
ROOT = math.sqrt(2.0 / math.pi)
CUBE = 0.044715


def gelu_parts(v):
    v2 = v * v
    t = jnp.tanh(ROOT * v * (1.0 + CUBE * v2))
    half = 0.5 * (1.0 + t)
    slope = half + 0.5 * v * (1.0 - t * t) * (ROOT * (1.0 + 3.0 * CUBE * v2))
    return v * half, slope


def grads_kernel(x_ref, c_ref, w_in_ref, w_out_ref, out_ref, sum_in, sq_in, sum_out, sq_out):
    step = pl.program_id(0)

    def dot(a, b, dims):
        return lax.dot_general(a, b, (dims, ((), ())), preferred_element_type=F32)

    x = jnp.concatenate([x_ref[0], x_ref[1]], axis=1)
    c = jnp.concatenate([c_ref[0], c_ref[1]], axis=1)
    pre = dot(w_in_ref[...], x, ((1,), (1,)))
    back = dot(w_out_ref[...], c, ((1,), (1,)))
    act, slope = gelu_parts(pre)
    act = act.astype(BF16)
    delta = (back * slope).astype(BF16)
    g_in = dot(delta, x, ((1,), (0,)))
    g_out = dot(act, c, ((1,), (0,)))

    @pl.when(step == 0)
    def _():
        sum_in[...] = g_in
        sq_in[...] = g_in * g_in
        sum_out[...] = g_out
        sq_out[...] = g_out * g_out

    @pl.when(step > 0)
    def _():
        sum_in[...] += g_in
        sq_in[...] += g_in * g_in
        sum_out[...] += g_out
        sq_out[...] += g_out * g_out

    @pl.when(step == pl.num_programs(0) - 1)
    def _():
        width = out_ref.shape[2] // 4
        for h in range(out_ref.shape[0]):
            rows = slice(h * width, (h + 1) * width)
            both = [r[rows, :] for r in (sum_in, sq_in, sum_out, sq_out)]
            out_ref[h] = jnp.concatenate(both, axis=0).T.astype(BF16)


def grads(x, c, w_in_t, w_out, blocks):
    hid, d = w_in_t.shape
    pieces, seq, part = x.shape
    per = d // part
    image = pl.BlockSpec((per, seq, part), lambda i: (i, 0, 0))
    whole = pl.BlockSpec((hid, d), lambda i: (0, 0))
    shape = (blocks, d, 4 * hid // blocks)
    return pl.pallas_call(
        grads_kernel,
        grid=(pieces // per,),
        in_specs=[image, image, whole, whole],
        out_specs=pl.BlockSpec(shape, lambda i: (0, 0, 0)),
        out_shape=jax.ShapeDtypeStruct(shape, BF16),
        scratch_shapes=[pltpu.VMEM((hid, d), F32)] * 4,
        compiler_params=pltpu.CompilerParams(vmem_limit_bytes=48 << 20),
    )(x, c, w_in_t, w_out)


def per_device(inputs, cotangent, w_in, w_out, prec_in, prec_out):
    d_own, h_own = w_in.shape
    blocks = lax.axis_size("xhi")
    dp = lax.axis_size("z") * lax.axis_size("xlo")
    both = jnp.concatenate([w_in, w_out.T], axis=0)
    weights = lax.all_gather(both, OWNERS)
    weights = weights.reshape(blocks, dp, 2, d_own, h_own).transpose(2, 0, 4, 1, 3)
    weights = weights.reshape(2, blocks * h_own, dp * d_own)
    x = lax.all_gather(inputs, GROUP)
    c = lax.all_gather(cotangent, GROUP)
    partial = grads(x, c, weights[0], weights[1], blocks)
    pieces = partial.reshape(blocks * dp, d_own, 4 * h_own)
    pieces = lax.all_to_all(pieces, OWNERS, 0, 0, tiled=True)
    total = jnp.sum(pieces.astype(F32), axis=0)
    sum_in, sq_in, sum_out, sq_out = jnp.split(total, 4, axis=1)
    images = x.shape[0] * x.shape[2] // (dp * d_own) * blocks * dp
    scale = 1.0 / images
    new_prec_in = 0.6 * prec_in + 0.4 * sq_in * scale
    new_prec_out = 0.6 * prec_out + 0.4 * sq_out.T * scale
    w_in_own = w_in.astype(F32)
    w_out_own = w_out.astype(F32)
    new_w_in = w_in_own - 1.0 * (sum_in * scale + 0.1 * w_in_own) / (new_prec_in + 0.1)
    new_w_out = w_out_own - 1.0 * (sum_out.T * scale + 0.1 * w_out_own) / (new_prec_out + 0.1)
    return (new_prec_in, new_prec_out, new_w_in, new_w_out)


def solution(mesh):
    torus = Mesh(mesh.devices.reshape(8, 2, 2, 8, 2), AXES)
    dp_mp = DP + MP
    in_specs = (P(None, dp_mp), P(None, dp_mp), P(DP, MP), P(MP, DP), P(DP, MP), P(MP, DP))
    out_specs = (P(DP, MP), P(MP, DP), P(DP, MP), P(MP, DP))
    return jax.shard_map(
        per_device, mesh=torus, in_specs=in_specs, out_specs=out_specs, check_vma=False
    )
```

time: 256 us -> 164 us (0.64); the launches traced: 251 us -> 162 us
  waiting for transfers between devices: 108 us -> 5.55 us
  blocking collectives: 54.8 us -> 128 us
  local copies, waits for them, and re-layouts: 44 us -> 3.79 us
  matrix products: 21 us -> 0 us
  Pallas kernels: 0 us -> 8.65 us
  starting transfers between devices: 7.74 us -> 0.08 us
    all_gather x4 -> x2, waiting for transfers between devices: 78.7 us -> 4.18 us  [the longest x1 4.16 us: per_device(): c = lax.all_gather(cotangent, GROUP)]
    all_to_all x0 -> x1, blocking collectives: none -> 44 us  [per_device(): pieces = lax.all_to_all(pieces, OWNERS, 0, 0, tiled=True)]
    all_to_all x2 -> x0, waiting for transfers between devices: 29.6 us -> none  [sum_at_owner(): pieces = lax.all_to_all(split_up(array, dim, size), axis, 0, 0, tiled=True)]
    all_gather x3 -> x1, blocking collectives: 54.8 us -> 83.6 us  [per_device(): weights = lax.all_gather(both, OWNERS)]
    dot_general x3 -> x0, matrix products: 21 us -> none  [the longest x1 10.4 us: per_device(): jnp.einsum('snd,snh->ndh', rows3, delta, preferred_element_type=jnp.float32)]
    all_gather x4 -> x0, local copies, waits for them, and re-layouts: 16.8 us -> none  [gather_in_order(): pieces = lax.all_gather(pieces, axes[k])]
    another operation x2 -> x0, local copies, waits for them, and re-layouts: 16.4 us -> none  [the longest x1 8.19 us: per_device(): rows3 = whole.reshape(SEQ, -1, D)]
    pallas_call x0 -> x1, Pallas kernels: none -> 8.65 us  [grads(): pl.pallas_call(grads_kernel, grid=(pieces // per,), in_specs=[image, imag...]
  transfers between devices with their start and end apart: 6 -> 2, of which waited for: 4 -> 1; matrix products, arithmetic and copies ran while one was open for 14% -> 2% of each run, Pallas kernels for 0% -> 0%
where the time goes in v1:
time: 164 us; the launch traced here: 162 us
  blocking collectives  128 us (78%)
  between operations  14.1 us (9%)
  Pallas kernels  8.65 us (5%)
  waiting for transfers between devices  5.55 us (3%)
  local copies, waits for them, and re-layouts  3.79 us (2%)
  other arithmetic  2.29 us (1%)
    all_gather x1, blocking collectives, per_device(): weights = lax.all_gather(both, OWNERS)  83.6 us
    all_to_all x1, blocking collectives, per_device(): pieces = lax.all_to_all(pieces, OWNERS, 0, 0, tiled=True)  44 us
    pallas_call x1, Pallas kernels, grads(): pl.pallas_call(grads_kernel, grid=(pieces // per,), in_specs=[image, imag...  8.65 us
    all_gather x1, waiting for transfers between devices, per_device(): c = lax.all_gather(cotangent, GROUP)  4.16 us
  transfers between devices with their start and end apart: 2, of which 1 were waited for; matrix products, arithmetic and copies ran while one was open for 2% of the time, Pallas kernels for 0%

profile of v1, /device:TPU:56, one launch (start us, length us, event | category | flops | bytes accessed | tf_op | source)
XLA Modules:
  0.0 162.1 jit_solution(4384593025472626738)
XLA Ops:
  7.2 0.0 all-gather.8.cloned.1.call-start
  7.2 0.7 all-gather.8.cloned.1.call-update
  7.9 0.0 all-gather.10.cloned.1.call-start
  7.9 0.7 all-gather.10.cloned.1.call-update
  8.6 0.7 pad_maximum_fusion
  9.4 83.6 %all-gather.2 = bf16[3072,96]{1,0:T(8,128)(2,1)S(1)} all-gather(bf16[96,96]{1,0:T(8,128)(2,1)S(1)} %pad_maximum_fusion), channel_id=4, replica_groups=mesh['z'=8,'xlo'=2,'xhi'=2,'y'=8,'core'=2] {'xhi','z','xlo'}, dimensions={0}, use_global_device_ids=true | all-gather | bytes 608256 | tf_op jit(solution)/shard_map/all_gather | solution.py:92
  93.0 0.8 copy.18
  93.8 0.5 fusion.10
  94.3 0.2 squeeze.7
  94.5 0.2 copy.16.w_out_ref
  94.7 0.2 squeeze.6
  94.9 0.2 copy.15.w_in_ref
  95.1 0.0 all-gather.8.cloned.1.call-done.x_ref
  95.1 4.2 %all-gather.10.cloned.1.call-done.c_ref = bf16[16,197,384]{2,1,0:T(8,128)(2,1)} async-done(((bf16[1,197,384]{2,1,0:T(8,128)(2,1)}), bf16[16,197,384]{2,1,0:T(8,128)(2,1)}) %all-gather.10.cloned.1.call-update) | async-done | bytes 2420752 | tf_op jit(solution)/shard_map/all_gather | solution.py:96
  99.3 0.0 copy-start
  99.3 1.7 %copy-done = bf16[16,197,384]{2,1,0:T(8,128)(2,1)S(1)} copy-done((bf16[16,197,384]{2,1,0:T(8,128)(2,1)S(1)}, bf16[16,197,384]{2,1,0:T(8,128)(2,1)}, u32[]{:S(2)}) %copy-start) | copy-done | bytes 2420760
  101.0 8.6 %shard_map.93 = bf16[2,768,384]{2,1,0:T(8,128)(2,1)S(1)} custom-call(bf16[16,197,384]{2,1,0:T(8,128)(2,1)S(1)} %copy-done, bf16[16,197,384]{2,1,0:T(8,128)(2,1)} %all-gather.10.cloned.1.call-done.c_ref, bf16[192,768]{1,0:T(8,128)(2,1)S(1)} %copy.15.w_in_ref, bf16[192,768]{1,0:T(8,128)(2,1)S(1)} %copy.16.w_out_ref), custom_call_target="tpu_custom_call" | custom-call | tf_op jit(solution)/shard_map/pallas_call | solution.py:76
  109.6 0.0 copy-start.1
  109.6 0.0 copy-start.3
  109.6 0.0 copy-start.2
  109.7 0.0 copy-start.4
  109.7 44.0 %all_to_all.5 = bf16[32,48,384]{2,1,0:T(8,128)(2,1)S(1)} all-to-all(bf16[32,48,384]{2,1,0:T(8,128)(2,1)S(1)} %bitcast.21), channel_id=1, replica_groups=mesh['z'=8,'xlo'=2,'xhi'=2,'y'=8,'core'=2] {'xhi','z','xlo'}, dimensions={0} | all-to-all | bytes 2359296 | tf_op jit(solution)/shard_map/all_to_all | solution.py:99
  153.7 0.2 convert_reduce_fusion
  153.9 0.0 copy-done.1
  153.9 0.0 copy-done.3
  153.9 0.7 convert_subtract_fusion
  154.6 0.0 copy-done.2
  154.6 0.0 copy-done.4
  154.6 0.7 convert_subtract_fusion.1
Async XLA Ops:
  7.2 87.9 %all-gather.8.cloned.1.call-start = ((), (), s32[]{:S(2)}) async-start(), calls=%async_computation.1 | async-start | bytes 2611200 | tf_op jit(solution)/shard_map/all_gather | solution.py:95
  7.9 91.4 %all-gather.10.cloned.1.call-start = ((), (), s32[]{:S(2)}) async-start(), calls=%async_computation.2 | async-start | bytes 2611200 | tf_op jit(solution)/shard_map/all_gather | solution.py:96
  99.3 1.7 %copy-start = (bf16[16,197,384]{2,1,0:T(8,128)(2,1)S(1)}, bf16[16,197,384]{2,1,0:T(8,128)(2,1)}, u32[]{:S(2)}) copy-start(bf16[16,197,384]{2,1,0:T(8,128)(2,1)} %all-gather.8.cloned.1.call-done.x_ref) | copy-start | bytes 7262212
  109.6 44.3 %copy-start.1 = (bf16[96,48]{0,1:T(8,128)(2,1)S(1)}, bf16[96,48]{0,1:T(8,128)(2,1)}, u32[]{:S(2)}) copy-start(bf16[96,48]{0,1:T(8,128)(2,1)} %param.9) | copy-start | bytes 27652
  109.6 44.3 %copy-start.3 = (f32[96,48]{0,1:T(8,128)S(1)}, f32[96,48]{0,1:T(8,128)}, u32[]{:S(2)}) copy-start(f32[96,48]{0,1:T(8,128)} %param.11) | copy-start | bytes 55300
  109.6 45.0 %copy-start.2 = (bf16[48,96]{1,0:T(8,128)(2,1)S(1)}, bf16[48,96]{1,0:T(8,128)(2,1)}, u32[]{:S(2)}) copy-start(bf16[48,96]{1,0:T(8,128)(2,1)} %param.8) | copy-start | bytes 27652
  109.7 44.9 %copy-start.4 = (f32[48,96]{1,0:T(8,128)S(1)}, f32[48,96]{1,0:T(8,128)}, u32[]{:S(2)}) copy-start(f32[48,96]{1,0:T(8,128)} %param.10) | copy-start | bytes 55300
Sparse Core Ops, SparseCore 0:
  10.1 45.3 all-gather.7
  57.7 41.5 all-gather.9

commit v2 on v1

--- a/solution.py
+++ b/solution.py
@@ -13,6 +13,7 @@
 MP = ("xhi", "y", "core")
 GROUP = ("y", "core")
 OWNERS = ("xhi", "z", "xlo")
+ROW = ("xhi", "xlo")
 BF16 = jnp.bfloat16
 F32 = jnp.float32
 ROOT = math.sqrt(2.0 / math.pi)
@@ -27,14 +28,14 @@
     return v * half, slope
 
 
-def grads_kernel(x_ref, c_ref, w_in_ref, w_out_ref, out_ref, sum_in, sq_in, sum_out, sq_out):
+def grads_kernel(xc_ref, w_in_ref, w_out_ref, out_ref, sum_in, sq_in, sum_out, sq_out):
     step = pl.program_id(0)
 
     def dot(a, b, dims):
         return lax.dot_general(a, b, (dims, ((), ())), preferred_element_type=F32)
 
-    x = jnp.concatenate([x_ref[0], x_ref[1]], axis=1)
-    c = jnp.concatenate([c_ref[0], c_ref[1]], axis=1)
+    x = jnp.concatenate([xc_ref[0, 0], xc_ref[1, 0]], axis=1)
+    c = jnp.concatenate([xc_ref[0, 1], xc_ref[1, 1]], axis=1)
     pre = dot(w_in_ref[...], x, ((1,), (1,)))
     back = dot(w_out_ref[...], c, ((1,), (1,)))
     act, slope = gelu_parts(pre)
@@ -59,47 +60,49 @@
 
     @pl.when(step == pl.num_programs(0) - 1)
     def _():
-        width = out_ref.shape[2] // 4
-        for h in range(out_ref.shape[0]):
-            rows = slice(h * width, (h + 1) * width)
-            both = [r[rows, :] for r in (sum_in, sq_in, sum_out, sq_out)]
-            out_ref[h] = jnp.concatenate(both, axis=0).T.astype(BF16)
+        cols, pairs, deep, rows, packed = out_ref.shape
+        width = packed // 4
+        for h in range(cols):
+            part = slice(h * width, (h + 1) * width)
+            both = [r[part, :] for r in (sum_in, sq_in, sum_out, sq_out)]
+            turned = jnp.concatenate(both, axis=0).T.astype(BF16)
+            for k in range(deep * pairs):
+                out_ref[h, k % pairs, k // pairs] = turned[k * rows : (k + 1) * rows]
 
 
-def grads(x, c, w_in_t, w_out, blocks):
+def grads(xc, w_in_t, w_out, shape):
     hid, d = w_in_t.shape
-    pieces, seq, part = x.shape
+    pieces, two, seq, part = xc.shape
     per = d // part
-    image = pl.BlockSpec((per, seq, part), lambda i: (i, 0, 0))
     whole = pl.BlockSpec((hid, d), lambda i: (0, 0))
-    shape = (blocks, d, 4 * hid // blocks)
     return pl.pallas_call(
         grads_kernel,
         grid=(pieces // per,),
-        in_specs=[image, image, whole, whole],
-        out_specs=pl.BlockSpec(shape, lambda i: (0, 0, 0)),
+        in_specs=[pl.BlockSpec((per, two, seq, part), lambda i: (i, 0, 0, 0)), whole, whole],
+        out_specs=pl.BlockSpec(shape, lambda i: (0,) * len(shape)),
         out_shape=jax.ShapeDtypeStruct(shape, BF16),
         scratch_shapes=[pltpu.VMEM((hid, d), F32)] * 4,
         compiler_params=pltpu.CompilerParams(vmem_limit_bytes=48 << 20),
-    )(x, c, w_in_t, w_out)
+    )(xc, w_in_t, w_out)
 
 
 def per_device(inputs, cotangent, w_in, w_out, prec_in, prec_out):
     d_own, h_own = w_in.shape
-    blocks = lax.axis_size("xhi")
-    dp = lax.axis_size("z") * lax.axis_size("xlo")
+    cols, pairs, deep = (lax.axis_size(a) for a in ("xhi", "xlo", "z"))
+    dp = deep * pairs
+    xc = lax.all_gather(jnp.stack([inputs, cotangent]), GROUP)
     both = jnp.concatenate([w_in, w_out.T], axis=0)
-    weights = lax.all_gather(both, OWNERS)
-    weights = weights.reshape(blocks, dp, 2, d_own, h_own).transpose(2, 0, 4, 1, 3)
-    weights = weights.reshape(2, blocks * h_own, dp * d_own)
-    x = lax.all_gather(inputs, GROUP)
-    c = lax.all_gather(cotangent, GROUP)
-    partial = grads(x, c, weights[0], weights[1], blocks)
-    pieces = partial.reshape(blocks * dp, d_own, 4 * h_own)
-    pieces = lax.all_to_all(pieces, OWNERS, 0, 0, tiled=True)
+    both = jnp.broadcast_to(both[None], (cols * dp, *both.shape))
+    weights = lax.all_to_all(both, OWNERS, 0, 0, tiled=True)
+    weights = weights.reshape(cols, dp, 2, d_own, h_own).transpose(2, 0, 4, 1, 3)
+    weights = weights.reshape(2, cols * h_own, dp * d_own)
+    pieces = grads(xc, weights[0], weights[1], (cols, pairs, deep, d_own, 4 * h_own))
+    pieces = lax.all_to_all(pieces.reshape(cols * pairs, deep, d_own, 4 * h_own), ROW, 0, 0, tiled=True)
+    pieces = sum(pieces[k].astype(F32) for k in range(cols * pairs)).astype(BF16)
+    pieces = lax.all_to_all(pieces, "z", 0, 0, tiled=True)
     total = jnp.sum(pieces.astype(F32), axis=0)
     sum_in, sq_in, sum_out, sq_out = jnp.split(total, 4, axis=1)
-    images = x.shape[0] * x.shape[2] // (dp * d_own) * blocks * dp
+    images = xc.shape[0] * xc.shape[3] // (dp * d_own) * cols * dp
     scale = 1.0 / images
     new_prec_in = 0.6 * prec_in + 0.4 * sq_in * scale
     new_prec_out = 0.6 * prec_out + 0.4 * sq_out.T * scale

time: 164 us -> 118 us (0.72)
  blocking collectives: 128 us -> 77.4 us
  waiting for transfers between devices: 5.55 us -> 8.73 us
  other arithmetic: 2.29 us -> 4.07 us
    all_gather x1 -> x0, blocking collectives: 83.6 us -> none  [per_device(): weights = lax.all_gather(both, OWNERS)]
    all_to_all x1 -> x3, blocking collectives: 44 us -> 77.4 us  [the longest x1 37.4 us: per_device(): weights = lax.all_to_all(both, OWNERS, 0, 0, tiled=True)]
    all_gather x2 -> x1, waiting for transfers between devices: 4.18 us -> 8.71 us  [per_device(): xc = lax.all_gather(jnp.stack([inputs, cotangent]), GROUP)]
    squeeze x4, local copies, waits for them, and re-layouts: 0.72 us -> 2.74 us  [the longest x2 1.37 us: per_device(): weights[0]]
    another operation x0 -> x1, other arithmetic: none -> 1.75 us  [per_device(): xc = lax.all_gather(jnp.stack([inputs, cotangent]), GROUP)]
    unnamed x10 -> x8, local copies, waits for them, and re-layouts: 1.72 us -> 0.01 us
  transfers between devices with their start and end apart: 2 -> 1, of which waited for: 1 -> 1; matrix products, arithmetic and copies ran while one was open for 2% -> 3% of each run, Pallas kernels for 0% -> 0%
where the time goes in v2:
time: 118 us; the launch traced here: 116 us
  blocking collectives  77.4 us (66%)
  between operations  14.1 us (12%)
  Pallas kernels  9.2 us (8%)
  waiting for transfers between devices  8.73 us (7%)
  other arithmetic  4.07 us (3%)
  local copies, waits for them, and re-layouts  2.9 us (2%)
    all_to_all x1, blocking collectives, per_device(): weights = lax.all_to_all(both, OWNERS, 0, 0, tiled=True)  37.4 us
    all_to_all x1, blocking collectives, per_device(): lax.all_to_all(pieces.reshape(cols * pairs, deep, d_own, 4 * h_own), ROW,...  21 us
    all_to_all x1, blocking collectives, per_device(): pieces = lax.all_to_all(pieces, 'z', 0, 0, tiled=True)  19 us
    pallas_call x1, Pallas kernels, grads(): pl.pallas_call(grads_kernel, grid=(pieces // per,), in_specs=[pl.BlockSpe...  9.2 us
    all_gather x1, waiting for transfers between devices, per_device(): xc = lax.all_gather(jnp.stack([inputs, cotangent]), GROUP)  8.71 us
  transfers between devices with their start and end apart: 1, of which 1 were waited for; matrix products, arithmetic and copies ran while one was open for 3% of the time, Pallas kernels for 0%

profile of v2, /device:TPU:56, one launch (start us, length us, event | category | flops | bytes accessed | tf_op | source)
XLA Modules:
  0.0 116.4 jit_solution(10998772386992169442)
XLA Ops:
  7.2 0.0 all-gather.3.cloned.1.call-start
  7.2 1.8 %pad_maximum_fusion = bf16[2,197,384]{2,1,0:T(8,128)(2,1)} fusion(bf16[1,197,384]{2,1,0:T(8,128)(2,1)} %bitcast.26, bf16[1,197,384]{2,1,0:T(8,128)(2,1)} %bitcast.27), kind=kLoop, calls=%fused_computation.2 | loop fusion | flops 151296 | bytes 605184 | tf_op jit(solution)/shard_map/stack | solution.py:93
  9.0 0.0 all-gather.3.cloned.1.call-update
  9.0 0.7 pad_maximum_fusion.1
  9.7 0.1 broadcast_in_dim.2
  9.8 37.4 %all_to_all.15 = bf16[32,96,96]{2,1,0:T(8,128)(2,1)S(1)} all-to-all(bf16[32,96,96]{2,1,0:T(8,128)(2,1)S(1)} %broadcast_in_dim.2), channel_id=1, replica_groups=mesh['z'=8,'xlo'=2,'xhi'=2,'y'=8,'core'=2] {'xhi','z','xlo'}, dimensions={0} | all-to-all | bytes 1179648 | tf_op jit(solution)/shard_map/all_to_all | solution.py:96
  47.2 0.1 fusion.11
  47.3 0.6 copy.19
  47.9 0.8 reshape.32.w_out_ref
  48.7 0.6 copy.18
  49.3 0.8 reshape.31.w_in_ref
  50.0 8.7 %all-gather.3.cloned.1.call-done = bf16[32,197,384]{2,1,0:T(8,128)(2,1)} async-done(((bf16[2,197,384]{2,1,0:T(8,128)(2,1)}), bf16[32,197,384]{2,1,0:T(8,128)(2,1)}) %all-gather.3.cloned.1.call-update) | async-done | bytes 4841488 | tf_op jit(solution)/shard_map/all_gather | solution.py:93
  58.7 9.2 %shard_map.93 = bf16[2,2,8,48,384]{4,3,2,1,0:T(8,128)(2,1)S(1)} custom-call(bf16[16,2,197,384]{3,2,1,0:T(8,128)(2,1)} %bitcast.24, bf16[192,768]{1,0:T(8,128)(2,1)S(1)} %reshape.31.w_in_ref, bf16[192,768]{1,0:T(8,128)(2,1)S(1)} %reshape.32.w_out_ref), custom_call_target="tpu_custom_call" | custom-call | tf_op jit(solution)/shard_map/pallas_call | solution.py:78
  68.0 21.0 %all_to_all.16 = bf16[4,8,48,384]{3,2,1,0:T(8,128)(2,1)S(1)} all-to-all(bf16[4,8,48,384]{3,2,1,0:T(8,128)(2,1)S(1)} %bitcast.23), channel_id=1, replica_groups=mesh['z'=8,'xlo'=2,'xhi'=2,'y'=8,'core'=2] {'xhi','xlo'}, dimensions={0} | all-to-all | bytes 2359296 | tf_op jit(solution)/shard_map/all_to_all | solution.py:100
  88.9 0.0 copy-start
  88.9 0.0 copy-start.2
  88.9 0.0 copy-start.1
  88.9 0.0 copy-start.3
  88.9 0.2 fusion
  89.1 19.0 %all_to_all.17 = bf16[8,48,384]{2,1,0:T(8,128)(2,1)S(1)} all-to-all(bf16[8,48,384]{2,1,0:T(8,128)(2,1)S(1)} %fusion), channel_id=1, replica_groups=mesh['z'=8,'xlo'=2,'xhi'=2,'y'=8,'core'=2] {'z'}, dimensions={0} | all-to-all | bytes 589824 | tf_op jit(solution)/shard_map/all_to_all | solution.py:102
  108.1 0.0 copy-done
  108.1 0.0 copy-done.2
  108.2 0.7 convert_subtract_fusion
  108.9 0.0 copy-done.1
  108.9 0.0 copy-done.3
  108.9 0.7 convert_subtract_fusion.1
  (1 shorter events, 0.0 us)
Async XLA Ops:
  7.2 51.6 %all-gather.3.cloned.1.call-start = ((), (), s32[]{:S(2)}) async-start(), calls=%async_computation.3 | async-start | bytes 5222400 | tf_op jit(solution)/shard_map/all_gather | solution.py:93
  88.9 19.2 %copy-start = (bf16[96,48]{0,1:T(8,128)(2,1)S(1)}, bf16[96,48]{0,1:T(8,128)(2,1)}, u32[]{:S(2)}) copy-start(bf16[96,48]{0,1:T(8,128)(2,1)} %param.9) | copy-start | bytes 27652
  88.9 19.2 %copy-start.2 = (f32[96,48]{0,1:T(8,128)S(1)}, f32[96,48]{0,1:T(8,128)}, u32[]{:S(2)}) copy-start(f32[96,48]{0,1:T(8,128)} %param.11) | copy-start | bytes 55300
  88.9 19.9 %copy-start.1 = (bf16[48,96]{1,0:T(8,128)(2,1)S(1)}, bf16[48,96]{1,0:T(8,128)(2,1)}, u32[]{:S(2)}) copy-start(bf16[48,96]{1,0:T(8,128)(2,1)} %param.8) | copy-start | bytes 27652
  88.9 19.9 %copy-start.3 = (f32[48,96]{1,0:T(8,128)S(1)}, f32[48,96]{1,0:T(8,128)}, u32[]{:S(2)}) copy-start(f32[48,96]{1,0:T(8,128)} %param.10) | copy-start | bytes 55300
Sparse Core Ops, SparseCore 0:
  10.1 48.5 all-gather.2

commit v3 on v2

v3 whole, which is shorter than its diff:
```python
import math
import jax
import jax.numpy as jnp
from jax import lax
from jax.experimental import pallas as pl
from jax.experimental.pallas import tpu as pltpu
from jax.sharding import Mesh
from jax.sharding import PartitionSpec as P

AXES = ("z", "xlo", "xhi", "y", "core")
DP = ("z", "xlo")
MP = ("xhi", "y", "core")
GROUP = ("y", "core")
OWNERS = ("xhi", "z", "xlo")
ROW = ("xhi", "xlo")
BF16 = jnp.bfloat16
F32 = jnp.float32
ROOT = math.sqrt(2.0 / math.pi)
CUBE = 0.044715


def gelu_parts(v):
    v2 = v * v
    t = jnp.tanh(ROOT * v * (1.0 + CUBE * v2))
    half = 0.5 * (1.0 + t)
    slope = half + 0.5 * v * (1.0 - t * t) * (ROOT * (1.0 + 3.0 * CUBE * v2))
    return v * half, slope


def image_grads(core_ref, own_ref, far_ref, w_in_ref, w_out_ref):
    def dot(a, b, dims):
        return lax.dot_general(a, b, (dims, ((), ())), preferred_element_type=F32)

    first = core_ref[0] == 0

    def whole(k):
        own, far = own_ref[k], far_ref[k]
        return jnp.concatenate(
            [jnp.where(first, own, far), jnp.where(first, far, own)], axis=1
        )

    x, c = whole(0), whole(1)
    pre = dot(w_in_ref[...], x, ((1,), (1,)))
    back = dot(w_out_ref[...], c, ((1,), (1,)))
    act, slope = gelu_parts(pre)
    act = act.astype(BF16)
    delta = (back * slope).astype(BF16)
    return dot(delta, x, ((1,), (0,))), dot(act, c, ((1,), (0,)))


def add_image(sums, g_in, g_out):
    for ref, term in zip(sums, (g_in, g_in * g_in, g_out, g_out * g_out)):
        ref[...] += term


def first_kernel(core_ref, own_ref, far_ref, w_in_ref, w_out_ref, *sums):
    @pl.when(pl.program_id(0) == 0)
    def _():
        for ref in sums:
            ref[...] = jnp.zeros_like(ref)

    add_image(sums, *image_grads(core_ref, own_ref, far_ref, w_in_ref, w_out_ref))


def last_kernel(core_ref, own_ref, far_ref, w_in_ref, w_out_ref, s0, s1, s2, s3, out_ref, *sums):
    step = pl.program_id(0)

    @pl.when(step == 0)
    def _():
        for ref, start in zip(sums, (s0, s1, s2, s3)):
            ref[...] = start[...]

    add_image(sums, *image_grads(core_ref, own_ref, far_ref, w_in_ref, w_out_ref))

    @pl.when(step == pl.num_programs(0) - 1)
    def _():
        cols, pairs, deep, rows, packed = out_ref.shape
        width = packed // 4
        for h in range(cols):
            part = slice(h * width, (h + 1) * width)
            turned = jnp.concatenate([r[part, :] for r in sums], axis=0).T.astype(BF16)
            for k in range(deep * pairs):
                out_ref[h, k % pairs, k // pairs] = turned[k * rows : (k + 1) * rows]


def run_images(kernel, core, own, far, w_in_t, w_out, sums, out_shape):
    pieces, seq, part = own.shape
    hid, d = w_in_t.shape
    images = pieces // 2
    last = images - 1
    block = (2, seq, part)
    whole = pl.BlockSpec((hid, d), lambda i: (0, 0))
    final = bool(sums)
    out_specs = (
        pl.BlockSpec(out_shape, lambda i: (0,) * len(out_shape)) if final else [whole] * 4
    )
    outs = (
        jax.ShapeDtypeStruct(out_shape, BF16)
        if final
        else [jax.ShapeDtypeStruct((hid, d), F32)] * 4
    )
    return pl.pallas_call(
        kernel,
        grid=(images,),
        in_specs=[
            pl.BlockSpec(memory_space=pltpu.SMEM),
            pl.BlockSpec(block, lambda i: (i, 0, 0)),
            pl.BlockSpec(block, lambda i: (jnp.where(i < last, i ^ 1, i), 0, 0)),
            whole,
            whole,
        ]
        + [whole] * len(sums),
        out_specs=out_specs,
        out_shape=outs,
        scratch_shapes=[pltpu.VMEM((hid, d), F32)] * (4 if final else 0),
        compiler_params=pltpu.CompilerParams(vmem_limit_bytes=40 << 20),
        cost_estimate=pl.CostEstimate(
            flops=images * 8 * seq * hid * d,
            bytes_accessed=images * 8 * seq * part,
            transcendentals=images * seq * hid,
        ),
    )(core, own, far, w_in_t, w_out, *sums)


def round_the_ring(own, weights):
    n, cores = lax.axis_size("y"), lax.axis_size("core")

    def turned(step):
        return [
            (y * cores + k, (y + (step if k == 0 else -step)) % n * cores + k)
            for y in range(n)
            for k in range(cores)
        ]

    def swap(a):
        pairs = [(y * cores + k, y * cores + 1 - k) for y in range(n) for k in range(cores)]
        return lax.ppermute(a, GROUP, pairs)

    up, down = [own], [own]
    for _ in range(n // 2 - 1):
        up.append(lax.ppermute(up[-1], GROUP, turned(1)))
        down.append(lax.ppermute(down[-1], GROUP, turned(-1)))
    up[3], down[3], weights = lax.optimization_barrier((up[3], down[3], weights))
    opposite = [lax.ppermute(up[3][:1], GROUP, turned(1)), lax.ppermute(down[3][1:], GROUP, turned(-1))]
    early = jnp.concatenate([up[1], down[1], up[2], down[2], own])
    late = jnp.concatenate([up[3], down[3], *opposite])
    return (early, swap(early)), (late, swap(late)), weights


def per_device(inputs, cotangent, w_in, w_out, prec_in, prec_out):
    d_own, h_own = w_in.shape
    cols, pairs, deep = (lax.axis_size(a) for a in ("xhi", "xlo", "z"))
    dp = deep * pairs
    both = jnp.concatenate([w_in, w_out.T], axis=0)
    both = jnp.broadcast_to(both[None], (cols * dp, *both.shape))
    weights = lax.all_to_all(both, OWNERS, 0, 0, tiled=True)
    weights = weights.reshape(cols, dp, 2, d_own, h_own).transpose(2, 0, 4, 1, 3)
    weights = weights.reshape(2, cols * h_own, dp * d_own)
    early, late, weights = round_the_ring(jnp.stack([inputs, cotangent]), weights)
    core = lax.axis_index("core").reshape(1).astype(jnp.int32)
    shape = (cols, pairs, deep, d_own, 4 * h_own)
    sums = run_images(first_kernel, core, *early, weights[0], weights[1], (), shape)
    pieces = run_images(last_kernel, core, *late, weights[0], weights[1], tuple(sums), shape)
    pieces = lax.all_to_all(pieces.reshape(cols * pairs, *shape[2:]), ROW, 0, 0, tiled=True)
    pieces = sum(pieces[k].astype(F32) for k in range(cols * pairs))
    pieces = lax.all_to_all(pieces, "z", 0, 0, tiled=True)
    total = jnp.sum(pieces, axis=0)
    sum_in, sq_in, sum_out, sq_out = jnp.split(total, 4, axis=1)
    scale = 1.0 / (lax.axis_size("y") * cols * dp)
    new_prec_in = 0.6 * prec_in + 0.4 * sq_in * scale
    new_prec_out = 0.6 * prec_out + 0.4 * sq_out.T * scale
    w_in_own = w_in.astype(F32)
    w_out_own = w_out.astype(F32)
    new_w_in = w_in_own - 1.0 * (sum_in * scale + 0.1 * w_in_own) / (new_prec_in + 0.1)
    new_w_out = w_out_own - 1.0 * (sum_out.T * scale + 0.1 * w_out_own) / (new_prec_out + 0.1)
    return (new_prec_in, new_prec_out, new_w_in, new_w_out)


def solution(mesh):
    torus = Mesh(mesh.devices.reshape(8, 2, 2, 8, 2), AXES)
    dp_mp = DP + MP
    in_specs = (P(None, dp_mp), P(None, dp_mp), P(DP, MP), P(MP, DP), P(DP, MP), P(MP, DP))
    out_specs = (P(DP, MP), P(MP, DP), P(DP, MP), P(MP, DP))
    return jax.shard_map(
        per_device, mesh=torus, in_specs=in_specs, out_specs=out_specs, check_vma=False
    )
```

time: 118 us -> 129 us (1.093)
  the two profiles are of different devices: /device:TPU:56 before, /device:TPU:16 now
where the time goes in v3:
time: 129 us
  starting transfers between devices  43.4 us (34%)
  blocking collectives  41.1 us (32%)
  waiting for transfers between devices  21.2 us (16%)
  local copies, waits for them, and re-layouts  10.7 us (8%)
  Pallas kernels  7.89 us (6%)
  other arithmetic  3.32 us (3%)
    all_to_all x1, blocking collectives, per_device(): pieces = lax.all_to_all(pieces, 'z', 0, 0, tiled=True)  21.2 us
    all_to_all x1, blocking collectives, per_device(): lax.all_to_all(pieces.reshape(cols * pairs, *shape[2:]), ROW, 0, 0, tiled...  19.9 us
    ppermute x3, starting transfers between devices, round_the_ring(): up.append(lax.ppermute(up[-1], GROUP, turned(1)))  12.9 us
    all_to_all x1, waiting for transfers between devices, per_device(): weights = lax.all_to_all(both, OWNERS, 0, 0, tiled=True)  11.8 us
    all_to_all x1, starting transfers between devices, per_device(): weights = lax.all_to_all(both, OWNERS, 0, 0, tiled=True)  10.8 us
    ppermute x3, starting transfers between devices, round_the_ring(): down.append(lax.ppermute(down[-1], GROUP, turned(-1)))  8.69 us
    pallas_call x2, Pallas kernels, run_images(): pl.pallas_call(kernel, grid=(images,), in_specs=[pl.BlockSpec(memory_spac...  7.89 us
    ppermute x1, starting transfers between devices, round_the_ring(): lax.ppermute(up[3][:1], GROUP, turned(1))  5.3 us
  transfers between devices with their start and end apart: 11, of which 3 were waited for; matrix products, arithmetic and copies ran while one was open for 9% of the time, Pallas kernels for 4%

profile of v3, /device:TPU:16, one launch (start us, length us, event | category | flops | bytes accessed | tf_op | source)
XLA Modules:
  0.0 128.5 jit_solution(2566778633581822050)
XLA Ops:
  0.6 1.0 pad_maximum_fusion
  1.7 3.5 %collective-permute-start = (bf16[2,197,384]{2,1,0:T(8,128)(2,1)S(1)}, bf16[2,197,384]{2,1,0:T(8,128)(2,1)S(1)}, u32[]{:S(2)}, u32[]{:S(2)}) collective-permute-start(bf16[2,197,384]{2,1,0:T(8,128)(2,1)S(1)} %pad_maximum_fusion), channel_id=1, source_target_pairs={{0,2},{1,15},{2,4},{3,1},{4,6},{5,3},{6,8},{7,5},{8,10},{9,7},{10,... | collective-permute-start | bytes 907784 | tf_op jit(solution)/shard_map/ppermute | solution.py:141
  5.2 2.4 %collective-permute-start.3 = (bf16[2,197,384]{2,1,0:T(8,128)(2,1)S(1)}, bf16[2,197,384]{2,1,0:T(8,128)(2,1)S(1)}, u32[]{:S(2)}, u32[]{:S(2)}) collective-permute-start(bf16[2,197,384]{2,1,0:T(8,128)(2,1)S(1)} %pad_maximum_fusion), channel_id=1, source_target_pairs={{0,14},{1,3},{2,0},{3,5},{4,2},{5,7},{6,4},{7,9},{8,6},{9,11},{10,... | collective-permute-start | bytes 907784 | tf_op jit(solution)/shard_map/ppermute | solution.py:142
  7.5 5.2 %collective-permute-done = bf16[2,197,384]{2,1,0:T(8,128)(2,1)S(1)} collective-permute-done((bf16[2,197,384]{2,1,0:T(8,128)(2,1)S(1)}, bf16[2,197,384]{2,1,0:T(8,128)(2,1)S(1)}, u32[]{:S(2)}, u32[]{:S(2)}) %collective-permute-start) | collective-permute-done | bytes 302624 | tf_op jit(solution)/shard_map/ppermute | solution.py:141
  12.8 3.8 %collective-permute-start.1 = (bf16[2,197,384]{2,1,0:T(8,128)(2,1)S(1)}, bf16[2,197,384]{2,1,0:T(8,128)(2,1)}, u32[]{:S(2)}, u32[]{:S(2)}) collective-permute-start(bf16[2,197,384]{2,1,0:T(8,128)(2,1)S(1)} %collective-permute-done), channel_id=1, source_target_pairs={{0,2},{1,15},{2,4},{3,1},{4,6},{5,3},{6,8},{7,5},{8,10},{9,7},{10,... | collective-permute-start | bytes 907784 | tf_op jit(solution)/shard_map/ppermute | solution.py:141
  16.5 0.0 collective-permute-done.3
  16.6 4.4 %collective-permute-start.4 = (bf16[2,197,384]{2,1,0:T(8,128)(2,1)S(1)}, bf16[2,197,384]{2,1,0:T(8,128)(2,1)}, u32[]{:S(2)}, u32[]{:S(2)}) collective-permute-start(bf16[2,197,384]{2,1,0:T(8,128)(2,1)S(1)} %collective-permute-done.3), channel_id=1, source_target_pairs={{0,14},{1,3},{2,0},{3,5},{4,2},{5,7},{6,4},{7,9},{8,6},{9,11},{10,... | collective-permute-start | bytes 907784 | tf_op jit(solution)/shard_map/ppermute | solution.py:142
  21.0 0.7 pad_maximum_fusion.1
  21.7 1.0 broadcast_in_dim.2
  22.7 10.8 %all-to-all-start = ((bf16[32,96,96]{2,1,0:T(8,128)(2,1)}), bf16[32,96,96]{2,1,0:T(8,128)(2,1)S(1)}, u32[]{:S(2)}, u32[]{:S(2)}) async-start(bf16[32,96,96]{2,1,0:T(8,128)(2,1)} %broadcast_in_dim.2), calls=%async_computation | async-start | bytes 1572864 | tf_op jit(solution)/shard_map/all_to_all | solution.py:156
  33.5 0.0 copy-start
  33.5 0.0 copy-start.1
  33.6 0.1 constant_dynamic-update-slice_fusion.8
  33.6 0.0 collective-permute-done.1
  33.6 5.6 %collective-permute-start.2 = (bf16[2,197,384]{2,1,0:T(8,128)(2,1)}, bf16[2,197,384]{2,1,0:T(8,128)(2,1)S(1)}, u32[]{:S(2)}, u32[]{:S(2)}) collective-permute-start(bf16[2,197,384]{2,1,0:T(8,128)(2,1)} %collective-permute-done.1), channel_id=1, source_target_pairs={{0,2},{1,15},{2,4},{3,1},{4,6},{5,3},{6,8},{7,5},{8,10},{9,7},{10,... | collective-permute-start | bytes 907784 | tf_op jit(solution)/shard_map/ppermute | solution.py:141
  39.3 0.0 collective-permute-done.4
  39.3 1.9 %collective-permute-start.5 = (bf16[2,197,384]{2,1,0:T(8,128)(2,1)}, bf16[2,197,384]{2,1,0:T(8,128)(2,1)}, u32[]{:S(2)}, u32[]{:S(2)}) collective-permute-start(bf16[2,197,384]{2,1,0:T(8,128)(2,1)} %collective-permute-done.4), channel_id=1, source_target_pairs={{0,14},{1,3},{2,0},{3,5},{4,2},{5,7},{6,4},{7,9},{8,6},{9,11},{10,... | collective-permute-start | bytes 907784 | tf_op jit(solution)/shard_map/ppermute | solution.py:142
  41.2 1.0 constant_dynamic-update-slice_fusion.7
  42.2 1.0 constant_dynamic-update-slice_fusion.6
  43.2 0.0 copy-done
  43.3 0.0 copy-done.1
  43.3 1.9 %collective-permute-start.9 = (bf16[10,197,384]{2,1,0:T(8,128)(2,1)S(1)}, bf16[10,197,384]{2,1,0:T(8,128)(2,1)}, u32[]{:S(2)}, u32[]{:S(2)}) collective-permute-start(bf16[10,197,384]{2,1,0:T(8,128)(2,1)S(1)} %constant_dynamic-update-slice_fusion.4.own_ref), channel_id=1, source_target_pairs={{0,1},{1,0},{2,3},{3,2},{4,5},{5,4},{6,7},{7,6},{8,9},{9,8},{10,11... | collective-permute-start | bytes 4538888 | tf_op jit(solution)/shard_map/ppermute | solution.py:137
  45.3 11.8 %all-to-all-done = bf16[32,96,96]{2,1,0:T(8,128)(2,1)S(1)} async-done(((bf16[32,96,96]{2,1,0:T(8,128)(2,1)}), bf16[32,96,96]{2,1,0:T(8,128)(2,1)S(1)}, u32[]{:S(2)}, u32[]{:S(2)}) %all-to-all-start) | async-done | bytes 589856 | tf_op jit(solution)/shard_map/all_to_all | solution.py:156
  57.1 0.8 copy.10
  57.9 1.4 %reshape.30 = bf16[2,192,768]{1,2,0:T(8,128)(2,1)} reshape(bf16[2,2,96,16,48]{2,1,4,3,0:T(2,128)(2,1)S(1)} %copy.10) | data formatting | bytes 1179648 | tf_op jit(solution)/shard_map/reshape | solution.py:158
  59.3 0.0 collective-permute-done.2
  59.3 0.0 collective-permute-done.5
  59.3 5.3 %collective-permute-start.6 = (bf16[1,197,384]{2,1,0:T(8,128)(2,1)S(1)}, bf16[1,197,384]{2,1,0:T(8,128)(2,1)S(1)}, u32[]{:S(2)}, u32[]{:S(2)}) collective-permute-start(bf16[1,197,384]{2,1,0:T(8,128)(2,1)S(1)} %slice.26), channel_id=1, source_target_pairs={{0,2},{1,15},{2,4},{3,1},{4,6},{5,3},{6,8},{7,5},{8,10},{9,7},{10,... | collective-permute-start | bytes 453896 | tf_op jit(solution)/shard_map/ppermute | solution.py:144
  64.6 0.9 slice.27
  65.6 1.9 %collective-permute-start.7 = (bf16[1,197,384]{2,1,0:T(8,128)(2,1)S(1)}, bf16[1,197,384]{2,1,0:T(8,128)(2,1)S(1)}, u32[]{:S(2)}, u32[]{:S(2)}) collective-permute-start(bf16[1,197,384]{2,1,0:T(8,128)(2,1)S(1)} %slice.27), channel_id=1, source_target_pairs={{0,14},{1,3},{2,0},{3,5},{4,2},{5,7},{6,4},{7,9},{8,6},{9,11},{10,... | collective-permute-start | bytes 453896 | tf_op jit(solution)/shard_map/ppermute | solution.py:144
  67.5 1.0 constant_dynamic-update-slice_fusion.2
  68.5 0.0 collective-permute-done.6
  68.6 4.1 %collective-permute-done.7 = bf16[1,197,384]{2,1,0:T(8,128)(2,1)S(1)} collective-permute-done((bf16[1,197,384]{2,1,0:T(8,128)(2,1)S(1)}, bf16[1,197,384]{2,1,0:T(8,128)(2,1)S(1)}, u32[]{:S(2)}, u32[]{:S(2)}) %collective-permute-start.7) | collective-permute-done | bytes 151328 | tf_op jit(solution)/shard_map/ppermute | solution.py:144
  72.7 1.9 %collective-permute-start.8 = (bf16[6,197,384]{2,1,0:T(8,128)(2,1)S(1)}, bf16[6,197,384]{2,1,0:T(8,128)(2,1)S(1)}, u32[]{:S(2)}, u32[]{:S(2)}) collective-permute-start(bf16[6,197,384]{2,1,0:T(8,128)(2,1)S(1)} %constant_dynamic-update-slice_fusion.own_ref), channel_id=1, source_target_pairs={{0,1},{1,0},{2,3},{3,2},{4,5},{5,4},{6,7},{7,6},{8,9},{9,8},{10,11... | collective-permute-start | bytes 2723336 | tf_op jit(solution)/shard_map/ppermute | solution.py:137
  74.6 2.2 %copy.11 = bf16[2,192,768]{2,1,0:T(8,128)(2,1)} copy(bf16[2,192,768]{1,2,0:T(8,128)(2,1)} %reshape.30) | data formatting | bytes 1179648 | tf_op jit(solution)/shard_map/optimization_barrier | solution.py:143
  76.8 1.1 slice_bitcast_fusion
  77.9 0.0 collective-permute-done.9.far_ref
  77.9 5.2 %shard_map.93 = (f32[192,768]{1,0:T(8,128)S(1)}, f32[192,768]{1,0:T(8,128)S(1)}, f32[192,768]{1,0:T(8,128)S(1)}, f32[192,768]{1,0:T(8,128)S(1)}) custom-call(s32[1]{0:T(128)} %bitcast.core_ref, bf16[10,197,384]{2,1,0:T(8,128)(2,1)S(1)} %constant_dynamic-update-slice_fusion.4.own_ref, bf16[10,197,384]{2,1,0:T(8,128)(2,1)} %collective-permute-done.9.far_ref, ...), custom_call_target="tpu_custom_call" | custom-call | flops 1161953280 | bytes 3025920 | tf_op jit(solution)/shard_map/pallas_call | solution.py:102
  83.2 0.0 collective-permute-done.8.far_ref
  83.2 2.7 %shard_map.94 = bf16[2,2,8,48,384]{4,3,2,1,0:T(8,128)(2,1)S(1)} custom-call(s32[1]{0:T(128)} %bitcast.core_ref, bf16[6,197,384]{2,1,0:T(8,128)(2,1)S(1)} %constant_dynamic-update-slice_fusion.own_ref, bf16[6,197,384]{2,1,0:T(8,128)(2,1)S(1)} %collective-permute-done.8.far_ref, bf16[192,768]{1,0:T(8,128)(2,1)S(1)} %get-tuple-element.23.w_in_ref, ...), custom_call_target="tpu_custom_call" | custom-call | flops 697171968 | bytes 1815552 | tf_op jit(solution)/shard_map/pallas_call | solution.py:102
  85.9 19.9 %all_to_all.15 = bf16[4,8,48,384]{3,2,1,0:T(8,128)(2,1)S(1)} all-to-all(bf16[4,8,48,384]{3,2,1,0:T(8,128)(2,1)S(1)} %bitcast.27), channel_id=1, replica_groups=mesh['z'=8,'xlo'=2,'xhi'=2,'y'=8,'core'=2] {'xhi','xlo'}, dimensions={0} | all-to-all | bytes 2359296 | tf_op jit(solution)/shard_map/all_to_all | solution.py:164
  105.8 0.1 add_bitcast_fusion
  105.9 21.2 %all_to_all.16 = f32[8,48,384]{2,1,0:T(8,128)S(1)} all-to-all(f32[8,48,384]{2,1,0:T(8,128)S(1)} %add_bitcast_fusion), channel_id=1, replica_groups=mesh['z'=8,'xlo'=2,'xhi'=2,'y'=8,'core'=2] {'z'}, dimensions={0} | all-to-all | bytes 1179648 | tf_op jit(solution)/shard_map/all_to_all | solution.py:166
  127.1 0.0 copy-done.2
  127.1 0.0 copy-done.4
  127.1 0.7 convert_subtract_fusion
  127.8 0.0 copy-done.3
  127.8 0.7 convert_subtract_fusion.1
  (13 shorter events, 0.2 us)
Async XLA Ops:
  1.7 11.1 %collective-permute-start = (bf16[2,197,384]{2,1,0:T(8,128)(2,1)S(1)}, bf16[2,197,384]{2,1,0:T(8,128)(2,1)S(1)}, u32[]{:S(2)}, u32[]{:S(2)}) collective-permute-start(bf16[2,197,384]{2,1,0:T(8,128)(2,1)S(1)} %pad_maximum_fusion), channel_id=1, source_target_pairs={{0,2},{1,15},{2,4},{3,1},{4,6},{5,3},{6,8},{7,5},{8,10},{9,7},{10,... | collective-permute-start | bytes 907784 | tf_op jit(solution)/shard_map/ppermute | solution.py:141
  5.2 11.4 %collective-permute-start.3 = (bf16[2,197,384]{2,1,0:T(8,128)(2,1)S(1)}, bf16[2,197,384]{2,1,0:T(8,128)(2,1)S(1)}, u32[]{:S(2)}, u32[]{:S(2)}) collective-permute-start(bf16[2,197,384]{2,1,0:T(8,128)(2,1)S(1)} %pad_maximum_fusion), channel_id=1, source_target_pairs={{0,14},{1,3},{2,0},{3,5},{4,2},{5,7},{6,4},{7,9},{8,6},{9,11},{10,... | collective-permute-start | bytes 907784 | tf_op jit(solution)/shard_map/ppermute | solution.py:142
  12.8 20.9 %collective-permute-start.1 = (bf16[2,197,384]{2,1,0:T(8,128)(2,1)S(1)}, bf16[2,197,384]{2,1,0:T(8,128)(2,1)}, u32[]{:S(2)}, u32[]{:S(2)}) collective-permute-start(bf16[2,197,384]{2,1,0:T(8,128)(2,1)S(1)} %collective-permute-done), channel_id=1, source_target_pairs={{0,2},{1,15},{2,4},{3,1},{4,6},{5,3},{6,8},{7,5},{8,10},{9,7},{10,... | collective-permute-start | bytes 907784 | tf_op jit(solution)/shard_map/ppermute | solution.py:141
  16.6 22.7 %collective-permute-start.4 = (bf16[2,197,384]{2,1,0:T(8,128)(2,1)S(1)}, bf16[2,197,384]{2,1,0:T(8,128)(2,1)}, u32[]{:S(2)}, u32[]{:S(2)}) collective-permute-start(bf16[2,197,384]{2,1,0:T(8,128)(2,1)S(1)} %collective-permute-done.3), channel_id=1, source_target_pairs={{0,14},{1,3},{2,0},{3,5},{4,2},{5,7},{6,4},{7,9},{8,6},{9,11},{10,... | collective-permute-start | bytes 907784 | tf_op jit(solution)/shard_map/ppermute | solution.py:142
  22.7 34.4 %all-to-all-start = ((bf16[32,96,96]{2,1,0:T(8,128)(2,1)}), bf16[32,96,96]{2,1,0:T(8,128)(2,1)S(1)}, u32[]{:S(2)}, u32[]{:S(2)}) async-start(bf16[32,96,96]{2,1,0:T(8,128)(2,1)} %broadcast_in_dim.2), calls=%async_computation | async-start | bytes 1572864 | tf_op jit(solution)/shard_map/all_to_all | solution.py:156
  33.5 9.7 %copy-start = (bf16[197,384]{1,0:T(8,128)(2,1)S(1)}, bf16[197,384]{1,0:T(8,128)(2,1)}, u32[]{:S(2)}) copy-start(bf16[197,384]{1,0:T(8,128)(2,1)} %param.6) | copy-start | bytes 453892
  33.5 9.8 %copy-start.1 = (bf16[197,384]{1,0:T(8,128)(2,1)S(1)}, bf16[197,384]{1,0:T(8,128)(2,1)}, u32[]{:S(2)}) copy-start(bf16[197,384]{1,0:T(8,128)(2,1)} %param.7) | copy-start | bytes 453892
  33.6 25.6 %collective-permute-start.2 = (bf16[2,197,384]{2,1,0:T(8,128)(2,1)}, bf16[2,197,384]{2,1,0:T(8,128)(2,1)S(1)}, u32[]{:S(2)}, u32[]{:S(2)}) collective-permute-start(bf16[2,197,384]{2,1,0:T(8,128)(2,1)} %collective-permute-done.1), channel_id=1, source_target_pairs={{0,2},{1,15},{2,4},{3,1},{4,6},{5,3},{6,8},{7,5},{8,10},{9,7},{10,... | collective-permute-start | bytes 907784 | tf_op jit(solution)/shard_map/ppermute | solution.py:141
  39.3 20.0 %collective-permute-start.5 = (bf16[2,197,384]{2,1,0:T(8,128)(2,1)}, bf16[2,197,384]{2,1,0:T(8,128)(2,1)}, u32[]{:S(2)}, u32[]{:S(2)}) collective-permute-start(bf16[2,197,384]{2,1,0:T(8,128)(2,1)} %collective-permute-done.4), channel_id=1, source_target_pairs={{0,14},{1,3},{2,0},{3,5},{4,2},{5,7},{6,4},{7,9},{8,6},{9,11},{10,... | collective-permute-start | bytes 907784 | tf_op jit(solution)/shard_map/ppermute | solution.py:142
  43.3 34.6 %collective-permute-start.9 = (bf16[10,197,384]{2,1,0:T(8,128)(2,1)S(1)}, bf16[10,197,384]{2,1,0:T(8,128)(2,1)}, u32[]{:S(2)}, u32[]{:S(2)}) collective-permute-start(bf16[10,197,384]{2,1,0:T(8,128)(2,1)S(1)} %constant_dynamic-update-slice_fusion.4.own_ref), channel_id=1, source_target_pairs={{0,1},{1,0},{2,3},{3,2},{4,5},{5,4},{6,7},{7,6},{8,9},{9,8},{10,11... | collective-permute-start | bytes 4538888 | tf_op jit(solution)/shard_map/ppermute | solution.py:137
  59.3 9.2 %collective-permute-start.6 = (bf16[1,197,384]{2,1,0:T(8,128)(2,1)S(1)}, bf16[1,197,384]{2,1,0:T(8,128)(2,1)S(1)}, u32[]{:S(2)}, u32[]{:S(2)}) collective-permute-start(bf16[1,197,384]{2,1,0:T(8,128)(2,1)S(1)} %slice.26), channel_id=1, source_target_pairs={{0,2},{1,15},{2,4},{3,1},{4,6},{5,3},{6,8},{7,5},{8,10},{9,7},{10,... | collective-permute-start | bytes 453896 | tf_op jit(solution)/shard_map/ppermute | solution.py:144
  65.6 7.1 %collective-permute-start.7 = (bf16[1,197,384]{2,1,0:T(8,128)(2,1)S(1)}, bf16[1,197,384]{2,1,0:T(8,128)(2,1)S(1)}, u32[]{:S(2)}, u32[]{:S(2)}) collective-permute-start(bf16[1,197,384]{2,1,0:T(8,128)(2,1)S(1)} %slice.27), channel_id=1, source_target_pairs={{0,14},{1,3},{2,0},{3,5},{4,2},{5,7},{6,4},{7,9},{8,6},{9,11},{10,... | collective-permute-start | bytes 453896 | tf_op jit(solution)/shard_map/ppermute | solution.py:144
  72.7 10.5 %collective-permute-start.8 = (bf16[6,197,384]{2,1,0:T(8,128)(2,1)S(1)}, bf16[6,197,384]{2,1,0:T(8,128)(2,1)S(1)}, u32[]{:S(2)}, u32[]{:S(2)}) collective-permute-start(bf16[6,197,384]{2,1,0:T(8,128)(2,1)S(1)} %constant_dynamic-update-slice_fusion.own_ref), channel_id=1, source_target_pairs={{0,1},{1,0},{2,3},{3,2},{4,5},{5,4},{6,7},{7,6},{8,9},{9,8},{10,11... | collective-permute-start | bytes 2723336 | tf_op jit(solution)/shard_map/ppermute | solution.py:137
  105.8 21.4 %copy-start.2 = (bf16[96,48]{0,1:T(8,128)(2,1)S(1)}, bf16[96,48]{0,1:T(8,128)(2,1)}, u32[]{:S(2)}) copy-start(bf16[96,48]{0,1:T(8,128)(2,1)} %param.9) | copy-start | bytes 27652
  105.8 21.4 %copy-start.4 = (f32[96,48]{0,1:T(8,128)S(1)}, f32[96,48]{0,1:T(8,128)}, u32[]{:S(2)}) copy-start(f32[96,48]{0,1:T(8,128)} %param.11) | copy-start | bytes 55300
  105.8 22.1 %copy-start.3 = (bf16[48,96]{1,0:T(8,128)(2,1)S(1)}, bf16[48,96]{1,0:T(8,128)(2,1)}, u32[]{:S(2)}) copy-start(bf16[48,96]{1,0:T(8,128)(2,1)} %param.8) | copy-start | bytes 27652
  105.8 22.1 %copy-start.5 = (f32[48,96]{1,0:T(8,128)S(1)}, f32[48,96]{1,0:T(8,128)}, u32[]{:S(2)}) copy-start(f32[48,96]{1,0:T(8,128)} %param.10) | copy-start | bytes 55300

commit v4 on v2

--- a/solution.py
+++ b/solution.py
@@ -12,8 +12,8 @@
 DP = ("z", "xlo")
 MP = ("xhi", "y", "core")
 GROUP = ("y", "core")
-OWNERS = ("xhi", "z", "xlo")
-ROW = ("xhi", "xlo")
+OWNERS = ("z", "xlo", "xhi")
+STEP = 2
 BF16 = jnp.bfloat16
 F32 = jnp.float32
 ROOT = math.sqrt(2.0 / math.pi)
@@ -34,46 +34,51 @@
     def dot(a, b, dims):
         return lax.dot_general(a, b, (dims, ((), ())), preferred_element_type=F32)
 
-    x = jnp.concatenate([xc_ref[0, 0], xc_ref[1, 0]], axis=1)
-    c = jnp.concatenate([xc_ref[0, 1], xc_ref[1, 1]], axis=1)
-    pre = dot(w_in_ref[...], x, ((1,), (1,)))
-    back = dot(w_out_ref[...], c, ((1,), (1,)))
-    act, slope = gelu_parts(pre)
-    act = act.astype(BF16)
-    delta = (back * slope).astype(BF16)
-    g_in = dot(delta, x, ((1,), (0,)))
-    g_out = dot(act, c, ((1,), (0,)))
+    terms = []
+    for n in range(STEP):
+        x, c = (jnp.concatenate([xc_ref[2 * n, k], xc_ref[2 * n + 1, k]], axis=1) for k in (0, 1))
+        pre = dot(w_in_ref[...], x, ((1,), (1,)))
+        back = dot(w_out_ref[...], c, ((1,), (1,)))
+        act, slope = gelu_parts(pre)
+        act = act.astype(BF16)
+        delta = (back * slope).astype(BF16)
+        terms.append((dot(delta, x, ((1,), (0,))), dot(act, c, ((1,), (0,)))))
+    (g_in, g_out), more = terms[0], terms[1:]
+    s_in, s_out = g_in * g_in, g_out * g_out
+    for n_in, n_out in more:
+        g_in, g_out = g_in + n_in, g_out + n_out
+        s_in, s_out = s_in + n_in * n_in, s_out + n_out * n_out
 
     @pl.when(step == 0)
     def _():
         sum_in[...] = g_in
-        sq_in[...] = g_in * g_in
+        sq_in[...] = s_in
         sum_out[...] = g_out
-        sq_out[...] = g_out * g_out
+        sq_out[...] = s_out
 
     @pl.when(step > 0)
     def _():
         sum_in[...] += g_in
-        sq_in[...] += g_in * g_in
+        sq_in[...] += s_in
         sum_out[...] += g_out
-        sq_out[...] += g_out * g_out
+        sq_out[...] += s_out
 
     @pl.when(step == pl.num_programs(0) - 1)
     def _():
-        cols, pairs, deep, rows, packed = out_ref.shape
+        blocks, cols, rows, packed = out_ref.shape
         width = packed // 4
         for h in range(cols):
             part = slice(h * width, (h + 1) * width)
             both = [r[part, :] for r in (sum_in, sq_in, sum_out, sq_out)]
             turned = jnp.concatenate(both, axis=0).T.astype(BF16)
-            for k in range(deep * pairs):
-                out_ref[h, k % pairs, k // pairs] = turned[k * rows : (k + 1) * rows]
+            for k in range(blocks):
+                out_ref[k, h] = turned[k * rows : (k + 1) * rows]
 
 
 def grads(xc, w_in_t, w_out, shape):
     hid, d = w_in_t.shape
     pieces, two, seq, part = xc.shape
-    per = d // part
+    per = STEP * d // part
     whole = pl.BlockSpec((hid, d), lambda i: (0, 0))
     return pl.pallas_call(
         grads_kernel,
@@ -94,12 +99,10 @@
     both = jnp.concatenate([w_in, w_out.T], axis=0)
     both = jnp.broadcast_to(both[None], (cols * dp, *both.shape))
     weights = lax.all_to_all(both, OWNERS, 0, 0, tiled=True)
-    weights = weights.reshape(cols, dp, 2, d_own, h_own).transpose(2, 0, 4, 1, 3)
+    weights = weights.reshape(dp, cols, 2, d_own, h_own).transpose(2, 1, 4, 0, 3)
     weights = weights.reshape(2, cols * h_own, dp * d_own)
-    pieces = grads(xc, weights[0], weights[1], (cols, pairs, deep, d_own, 4 * h_own))
-    pieces = lax.all_to_all(pieces.reshape(cols * pairs, deep, d_own, 4 * h_own), ROW, 0, 0, tiled=True)
-    pieces = sum(pieces[k].astype(F32) for k in range(cols * pairs)).astype(BF16)
-    pieces = lax.all_to_all(pieces, "z", 0, 0, tiled=True)
+    pieces = grads(xc, weights[0], weights[1], (dp, cols, d_own, 4 * h_own))
+    pieces = lax.all_to_all(pieces.reshape(dp * cols, d_own, 4 * h_own), OWNERS, 0, 0, tiled=True)
     total = jnp.sum(pieces.astype(F32), axis=0)
     sum_in, sq_in, sum_out, sq_out = jnp.split(total, 4, axis=1)
     images = xc.shape[0] * xc.shape[3] // (dp * d_own) * cols * dp

time: 118 us -> 120 us (1.017)
  Pallas kernels: 9.2 us -> 7.27 us
  blocking collectives: 77.4 us -> 79.2 us
  waiting for transfers between devices: 8.73 us -> 10.2 us
    all_to_all x2 -> x1, blocking collectives: 40 us -> 43.3 us  [per_device(): lax.all_to_all(pieces.reshape(dp * cols, d_own, 4 * h_own), OWNERS, 0, 0,...]
    pallas_call x1, Pallas kernels: 9.2 us -> 7.27 us  [grads(): pl.pallas_call(grads_kernel, grid=(pieces // per,), in_specs=[pl.BlockSpe...]
    all_to_all x1, blocking collectives: 37.4 us -> 35.9 us  [per_device(): weights = lax.all_to_all(both, OWNERS, 0, 0, tiled=True)]
    all_gather x1, waiting for transfers between devices: 8.71 us -> 10.2 us  [per_device(): xc = lax.all_gather(jnp.stack([inputs, cotangent]), GROUP)]
where the time goes in v4:
time: 120 us; the launch traced here: 118 us
  blocking collectives  79.2 us (66%)
  between operations  14.1 us (12%)
  waiting for transfers between devices  10.2 us (8%)
  Pallas kernels  7.27 us (6%)
  other arithmetic  4.05 us (3%)
  local copies, waits for them, and re-layouts  3.48 us (3%)
    all_to_all x1, blocking collectives, per_device(): lax.all_to_all(pieces.reshape(dp * cols, d_own, 4 * h_own), OWNERS, 0, 0,...  43.3 us
    all_to_all x1, blocking collectives, per_device(): weights = lax.all_to_all(both, OWNERS, 0, 0, tiled=True)  35.9 us
    all_gather x1, waiting for transfers between devices, per_device(): xc = lax.all_gather(jnp.stack([inputs, cotangent]), GROUP)  10.2 us
    pallas_call x1, Pallas kernels, grads(): pl.pallas_call(grads_kernel, grid=(pieces // per,), in_specs=[pl.BlockSpe...  7.27 us
    squeeze x4, local copies, waits for them, and re-layouts, per_device(): pieces = grads(xc, weights[0], weights[1], (dp, cols, d_own, 4 * h_own))  2.74 us
  transfers between devices with their start and end apart: 1, of which 1 were waited for; matrix products, arithmetic and copies ran while one was open for 3% of the time, Pallas kernels for 0%

profile of v4, /device:TPU:56, one launch (start us, length us, event | category | flops | bytes accessed | tf_op | source)
XLA Modules:
  0.0 118.4 jit_solution(14715731621979805864)
XLA Ops:
  7.2 0.0 all-gather.3.cloned.1.call-start
  7.2 1.8 %pad_maximum_fusion = bf16[2,197,384]{2,1,0:T(8,128)(2,1)} fusion(bf16[1,197,384]{2,1,0:T(8,128)(2,1)} %bitcast.24, bf16[1,197,384]{2,1,0:T(8,128)(2,1)} %bitcast.25), kind=kLoop, calls=%fused_computation.1 | loop fusion | flops 151296 | bytes 605184 | tf_op jit(solution)/shard_map/stack | solution.py:98
  9.0 0.0 all-gather.3.cloned.1.call-update
  9.0 0.7 pad_maximum_fusion.1
  9.7 0.1 broadcast_in_dim.2
  9.8 35.9 %all_to_all.10 = bf16[32,96,96]{2,1,0:T(8,128)(2,1)S(1)} all-to-all(bf16[32,96,96]{2,1,0:T(8,128)(2,1)S(1)} %broadcast_in_dim.2), channel_id=1, replica_groups=mesh['z'=8,'xlo'=2,'xhi'=2,'y'=8,'core'=2] {'z','xlo','xhi'}, dimensions={0} | all-to-all | bytes 1179648 | tf_op jit(solution)/shard_map/all_to_all | solution.py:101
  45.7 0.1 fusion.10
  45.8 0.6 copy.19
  46.4 0.8 reshape.24.w_out_ref
  47.2 0.6 copy.18
  47.8 0.8 reshape.23.w_in_ref
  48.5 10.2 %all-gather.3.cloned.1.call-done = bf16[32,197,384]{2,1,0:T(8,128)(2,1)} async-done(((bf16[2,197,384]{2,1,0:T(8,128)(2,1)}), bf16[32,197,384]{2,1,0:T(8,128)(2,1)}) %all-gather.3.cloned.1.call-update) | async-done | bytes 4841488 | tf_op jit(solution)/shard_map/all_gather | solution.py:98
  58.7 7.3 %shard_map.93 = bf16[16,2,48,384]{3,2,1,0:T(8,128)(2,1)S(1)} custom-call(bf16[16,2,197,384]{3,2,1,0:T(8,128)(2,1)} %bitcast.22, bf16[192,768]{1,0:T(8,128)(2,1)S(1)} %reshape.23.w_in_ref, bf16[192,768]{1,0:T(8,128)(2,1)S(1)} %reshape.24.w_out_ref), custom_call_target="tpu_custom_call" | custom-call | tf_op jit(solution)/shard_map/pallas_call | solution.py:83
  66.0 43.3 %all_to_all.11 = bf16[32,48,384]{2,1,0:T(8,128)(2,1)S(1)} all-to-all(bf16[32,48,384]{2,1,0:T(8,128)(2,1)S(1)} %bitcast.21), channel_id=1, replica_groups=mesh['z'=8,'xlo'=2,'xhi'=2,'y'=8,'core'=2] {'z','xlo','xhi'}, dimensions={0} | all-to-all | bytes 2359296 | tf_op jit(solution)/shard_map/all_to_all | solution.py:105
  109.4 0.0 copy-start
  109.4 0.0 copy-start.2
  109.4 0.0 copy-start.1
  109.4 0.0 copy-start.3
  109.4 0.2 convert_reduce_fusion
  109.5 0.5 copy-done
  110.1 0.0 copy-done.2
  110.1 0.7 convert_subtract_fusion
  110.8 0.0 copy-done.1
  110.8 0.0 copy-done.3
  110.8 0.7 convert_subtract_fusion.1
Async XLA Ops:
  7.2 51.6 %all-gather.3.cloned.1.call-start = ((), (), s32[]{:S(2)}) async-start(), calls=%async_computation.2 | async-start | bytes 5222400 | tf_op jit(solution)/shard_map/all_gather | solution.py:98
  109.4 0.7 copy-start
  109.4 0.8 copy-start.2
  109.4 1.4 %copy-start.1 = (bf16[48,96]{1,0:T(8,128)(2,1)S(1)}, bf16[48,96]{1,0:T(8,128)(2,1)}, u32[]{:S(2)}) copy-start(bf16[48,96]{1,0:T(8,128)(2,1)} %param.8) | copy-start | bytes 27652
  109.4 1.4 %copy-start.3 = (f32[48,96]{1,0:T(8,128)S(1)}, f32[48,96]{1,0:T(8,128)}, u32[]{:S(2)}) copy-start(f32[48,96]{1,0:T(8,128)} %param.10) | copy-start | bytes 55300
Sparse Core Ops, SparseCore 0:
  10.1 48.5 all-gather.2

commit v5 on v3

v5 whole, which is shorter than its diff:
```python
import math
import jax
import jax.numpy as jnp
from jax import lax
from jax.experimental import pallas as pl
from jax.experimental.pallas import tpu as pltpu
from jax.sharding import Mesh
from jax.sharding import PartitionSpec as P

AXES = ("z", "xlo", "xhi", "y", "core")
DP = ("z", "xlo")
MP = ("xhi", "y", "core")
GROUP = ("y", "core")
ROW = ("xlo", "xhi")
BF16 = jnp.bfloat16
F32 = jnp.float32
ROOT = math.sqrt(2.0 / math.pi)
CUBE = 0.044715


def gelu_parts(v):
    v2 = v * v
    t = jnp.tanh(ROOT * v * (1.0 + CUBE * v2))
    half = 0.5 * (1.0 + t)
    slope = half + 0.5 * v * (1.0 - t * t) * (ROOT * (1.0 + 3.0 * CUBE * v2))
    return v * half, slope


def image_grads(core_ref, own_ref, far_ref, turned_ref):
    def dot(a, b, dims):
        return lax.dot_general(a, b, (dims, ((), ())), preferred_element_type=F32)

    first = core_ref[0] == 0
    hid = turned_ref.shape[0] // 2

    def whole(k):
        own, far = own_ref[k], far_ref[k]
        return jnp.concatenate(
            [jnp.where(first, own, far), jnp.where(first, far, own)], axis=1
        )

    x, c = whole(0), whole(1)
    pre = dot(turned_ref[:hid], x, ((1,), (1,)))
    back = dot(turned_ref[hid:], c, ((1,), (1,)))
    act, slope = gelu_parts(pre)
    act = act.astype(BF16)
    delta = (back * slope).astype(BF16)
    return dot(delta, x, ((1,), (0,))), dot(act, c, ((1,), (0,)))


def add_image(sums, g_in, g_out):
    for ref, term in zip(sums, (g_in, g_in * g_in, g_out, g_out * g_out)):
        ref[...] += term


def first_kernel(core_ref, own_ref, far_ref, weights_ref, turned_ref, *sums):
    @pl.when(pl.program_id(0) == 0)
    def _():
        turned_ref[...] = weights_ref[...].T
        for ref in sums:
            ref[...] = jnp.zeros_like(ref)

    add_image(sums, *image_grads(core_ref, own_ref, far_ref, turned_ref))


def last_kernel(core_ref, own_ref, far_ref, turned_ref, s0, s1, s2, s3, out_ref, *sums):
    step = pl.program_id(0)

    @pl.when(step == 0)
    def _():
        for ref, start in zip(sums, (s0, s1, s2, s3)):
            ref[...] = start[...]

    add_image(sums, *image_grads(core_ref, own_ref, far_ref, turned_ref))

    @pl.when(step == pl.num_programs(0) - 1)
    def _():
        pairs, cols, deep, rows, packed = out_ref.shape
        width = packed // 4
        for h in range(cols):
            part = slice(h * width, (h + 1) * width)
            turned = jnp.concatenate([r[part, :] for r in sums], axis=0).T.astype(BF16)
            for k in range(deep * pairs):
                out_ref[k % pairs, h, k // pairs] = turned[k * rows : (k + 1) * rows]


def run_images(kernel, core, own, far, weights, sums, outs):
    pieces, seq, part = own.shape
    last = pieces // 2 - 1
    hid, d = outs[-1].shape if sums == () else sums[0].shape
    block = (2, seq, part)

    def whole(a):
        return pl.BlockSpec(a.shape, lambda i: (0,) * len(a.shape))

    return pl.pallas_call(
        kernel,
        grid=(last + 1,),
        in_specs=[
            pl.BlockSpec(memory_space=pltpu.SMEM),
            pl.BlockSpec(block, lambda i: (i, 0, 0)),
            pl.BlockSpec(block, lambda i: (jnp.where(i < last, i ^ 1, i), 0, 0)),
            whole(weights),
        ]
        + [whole(a) for a in sums],
        out_specs=[whole(a) for a in outs],
        out_shape=outs,
        scratch_shapes=[pltpu.VMEM(a.shape, a.dtype) for a in sums],
        compiler_params=pltpu.CompilerParams(vmem_limit_bytes=40 << 20),
        cost_estimate=pl.CostEstimate(
            flops=pieces * 4 * seq * hid * d,
            bytes_accessed=pieces * 4 * seq * part,
            transcendentals=pieces * seq * hid // 2,
        ),
    )(core, own, far, weights, *sums)


def round_the_ring(own, weights):
    n, cores = lax.axis_size("y"), lax.axis_size("core")

    def turned(step):
        return [
            (y * cores + k, (y + (step if k == 0 else -step)) % n * cores + k)
            for y in range(n)
            for k in range(cores)
        ]

    def swap(a):
        pairs = [(y * cores + k, y * cores + 1 - k) for y in range(n) for k in range(cores)]
        return lax.ppermute(a, GROUP, pairs)

    up, down = [own], [own]
    for _ in range(n // 2 - 1):
        up.append(lax.ppermute(up[-1], GROUP, turned(1)))
        down.append(lax.ppermute(down[-1], GROUP, turned(-1)))
    up[3], down[3], weights = lax.optimization_barrier((up[3], down[3], weights))
    opposite = [lax.ppermute(up[3][:1], GROUP, turned(1)), lax.ppermute(down[3][1:], GROUP, turned(-1))]
    early = jnp.concatenate([up[1], down[1], up[2], down[2], own])
    late = jnp.concatenate([up[3], down[3], *opposite])
    return (early, swap(early)), (late, swap(late)), weights


def per_device(inputs, cotangent, w_in, w_out, prec_in, prec_out):
    d_own, h_own = w_in.shape
    cols, pairs, deep = (lax.axis_size(a) for a in ("xhi", "xlo", "z"))
    dp = deep * pairs
    hid = cols * h_own
    both = jnp.concatenate([w_in, w_out.T], axis=1)
    both = jnp.broadcast_to(both[None], (pairs * cols, *both.shape))
    both = lax.all_to_all(both, ROW, 0, 0, tiled=True).reshape(pairs, cols, d_own, 2, h_own)
    both = both.transpose(0, 2, 3, 1, 4).reshape(pairs, d_own, 2 * hid)
    weights = lax.all_to_all(jnp.broadcast_to(both[None], (deep, *both.shape)), "z", 0, 0, tiled=True)
    weights = weights.reshape(dp * d_own, 2 * hid)
    early, late, weights = round_the_ring(jnp.stack([inputs, cotangent]), weights)
    core = lax.axis_index("core").reshape(1).astype(jnp.int32)
    turned = jax.ShapeDtypeStruct((2 * hid, dp * d_own), BF16)
    partial = [jax.ShapeDtypeStruct((hid, dp * d_own), F32)] * 4
    packed = jax.ShapeDtypeStruct((pairs, cols, deep, d_own, 4 * h_own), BF16)
    turned, *partial = run_images(first_kernel, core, *early, weights, (), [turned, *partial])
    (pieces,) = run_images(last_kernel, core, *late, turned, tuple(partial), [packed])
    pieces = pieces.reshape(pairs * cols, deep, d_own, 4 * h_own)
    pieces = lax.all_to_all(pieces, ROW, 0, 0, tiled=True)
    pieces = sum(pieces[k].astype(F32) for k in range(cols * pairs)).astype(BF16)
    pieces = lax.all_to_all(pieces, "z", 0, 0, tiled=True)
    total = jnp.sum(pieces.astype(F32), axis=0)
    sum_in, sq_in, sum_out, sq_out = jnp.split(total, 4, axis=1)
    scale = 1.0 / (lax.axis_size("y") * cols * dp)
    new_prec_in = 0.6 * prec_in + 0.4 * sq_in * scale
    new_prec_out = 0.6 * prec_out + 0.4 * sq_out.T * scale
    w_in_own = w_in.astype(F32)
    w_out_own = w_out.astype(F32)
    new_w_in = w_in_own - 1.0 * (sum_in * scale + 0.1 * w_in_own) / (new_prec_in + 0.1)
    new_w_out = w_out_own - 1.0 * (sum_out.T * scale + 0.1 * w_out_own) / (new_prec_out + 0.1)
    return (new_prec_in, new_prec_out, new_w_in, new_w_out)


def solution(mesh):
    torus = Mesh(mesh.devices.reshape(8, 2, 2, 8, 2), AXES)
    dp_mp = DP + MP
    in_specs = (P(None, dp_mp), P(None, dp_mp), P(DP, MP), P(MP, DP), P(DP, MP), P(MP, DP))
    out_specs = (P(DP, MP), P(MP, DP), P(DP, MP), P(MP, DP))
    return jax.shard_map(
        per_device, mesh=torus, in_specs=in_specs, out_specs=out_specs, check_vma=False
    )
```

time: 129 us -> 122 us (0.946)
  the two profiles are of different devices: /device:TPU:16 before, /device:TPU:56 now
where the time goes in v5:
time: 122 us; the launch traced here: 121 us
  blocking collectives  46.7 us (38%)
  starting transfers between devices  44 us (36%)
  waiting for transfers between devices  12 us (10%)
  Pallas kernels  8.37 us (7%)
  local copies, waits for them, and re-layouts  5.76 us (5%)
  other arithmetic  3.42 us (3%)
    all_to_all x1, blocking collectives, per_device(): pieces = lax.all_to_all(pieces, ROW, 0, 0, tiled=True)  19.6 us
    all_to_all x1, blocking collectives, per_device(): pieces = lax.all_to_all(pieces, 'z', 0, 0, tiled=True)  19.2 us
    ppermute x3, starting transfers between devices, round_the_ring(): up.append(lax.ppermute(up[-1], GROUP, turned(1)))  16.2 us
    all_to_all x1, starting transfers between devices, per_device(): lax.all_to_all(jnp.broadcast_to(both[None], (deep, *both.shape)), 'z', 0,...  10.4 us
    pallas_call x2, Pallas kernels, run_images(): pl.pallas_call(kernel, grid=(last + 1,), in_specs=[pl.BlockSpec(memory_sp...  8.37 us
    all_to_all x1, blocking collectives, per_device(): lax.all_to_all(both, ROW, 0, 0, tiled=True)  7.91 us
    ppermute x3, starting transfers between devices, round_the_ring(): down.append(lax.ppermute(down[-1], GROUP, turned(-1)))  7.08 us
    ppermute x1, waiting for transfers between devices, round_the_ring(): lax.ppermute(down[3][1:], GROUP, turned(-1))  5.07 us
  transfers between devices with their start and end apart: 11, of which 4 were waited for; matrix products, arithmetic and copies ran while one was open for 5% of the time, Pallas kernels for 5%

profile of v5, /device:TPU:56, one launch (start us, length us, event | category | flops | bytes accessed | tf_op | source)
XLA Modules:
  0.0 121.1 jit_solution(4309995941081809431)
XLA Ops:
  0.6 1.0 pad_maximum_fusion
  1.7 3.3 %collective-permute-start.3 = (bf16[2,197,384]{2,1,0:T(8,128)(2,1)S(1)}, bf16[2,197,384]{2,1,0:T(8,128)(2,1)S(1)}, u32[]{:S(2)}, u32[]{:S(2)}) collective-permute-start(bf16[2,197,384]{2,1,0:T(8,128)(2,1)S(1)} %pad_maximum_fusion), channel_id=1, source_target_pairs={{0,14},{1,3},{2,0},{3,5},{4,2},{5,7},{6,4},{7,9},{8,6},{9,11},{10,... | collective-permute-start | bytes 907784 | tf_op jit(solution)/shard_map/ppermute | solution.py:135
  4.9 5.7 %collective-permute-start = (bf16[2,197,384]{2,1,0:T(8,128)(2,1)S(1)}, bf16[2,197,384]{2,1,0:T(8,128)(2,1)S(1)}, u32[]{:S(2)}, u32[]{:S(2)}) collective-permute-start(bf16[2,197,384]{2,1,0:T(8,128)(2,1)S(1)} %pad_maximum_fusion), channel_id=1, source_target_pairs={{0,2},{1,15},{2,4},{3,1},{4,6},{5,3},{6,8},{7,5},{8,10},{9,7},{10,... | collective-permute-start | bytes 907784 | tf_op jit(solution)/shard_map/ppermute | solution.py:134
  10.6 5.1 %collective-permute-done.3 = bf16[2,197,384]{2,1,0:T(8,128)(2,1)S(1)} collective-permute-done((bf16[2,197,384]{2,1,0:T(8,128)(2,1)S(1)}, bf16[2,197,384]{2,1,0:T(8,128)(2,1)S(1)}, u32[]{:S(2)}, u32[]{:S(2)}) %collective-permute-start.3) | collective-permute-done | bytes 302624 | tf_op jit(solution)/shard_map/ppermute | solution.py:135
  15.7 1.9 %collective-permute-start.4 = (bf16[2,197,384]{2,1,0:T(8,128)(2,1)S(1)}, bf16[2,197,384]{2,1,0:T(8,128)(2,1)S(1)}, u32[]{:S(2)}, u32[]{:S(2)}) collective-permute-start(bf16[2,197,384]{2,1,0:T(8,128)(2,1)S(1)} %collective-permute-done.3), channel_id=1, source_target_pairs={{0,14},{1,3},{2,0},{3,5},{4,2},{5,7},{6,4},{7,9},{8,6},{9,11},{10,... | collective-permute-start | bytes 907784 | tf_op jit(solution)/shard_map/ppermute | solution.py:135
  17.6 0.0 collective-permute-done
  17.6 5.4 %collective-permute-start.1 = (bf16[2,197,384]{2,1,0:T(8,128)(2,1)S(1)}, bf16[2,197,384]{2,1,0:T(8,128)(2,1)S(1)}, u32[]{:S(2)}, u32[]{:S(2)}) collective-permute-start(bf16[2,197,384]{2,1,0:T(8,128)(2,1)S(1)} %collective-permute-done), channel_id=1, source_target_pairs={{0,2},{1,15},{2,4},{3,1},{4,6},{5,3},{6,8},{7,5},{8,10},{9,7},{10,... | collective-permute-start | bytes 907784 | tf_op jit(solution)/shard_map/ppermute | solution.py:134
  23.0 0.8 pad_maximum_fusion.1
  23.8 7.9 %all_to_all.20 = bf16[4,48,192]{2,1,0:T(8,128)(2,1)S(1)} all-to-all(bf16[4,48,192]{2,1,0:T(8,128)(2,1)S(1)} %broadcast_in_dim.6), channel_id=1, replica_groups=mesh['z'=8,'xlo'=2,'xhi'=2,'y'=8,'core'=2] {'xlo','xhi'}, dimensions={0} | all-to-all | bytes 147456 | tf_op jit(solution)/shard_map/all_to_all | solution.py:150
  31.7 0.1 reshape.31
  31.9 0.1 copy.10
  31.9 0.1 broadcast_in_dim.14
  32.1 0.9 broadcast_in_dim.15
  33.0 10.4 %all-to-all-start.1 = ((bf16[8,2,48,384]{3,2,1,0:T(8,128)(2,1)}), bf16[8,2,48,384]{3,2,1,0:T(8,128)(2,1)S(1)}, u32[]{:S(2)}, u32[]{:S(2)}) async-start(bf16[8,2,48,384]{3,2,1,0:T(8,128)(2,1)} %broadcast_in_dim.15), calls=%async_computation.1 | async-start | bytes 1179648 | tf_op jit(solution)/shard_map/all_to_all | solution.py:152
  43.3 0.7 constant_dynamic-update-slice_fusion.9
  44.1 0.8 constant_dynamic-update-slice_fusion.8
  44.8 0.0 collective-permute-done.4
  44.8 1.9 %collective-permute-start.5 = (bf16[2,197,384]{2,1,0:T(8,128)(2,1)S(1)}, bf16[2,197,384]{2,1,0:T(8,128)(2,1)S(1)}, u32[]{:S(2)}, u32[]{:S(2)}) collective-permute-start(bf16[2,197,384]{2,1,0:T(8,128)(2,1)S(1)} %collective-permute-done.4), channel_id=1, source_target_pairs={{0,14},{1,3},{2,0},{3,5},{4,2},{5,7},{6,4},{7,9},{8,6},{9,11},{10,... | collective-permute-start | bytes 907784 | tf_op jit(solution)/shard_map/ppermute | solution.py:135
  46.8 0.0 collective-permute-done.1
  46.8 5.1 %collective-permute-start.2 = (bf16[2,197,384]{2,1,0:T(8,128)(2,1)S(1)}, bf16[2,197,384]{2,1,0:T(8,128)(2,1)S(1)}, u32[]{:S(2)}, u32[]{:S(2)}) collective-permute-start(bf16[2,197,384]{2,1,0:T(8,128)(2,1)S(1)} %collective-permute-done.1), channel_id=1, source_target_pairs={{0,2},{1,15},{2,4},{3,1},{4,6},{5,3},{6,8},{7,5},{8,10},{9,7},{10,... | collective-permute-start | bytes 907784 | tf_op jit(solution)/shard_map/ppermute | solution.py:134
  51.9 0.7 constant_dynamic-update-slice_fusion.7
  52.7 0.8 constant_dynamic-update-slice_fusion.6
  53.4 0.0 copy-done
  53.4 0.7 constant_dynamic-update-slice_fusion.5
  54.1 0.0 copy-done.1
  54.1 0.7 constant_dynamic-update-slice_fusion.4.own_ref
  54.8 1.9 %collective-permute-start.9 = (bf16[10,197,384]{2,1,0:T(8,128)(2,1)}, bf16[10,197,384]{2,1,0:T(8,128)(2,1)}, u32[]{:S(2)}, u32[]{:S(2)}) collective-permute-start(bf16[10,197,384]{2,1,0:T(8,128)(2,1)} %constant_dynamic-update-slice_fusion.4.own_ref), channel_id=1, source_target_pairs={{0,1},{1,0},{2,3},{3,2},{4,5},{5,4},{6,7},{7,6},{8,9},{9,8},{10,11... | collective-permute-start | bytes 4538888 | tf_op jit(solution)/shard_map/ppermute | solution.py:130
  56.7 0.0 collective-permute-done.5
  56.7 0.0 collective-permute-done.2
  56.7 0.6 all-to-all-done.1
  57.4 4.5 %collective-permute-start.6 = (bf16[1,197,384]{2,1,0:T(8,128)(2,1)S(1)}, bf16[1,197,384]{2,1,0:T(8,128)(2,1)S(1)}, u32[]{:S(2)}, u32[]{:S(2)}) collective-permute-start(bf16[1,197,384]{2,1,0:T(8,128)(2,1)S(1)} %slice.18), channel_id=1, source_target_pairs={{0,2},{1,15},{2,4},{3,1},{4,6},{5,3},{6,8},{7,5},{8,10},{9,7},{10,... | collective-permute-start | bytes 453896 | tf_op jit(solution)/shard_map/ppermute | solution.py:137
  62.0 1.9 %collective-permute-start.7 = (bf16[1,197,384]{2,1,0:T(8,128)(2,1)S(1)}, bf16[1,197,384]{2,1,0:T(8,128)(2,1)S(1)}, u32[]{:S(2)}, u32[]{:S(2)}) collective-permute-start(bf16[1,197,384]{2,1,0:T(8,128)(2,1)S(1)} %slice.19), channel_id=1, source_target_pairs={{0,14},{1,3},{2,0},{3,5},{4,2},{5,7},{6,4},{7,9},{8,6},{9,11},{10,... | collective-permute-start | bytes 453896 | tf_op jit(solution)/shard_map/ppermute | solution.py:137
  63.9 0.1 constant_dynamic-update-slice_fusion.2
  64.0 1.2 %collective-permute-done.6 = bf16[1,197,384]{2,1,0:T(8,128)(2,1)S(1)} collective-permute-done((bf16[1,197,384]{2,1,0:T(8,128)(2,1)S(1)}, bf16[1,197,384]{2,1,0:T(8,128)(2,1)S(1)}, u32[]{:S(2)}, u32[]{:S(2)}) %collective-permute-start.6) | collective-permute-done | bytes 151328 | tf_op jit(solution)/shard_map/ppermute | solution.py:137
  65.2 5.1 %collective-permute-done.7 = bf16[1,197,384]{2,1,0:T(8,128)(2,1)S(1)} collective-permute-done((bf16[1,197,384]{2,1,0:T(8,128)(2,1)S(1)}, bf16[1,197,384]{2,1,0:T(8,128)(2,1)S(1)}, u32[]{:S(2)}, u32[]{:S(2)}) %collective-permute-start.7) | collective-permute-done | bytes 151328 | tf_op jit(solution)/shard_map/ppermute | solution.py:137
  70.3 1.9 %collective-permute-start.8 = (bf16[6,197,384]{2,1,0:T(8,128)(2,1)S(1)}, bf16[6,197,384]{2,1,0:T(8,128)(2,1)S(1)}, u32[]{:S(2)}, u32[]{:S(2)}) collective-permute-start(bf16[6,197,384]{2,1,0:T(8,128)(2,1)S(1)} %constant_dynamic-update-slice_fusion.own_ref), channel_id=1, source_target_pairs={{0,1},{1,0},{2,3},{3,2},{4,5},{5,4},{6,7},{7,6},{8,9},{9,8},{10,11... | collective-permute-start | bytes 2723336 | tf_op jit(solution)/shard_map/ppermute | solution.py:130
  72.2 0.0 collective-permute-done.9.far_ref
  72.2 5.7 %shard_map.93 = (bf16[384,768]{1,0:T(8,128)(2,1)S(1)}, f32[192,768]{1,0:T(8,128)S(1)}, f32[192,768]{1,0:T(8,128)S(1)}, f32[192,768]{1,0:T(8,128)S(1)}, f32[192,768]{1,0:T(8,128)S(1)}) custom-call(s32[1]{0:T(128)} %bitcast.core_ref, bf16[10,197,384]{2,1,0:T(8,128)(2,1)} %constant_dynamic-update-slice_fusion.4.own_ref, ...), custom_call_target="tpu_custom_call" | custom-call | flops 1161953280 | bytes 3025920 | tf_op jit(solution)/shard_map/pallas_call | solution.py:96
  77.9 0.0 collective-permute-done.8.far_ref
  78.0 2.7 %shard_map.94 = bf16[2,2,8,48,384]{4,3,2,1,0:T(8,128)(2,1)S(1)} custom-call(s32[1]{0:T(128)} %bitcast.core_ref, bf16[6,197,384]{2,1,0:T(8,128)(2,1)S(1)} %constant_dynamic-update-slice_fusion.own_ref, bf16[6,197,384]{2,1,0:T(8,128)(2,1)S(1)} %collective-permute-done.8.far_ref, bf16[384,768]{1,0:T(8,128)(2,1)S(1)} %get-tuple-element.15.turned_ref, ...), custom_call_target="tpu_custom_call" | custom-call | flops 697171968 | bytes 1815552 | tf_op jit(solution)/shard_map/pallas_call | solution.py:96
  80.7 19.6 %all_to_all.21 = bf16[4,8,48,384]{3,2,1,0:T(8,128)(2,1)S(1)} all-to-all(bf16[4,8,48,384]{3,2,1,0:T(8,128)(2,1)S(1)} %bitcast.20), channel_id=1, replica_groups=mesh['z'=8,'xlo'=2,'xhi'=2,'y'=8,'core'=2] {'xlo','xhi'}, dimensions={0} | all-to-all | bytes 2359296 | tf_op jit(solution)/shard_map/all_to_all | solution.py:162
  100.3 0.2 fusion
  100.4 19.2 %all_to_all.22 = bf16[8,48,384]{2,1,0:T(8,128)(2,1)S(1)} all-to-all(bf16[8,48,384]{2,1,0:T(8,128)(2,1)S(1)} %fusion), channel_id=1, replica_groups=mesh['z'=8,'xlo'=2,'xhi'=2,'y'=8,'core'=2] {'z'}, dimensions={0} | all-to-all | bytes 589824 | tf_op jit(solution)/shard_map/all_to_all | solution.py:164
  119.6 0.0 copy-done.2
  119.7 0.0 copy-done.4
  119.7 0.7 convert_subtract_fusion
  120.4 0.0 copy-done.5
  120.4 0.7 convert_subtract_fusion.1
  (14 shorter events, 0.2 us)
Async XLA Ops:
  1.7 14.0 %collective-permute-start.3 = (bf16[2,197,384]{2,1,0:T(8,128)(2,1)S(1)}, bf16[2,197,384]{2,1,0:T(8,128)(2,1)S(1)}, u32[]{:S(2)}, u32[]{:S(2)}) collective-permute-start(bf16[2,197,384]{2,1,0:T(8,128)(2,1)S(1)} %pad_maximum_fusion), channel_id=1, source_target_pairs={{0,14},{1,3},{2,0},{3,5},{4,2},{5,7},{6,4},{7,9},{8,6},{9,11},{10,... | collective-permute-start | bytes 907784 | tf_op jit(solution)/shard_map/ppermute | solution.py:135
  4.9 12.7 %collective-permute-start = (bf16[2,197,384]{2,1,0:T(8,128)(2,1)S(1)}, bf16[2,197,384]{2,1,0:T(8,128)(2,1)S(1)}, u32[]{:S(2)}, u32[]{:S(2)}) collective-permute-start(bf16[2,197,384]{2,1,0:T(8,128)(2,1)S(1)} %pad_maximum_fusion), channel_id=1, source_target_pairs={{0,2},{1,15},{2,4},{3,1},{4,6},{5,3},{6,8},{7,5},{8,10},{9,7},{10,... | collective-permute-start | bytes 907784 | tf_op jit(solution)/shard_map/ppermute | solution.py:134
  15.7 29.1 %collective-permute-start.4 = (bf16[2,197,384]{2,1,0:T(8,128)(2,1)S(1)}, bf16[2,197,384]{2,1,0:T(8,128)(2,1)S(1)}, u32[]{:S(2)}, u32[]{:S(2)}) collective-permute-start(bf16[2,197,384]{2,1,0:T(8,128)(2,1)S(1)} %collective-permute-done.3), channel_id=1, source_target_pairs={{0,14},{1,3},{2,0},{3,5},{4,2},{5,7},{6,4},{7,9},{8,6},{9,11},{10,... | collective-permute-start | bytes 907784 | tf_op jit(solution)/shard_map/ppermute | solution.py:135
  17.6 29.1 %collective-permute-start.1 = (bf16[2,197,384]{2,1,0:T(8,128)(2,1)S(1)}, bf16[2,197,384]{2,1,0:T(8,128)(2,1)S(1)}, u32[]{:S(2)}, u32[]{:S(2)}) collective-permute-start(bf16[2,197,384]{2,1,0:T(8,128)(2,1)S(1)} %collective-permute-done), channel_id=1, source_target_pairs={{0,2},{1,15},{2,4},{3,1},{4,6},{5,3},{6,8},{7,5},{8,10},{9,7},{10,... | collective-permute-start | bytes 907784 | tf_op jit(solution)/shard_map/ppermute | solution.py:134
  33.0 20.5 %copy-start = (bf16[197,384]{1,0:T(8,128)(2,1)S(1)}, bf16[197,384]{1,0:T(8,128)(2,1)}, u32[]{:S(2)}) copy-start(bf16[197,384]{1,0:T(8,128)(2,1)} %param.6) | copy-start | bytes 453892
  33.0 24.4 %all-to-all-start.1 = ((bf16[8,2,48,384]{3,2,1,0:T(8,128)(2,1)}), bf16[8,2,48,384]{3,2,1,0:T(8,128)(2,1)S(1)}, u32[]{:S(2)}, u32[]{:S(2)}) async-start(bf16[8,2,48,384]{3,2,1,0:T(8,128)(2,1)} %broadcast_in_dim.15), calls=%async_computation.1 | async-start | bytes 1179648 | tf_op jit(solution)/shard_map/all_to_all | solution.py:152
  43.3 10.8 %copy-start.1 = (bf16[197,384]{1,0:T(8,128)(2,1)S(1)}, bf16[197,384]{1,0:T(8,128)(2,1)}, u32[]{:S(2)}) copy-start(bf16[197,384]{1,0:T(8,128)(2,1)} %param.7) | copy-start | bytes 453892
  44.8 11.9 %collective-permute-start.5 = (bf16[2,197,384]{2,1,0:T(8,128)(2,1)S(1)}, bf16[2,197,384]{2,1,0:T(8,128)(2,1)S(1)}, u32[]{:S(2)}, u32[]{:S(2)}) collective-permute-start(bf16[2,197,384]{2,1,0:T(8,128)(2,1)S(1)} %collective-permute-done.4), channel_id=1, source_target_pairs={{0,14},{1,3},{2,0},{3,5},{4,2},{5,7},{6,4},{7,9},{8,6},{9,11},{10,... | collective-permute-start | bytes 907784 | tf_op jit(solution)/shard_map/ppermute | solution.py:135
  46.8 9.9 %collective-permute-start.2 = (bf16[2,197,384]{2,1,0:T(8,128)(2,1)S(1)}, bf16[2,197,384]{2,1,0:T(8,128)(2,1)S(1)}, u32[]{:S(2)}, u32[]{:S(2)}) collective-permute-start(bf16[2,197,384]{2,1,0:T(8,128)(2,1)S(1)} %collective-permute-done.1), channel_id=1, source_target_pairs={{0,2},{1,15},{2,4},{3,1},{4,6},{5,3},{6,8},{7,5},{8,10},{9,7},{10,... | collective-permute-start | bytes 907784 | tf_op jit(solution)/shard_map/ppermute | solution.py:134
  54.8 17.5 %collective-permute-start.9 = (bf16[10,197,384]{2,1,0:T(8,128)(2,1)}, bf16[10,197,384]{2,1,0:T(8,128)(2,1)}, u32[]{:S(2)}, u32[]{:S(2)}) collective-permute-start(bf16[10,197,384]{2,1,0:T(8,128)(2,1)} %constant_dynamic-update-slice_fusion.4.own_ref), channel_id=1, source_target_pairs={{0,1},{1,0},{2,3},{3,2},{4,5},{5,4},{6,7},{7,6},{8,9},{9,8},{10,11... | collective-permute-start | bytes 4538888 | tf_op jit(solution)/shard_map/ppermute | solution.py:130
  57.4 7.8 %collective-permute-start.6 = (bf16[1,197,384]{2,1,0:T(8,128)(2,1)S(1)}, bf16[1,197,384]{2,1,0:T(8,128)(2,1)S(1)}, u32[]{:S(2)}, u32[]{:S(2)}) collective-permute-start(bf16[1,197,384]{2,1,0:T(8,128)(2,1)S(1)} %slice.18), channel_id=1, source_target_pairs={{0,2},{1,15},{2,4},{3,1},{4,6},{5,3},{6,8},{7,5},{8,10},{9,7},{10,... | collective-permute-start | bytes 453896 | tf_op jit(solution)/shard_map/ppermute | solution.py:137
  62.0 8.3 %collective-permute-start.7 = (bf16[1,197,384]{2,1,0:T(8,128)(2,1)S(1)}, bf16[1,197,384]{2,1,0:T(8,128)(2,1)S(1)}, u32[]{:S(2)}, u32[]{:S(2)}) collective-permute-start(bf16[1,197,384]{2,1,0:T(8,128)(2,1)S(1)} %slice.19), channel_id=1, source_target_pairs={{0,14},{1,3},{2,0},{3,5},{4,2},{5,7},{6,4},{7,9},{8,6},{9,11},{10,... | collective-permute-start | bytes 453896 | tf_op jit(solution)/shard_map/ppermute | solution.py:137
  70.3 7.6 %collective-permute-start.8 = (bf16[6,197,384]{2,1,0:T(8,128)(2,1)S(1)}, bf16[6,197,384]{2,1,0:T(8,128)(2,1)S(1)}, u32[]{:S(2)}, u32[]{:S(2)}) collective-permute-start(bf16[6,197,384]{2,1,0:T(8,128)(2,1)S(1)} %constant_dynamic-update-slice_fusion.own_ref), channel_id=1, source_target_pairs={{0,1},{1,0},{2,3},{3,2},{4,5},{5,4},{6,7},{7,6},{8,9},{9,8},{10,11... | collective-permute-start | bytes 2723336 | tf_op jit(solution)/shard_map/ppermute | solution.py:130
  100.2 19.4 %copy-start.2 = (bf16[96,48]{0,1:T(8,128)(2,1)S(1)}, bf16[96,48]{0,1:T(8,128)(2,1)}, u32[]{:S(2)}) copy-start(bf16[96,48]{0,1:T(8,128)(2,1)} %param.9) | copy-start | bytes 27652
  100.2 19.4 %copy-start.4 = (f32[96,48]{0,1:T(8,128)S(1)}, f32[96,48]{0,1:T(8,128)}, u32[]{:S(2)}) copy-start(f32[96,48]{0,1:T(8,128)} %param.11) | copy-start | bytes 55300
  100.3 20.1 %copy-start.3 = (bf16[48,96]{1,0:T(8,128)(2,1)S(1)}, bf16[48,96]{1,0:T(8,128)(2,1)}, u32[]{:S(2)}) copy-start(bf16[48,96]{1,0:T(8,128)(2,1)} %param.8) | copy-start | bytes 27652
  100.3 20.1 %copy-start.5 = (f32[48,96]{1,0:T(8,128)S(1)}, f32[48,96]{1,0:T(8,128)}, u32[]{:S(2)}) copy-start(f32[48,96]{1,0:T(8,128)} %param.10) | copy-start | bytes 55300

commit v6 on v4

--- a/solution.py
+++ b/solution.py
@@ -12,8 +12,8 @@
 DP = ("z", "xlo")
 MP = ("xhi", "y", "core")
 GROUP = ("y", "core")
-OWNERS = ("z", "xlo", "xhi")
-STEP = 2
+OWNERS = ("xlo", "xhi", "z")
+STEP = 4
 BF16 = jnp.bfloat16
 F32 = jnp.float32
 ROOT = math.sqrt(2.0 / math.pi)
@@ -36,7 +36,10 @@
 
     terms = []
     for n in range(STEP):
-        x, c = (jnp.concatenate([xc_ref[2 * n, k], xc_ref[2 * n + 1, k]], axis=1) for k in (0, 1))
+        halves = (xc_ref[2 * n], xc_ref[2 * n + 1])
+        part = halves[0].shape[1] // 2
+        x = jnp.concatenate([h[:, :part] for h in halves], axis=1)
+        c = jnp.concatenate([h[:, part:] for h in halves], axis=1)
         pre = dot(w_in_ref[...], x, ((1,), (1,)))
         back = dot(w_out_ref[...], c, ((1,), (1,)))
         act, slope = gelu_parts(pre)
@@ -65,25 +68,25 @@
 
     @pl.when(step == pl.num_programs(0) - 1)
     def _():
-        blocks, cols, rows, packed = out_ref.shape
+        pairs, cols, deep, rows, packed = out_ref.shape
         width = packed // 4
         for h in range(cols):
             part = slice(h * width, (h + 1) * width)
             both = [r[part, :] for r in (sum_in, sq_in, sum_out, sq_out)]
             turned = jnp.concatenate(both, axis=0).T.astype(BF16)
-            for k in range(blocks):
-                out_ref[k, h] = turned[k * rows : (k + 1) * rows]
+            for k in range(deep * pairs):
+                out_ref[k % pairs, h, k // pairs] = turned[k * rows : (k + 1) * rows]
 
 
 def grads(xc, w_in_t, w_out, shape):
     hid, d = w_in_t.shape
-    pieces, two, seq, part = xc.shape
-    per = STEP * d // part
+    pieces, seq, part = xc.shape
+    per = STEP * 2 * d // part
     whole = pl.BlockSpec((hid, d), lambda i: (0, 0))
     return pl.pallas_call(
         grads_kernel,
         grid=(pieces // per,),
-        in_specs=[pl.BlockSpec((per, two, seq, part), lambda i: (i, 0, 0, 0)), whole, whole],
+        in_specs=[pl.BlockSpec((per, seq, part), lambda i: (i, 0, 0)), whole, whole],
         out_specs=pl.BlockSpec(shape, lambda i: (0,) * len(shape)),
         out_shape=jax.ShapeDtypeStruct(shape, BF16),
         scratch_shapes=[pltpu.VMEM((hid, d), F32)] * 4,
@@ -95,17 +98,17 @@
     d_own, h_own = w_in.shape
     cols, pairs, deep = (lax.axis_size(a) for a in ("xhi", "xlo", "z"))
     dp = deep * pairs
-    xc = lax.all_gather(jnp.stack([inputs, cotangent]), GROUP)
+    xc = lax.all_gather(jnp.concatenate([inputs, cotangent], axis=1), GROUP)
     both = jnp.concatenate([w_in, w_out.T], axis=0)
     both = jnp.broadcast_to(both[None], (cols * dp, *both.shape))
     weights = lax.all_to_all(both, OWNERS, 0, 0, tiled=True)
-    weights = weights.reshape(dp, cols, 2, d_own, h_own).transpose(2, 1, 4, 0, 3)
+    weights = weights.reshape(pairs, cols, deep, 2, d_own, h_own).transpose(3, 1, 5, 2, 0, 4)
     weights = weights.reshape(2, cols * h_own, dp * d_own)
-    pieces = grads(xc, weights[0], weights[1], (dp, cols, d_own, 4 * h_own))
+    pieces = grads(xc, weights[0], weights[1], (pairs, cols, deep, d_own, 4 * h_own))
     pieces = lax.all_to_all(pieces.reshape(dp * cols, d_own, 4 * h_own), OWNERS, 0, 0, tiled=True)
     total = jnp.sum(pieces.astype(F32), axis=0)
     sum_in, sq_in, sum_out, sq_out = jnp.split(total, 4, axis=1)
-    images = xc.shape[0] * xc.shape[3] // (dp * d_own) * cols * dp
+    images = lax.axis_size("y") * cols * dp
     scale = 1.0 / images
     new_prec_in = 0.6 * prec_in + 0.4 * sq_in * scale
     new_prec_out = 0.6 * prec_out + 0.4 * sq_out.T * scale

time: 120 us -> 120 us (level)
  waiting for transfers between devices: 10.2 us -> 8.86 us
    another operation x1 -> x0, other arithmetic: 1.75 us -> none  [per_device(): xc = lax.all_gather(jnp.stack([inputs, cotangent]), GROUP)]
    unnamed x0 -> x1, other arithmetic: none -> 1.74 us
    all_gather x1, waiting for transfers between devices: 10.2 us -> 8.85 us  [per_device(): xc = lax.all_gather(jnp.concatenate([inputs, cotangent], axis=1), GROUP)]
  transfers between devices with their start and end apart: 1 -> 1, of which waited for: 1 -> 1; matrix products, arithmetic and copies ran while one was open for 3% -> 4% of each run, Pallas kernels for 0% -> 0%
where the time goes in v6:
time: 120 us; the launch traced here: 119 us
  blocking collectives  79.8 us (66%)
  between operations  14.1 us (12%)
  waiting for transfers between devices  8.86 us (7%)
  Pallas kernels  7.39 us (6%)
  local copies, waits for them, and re-layouts  4.4 us (4%)
  other arithmetic  4.04 us (3%)
    all_to_all x1, blocking collectives, per_device(): lax.all_to_all(pieces.reshape(dp * cols, d_own, 4 * h_own), OWNERS, 0, 0,...  43.4 us
    all_to_all x1, blocking collectives, per_device(): weights = lax.all_to_all(both, OWNERS, 0, 0, tiled=True)  36.3 us
    all_gather x1, waiting for transfers between devices, per_device(): xc = lax.all_gather(jnp.concatenate([inputs, cotangent], axis=1), GROUP)  8.85 us
    pallas_call x1, Pallas kernels, grads(): pl.pallas_call(grads_kernel, grid=(pieces // per,), in_specs=[pl.BlockSpe...  7.39 us
  transfers between devices with their start and end apart: 1, of which 1 were waited for; matrix products, arithmetic and copies ran while one was open for 4% of the time, Pallas kernels for 0%

profile of v6, /device:TPU:56, one launch (start us, length us, event | category | flops | bytes accessed | tf_op | source)
XLA Modules:
  0.0 118.6 jit_solution(5571449007653441534)
XLA Ops:
  7.2 0.0 all-gather.4.cloned.1.call-start
  7.2 1.7 %maximum_bitcast_fusion = bf16[1,197,768]{2,1,0:T(8,128)(2,1)} fusion(bf16[197,384]{1,0:T(8,128)(2,1)} %param.7, bf16[197,384]{1,0:T(8,128)(2,1)} %param.6), kind=kLoop, calls=%fused_computation.1 | loop fusion | flops 605184 | bytes 605184
  9.0 0.0 all-gather.4.cloned.1.call-update
  9.0 0.7 pad_maximum_fusion
  9.7 0.1 broadcast_in_dim.2
  9.8 36.3 %all_to_all.10 = bf16[32,96,96]{2,1,0:T(8,128)(2,1)S(1)} all-to-all(bf16[32,96,96]{2,1,0:T(8,128)(2,1)S(1)} %broadcast_in_dim.2), channel_id=1, replica_groups=mesh['z'=8,'xlo'=2,'xhi'=2,'y'=8,'core'=2] {'xlo','xhi','z'}, dimensions={0} | all-to-all | bytes 1179648 | tf_op jit(solution)/shard_map/all_to_all | solution.py:104
  46.2 0.1 fusion.10
  46.2 1.1 copy.19
  47.3 0.8 reshape.27.w_out_ref
  48.1 1.1 copy.18
  49.1 0.8 reshape.26.w_in_ref
  49.9 8.8 %all-gather.4.cloned.1.call-done.xc_ref = bf16[16,197,768]{2,1,0:T(8,128)(2,1)} async-done(((bf16[1,197,768]{2,1,0:T(8,128)(2,1)}), bf16[16,197,768]{2,1,0:T(8,128)(2,1)}) %all-gather.4.cloned.1.call-update) | async-done | bytes 4841488 | tf_op jit(solution)/shard_map/all_gather | solution.py:101
  58.7 7.4 %shard_map.93 = bf16[2,2,8,48,384]{4,3,2,1,0:T(8,128)(2,1)S(1)} custom-call(bf16[16,197,768]{2,1,0:T(8,128)(2,1)} %all-gather.4.cloned.1.call-done.xc_ref, bf16[192,768]{1,0:T(8,128)(2,1)S(1)} %reshape.26.w_in_ref, bf16[192,768]{1,0:T(8,128)(2,1)S(1)} %reshape.27.w_out_ref), custom_call_target="tpu_custom_call" | custom-call | tf_op jit(solution)/shard_map/pallas_call | solution.py:86
  66.1 43.4 %all_to_all.11 = bf16[32,48,384]{2,1,0:T(8,128)(2,1)S(1)} all-to-all(bf16[32,48,384]{2,1,0:T(8,128)(2,1)S(1)} %bitcast.16), channel_id=1, replica_groups=mesh['z'=8,'xlo'=2,'xhi'=2,'y'=8,'core'=2] {'xlo','xhi','z'}, dimensions={0} | all-to-all | bytes 2359296 | tf_op jit(solution)/shard_map/all_to_all | solution.py:108
  109.6 0.0 copy-start
  109.6 0.0 copy-start.2
  109.6 0.0 copy-start.1
  109.6 0.0 copy-start.3
  109.6 0.2 convert_reduce_fusion
  109.8 0.5 copy-done
  110.3 0.0 copy-done.2
  110.3 0.7 convert_subtract_fusion
  111.0 0.0 copy-done.1
  111.0 0.0 copy-done.3
  111.0 0.7 convert_subtract_fusion.1
Async XLA Ops:
  7.2 51.6 %all-gather.4.cloned.1.call-start = ((), (), s32[]{:S(2)}) async-start(), calls=%async_computation.2 | async-start | bytes 5222400 | tf_op jit(solution)/shard_map/all_gather | solution.py:101
  109.6 0.7 copy-start
  109.6 0.8 copy-start.2
  109.6 1.4 %copy-start.1 = (bf16[48,96]{1,0:T(8,128)(2,1)S(1)}, bf16[48,96]{1,0:T(8,128)(2,1)}, u32[]{:S(2)}) copy-start(bf16[48,96]{1,0:T(8,128)(2,1)} %param.8) | copy-start | bytes 27652
  109.6 1.4 %copy-start.3 = (f32[48,96]{1,0:T(8,128)S(1)}, f32[48,96]{1,0:T(8,128)}, u32[]{:S(2)}) copy-start(f32[48,96]{1,0:T(8,128)} %param.10) | copy-start | bytes 55300
Sparse Core Ops, SparseCore 0:
  10.1 48.5 all-gather.3

commit v7 on v6

--- a/solution.py
+++ b/solution.py
@@ -13,7 +13,8 @@
 MP = ("xhi", "y", "core")
 GROUP = ("y", "core")
 OWNERS = ("xlo", "xhi", "z")
-STEP = 4
+ROW = ("xlo", "xhi")
+STEP = 2
 BF16 = jnp.bfloat16
 F32 = jnp.float32
 ROOT = math.sqrt(2.0 / math.pi)
@@ -94,6 +95,20 @@
     )(xc, w_in_t, w_out)
 
 
+def update_kernel(pieces_ref, w_in_ref, w_out_ref, prec_in_ref, prec_out_ref, *outs, scale):
+    total = pieces_ref[0].astype(F32)
+    for k in range(1, pieces_ref.shape[0]):
+        total += pieces_ref[k].astype(F32)
+    width = w_in_ref.shape[1]
+    for n, (w_ref, prec_ref) in enumerate(((w_in_ref, prec_in_ref), (w_out_ref, prec_out_ref))):
+        grad = total[:, 2 * n * width : (2 * n + 1) * width]
+        square = total[:, (2 * n + 1) * width : (2 * n + 2) * width]
+        prec = 0.6 * prec_ref[...] + 0.4 * square * scale
+        w = w_ref[...].astype(F32)
+        outs[n][...] = prec
+        outs[2 + n][...] = w - 1.0 * (grad * scale + 0.1 * w) / (prec + 0.1)
+
+
 def per_device(inputs, cotangent, w_in, w_out, prec_in, prec_out):
     d_own, h_own = w_in.shape
     cols, pairs, deep = (lax.axis_size(a) for a in ("xhi", "xlo", "z"))
@@ -105,18 +120,16 @@
     weights = weights.reshape(pairs, cols, deep, 2, d_own, h_own).transpose(3, 1, 5, 2, 0, 4)
     weights = weights.reshape(2, cols * h_own, dp * d_own)
     pieces = grads(xc, weights[0], weights[1], (pairs, cols, deep, d_own, 4 * h_own))
-    pieces = lax.all_to_all(pieces.reshape(dp * cols, d_own, 4 * h_own), OWNERS, 0, 0, tiled=True)
-    total = jnp.sum(pieces.astype(F32), axis=0)
-    sum_in, sq_in, sum_out, sq_out = jnp.split(total, 4, axis=1)
+    pieces = pieces.reshape(pairs * cols, deep, d_own, 4 * h_own)
+    pieces = lax.all_to_all(pieces, ROW, 0, 0, tiled=True)
+    pieces = sum(pieces[k].astype(F32) for k in range(cols * pairs)).astype(BF16)
+    pieces = lax.all_to_all(pieces, "z", 0, 0, tiled=True)
     images = lax.axis_size("y") * cols * dp
-    scale = 1.0 / images
-    new_prec_in = 0.6 * prec_in + 0.4 * sq_in * scale
-    new_prec_out = 0.6 * prec_out + 0.4 * sq_out.T * scale
-    w_in_own = w_in.astype(F32)
-    w_out_own = w_out.astype(F32)
-    new_w_in = w_in_own - 1.0 * (sum_in * scale + 0.1 * w_in_own) / (new_prec_in + 0.1)
-    new_w_out = w_out_own - 1.0 * (sum_out.T * scale + 0.1 * w_out_own) / (new_prec_out + 0.1)
-    return (new_prec_in, new_prec_out, new_w_in, new_w_out)
+    new_prec_in, new_prec_out, new_w_in, new_w_out = pl.pallas_call(
+        functools.partial(update_kernel, scale=1.0 / images),
+        out_shape=[jax.ShapeDtypeStruct((d_own, h_own), F32)] * 4,
+    )(pieces, w_in, w_out.T, prec_in, prec_out.T)
+    return (new_prec_in, new_prec_out.T, new_w_in, new_w_out.T)
 
 
 def solution(mesh):

time: 120 us -> 116 us (0.967)
  blocking collectives: 79.8 us -> 76 us
  Pallas kernels: 7.39 us -> 9.12 us
  other arithmetic: 4.04 us -> 2.62 us
    all_to_all x1 -> x2, blocking collectives: 43.4 us -> 39.7 us  [the longest x1 20.7 us: per_device(): pieces = lax.all_to_all(pieces, ROW, 0, 0, tiled=True)]
    pallas_call x0 -> x1, Pallas kernels: none -> 1.85 us  [per_device(): pl.pallas_call(functools.partial(update_kernel, scale=1.0 / images), out_...]
    sub x2 -> x0, other arithmetic: 1.39 us -> none  [the longest x1 0.7 us: per_device(): w_in_own - 1.0 * (sum_in * scale + 0.1 * w_in_own) / (new_prec_in + 0.1)]
where the time goes in v7:
time: 116 us; the launch traced here: 115 us
  blocking collectives  76 us (66%)
  between operations  14.1 us (12%)
  Pallas kernels  9.12 us (8%)
  waiting for transfers between devices  8.87 us (8%)
  local copies, waits for them, and re-layouts  3.81 us (3%)
  other arithmetic  2.62 us (2%)
    all_to_all x1, blocking collectives, per_device(): weights = lax.all_to_all(both, OWNERS, 0, 0, tiled=True)  36.3 us
    all_to_all x1, blocking collectives, per_device(): pieces = lax.all_to_all(pieces, ROW, 0, 0, tiled=True)  20.7 us
    all_to_all x1, blocking collectives, per_device(): pieces = lax.all_to_all(pieces, 'z', 0, 0, tiled=True)  19 us
    all_gather x1, waiting for transfers between devices, per_device(): xc = lax.all_gather(jnp.concatenate([inputs, cotangent], axis=1), GROUP)  8.85 us
    pallas_call x1, Pallas kernels, grads(): pl.pallas_call(grads_kernel, grid=(pieces // per,), in_specs=[pl.BlockSpe...  7.27 us
  transfers between devices with their start and end apart: 1, of which 1 were waited for; matrix products, arithmetic and copies ran while one was open for 4% of the time, Pallas kernels for 0%

profile of v7, /device:TPU:56, one launch (start us, length us, event | category | flops | bytes accessed | tf_op | source)
XLA Modules:
  0.0 114.5 jit_solution(15044863236623852239)
XLA Ops:
  7.2 0.0 all-gather.4.cloned.1.call-start
  7.2 1.7 %maximum_bitcast_fusion = bf16[1,197,768]{2,1,0:T(8,128)(2,1)} fusion(bf16[197,384]{1,0:T(8,128)(2,1)} %param.7, bf16[197,384]{1,0:T(8,128)(2,1)} %param.6), kind=kLoop, calls=%fused_computation.1 | loop fusion | flops 605184 | bytes 605184
  8.9 0.0 all-gather.4.cloned.1.call-update
  9.0 0.7 pad_maximum_fusion
  9.7 0.1 broadcast_in_dim.2
  9.8 36.3 %all_to_all.15 = bf16[32,96,96]{2,1,0:T(8,128)(2,1)S(1)} all-to-all(bf16[32,96,96]{2,1,0:T(8,128)(2,1)S(1)} %broadcast_in_dim.2), channel_id=1, replica_groups=mesh['z'=8,'xlo'=2,'xhi'=2,'y'=8,'core'=2] {'xlo','xhi','z'}, dimensions={0} | all-to-all | bytes 1179648 | tf_op jit(solution)/shard_map/all_to_all | solution.py:119
  46.2 0.1 fusion.1
  46.2 1.1 copy.19
  47.3 0.8 reshape.35.w_out_ref
  48.1 1.1 copy.18
  49.1 0.8 reshape.34.w_in_ref
  49.9 8.9 %all-gather.4.cloned.1.call-done.xc_ref = bf16[16,197,768]{2,1,0:T(8,128)(2,1)} async-done(((bf16[1,197,768]{2,1,0:T(8,128)(2,1)}), bf16[16,197,768]{2,1,0:T(8,128)(2,1)}) %all-gather.4.cloned.1.call-update) | async-done | bytes 4841488 | tf_op jit(solution)/shard_map/all_gather | solution.py:116
  58.7 7.3 %shard_map.93 = bf16[2,2,8,48,384]{4,3,2,1,0:T(8,128)(2,1)S(1)} custom-call(bf16[16,197,768]{2,1,0:T(8,128)(2,1)} %all-gather.4.cloned.1.call-done.xc_ref, bf16[192,768]{1,0:T(8,128)(2,1)S(1)} %reshape.34.w_in_ref, bf16[192,768]{1,0:T(8,128)(2,1)S(1)} %reshape.35.w_out_ref), custom_call_target="tpu_custom_call" | custom-call | tf_op jit(solution)/shard_map/pallas_call | solution.py:87
  66.0 20.7 %all_to_all.16 = bf16[4,8,48,384]{3,2,1,0:T(8,128)(2,1)S(1)} all-to-all(bf16[4,8,48,384]{3,2,1,0:T(8,128)(2,1)S(1)} %bitcast.12), channel_id=1, replica_groups=mesh['z'=8,'xlo'=2,'xhi'=2,'y'=8,'core'=2] {'xlo','xhi'}, dimensions={0} | all-to-all | bytes 2359296 | tf_op jit(solution)/shard_map/all_to_all | solution.py:124
  86.7 0.1 fusion
  86.8 19.0 %all_to_all.17.pieces_ref = bf16[8,48,384]{2,1,0:T(8,128)(2,1)} all-to-all(bf16[8,48,384]{2,1,0:T(8,128)(2,1)S(1)} %fusion), channel_id=1, replica_groups=mesh['z'=8,'xlo'=2,'xhi'=2,'y'=8,'core'=2] {'z'}, dimensions={0} | all-to-all | bytes 589824 | tf_op jit(solution)/shard_map/all_to_all | solution.py:126
  105.9 1.8 %shard_map.94 = (f32[48,96]{1,0:T(8,128)}, f32[48,96]{1,0:T(8,128)}, f32[48,96]{1,0:T(8,128)}, f32[48,96]{1,0:T(8,128)}) custom-call(bf16[8,48,384]{2,1,0:T(8,128)(2,1)} %all_to_all.17.pieces_ref, bf16[48,96]{1,0:T(8,128)(2,1)} %w_in_ref.1, bf16[48,96]{1,0:T(8,128)(2,1)} %bitcast.15, f32[48,96]{1,0:T(8,128)} %prec_in_ref.1, f32[48,96]{1,0:T(8,128)} %bitcast.16), custom_call_target="tpu_custom_call" | custom-call | tf_op jit(solution)/shard_map/pallas_call | solution.py:128
Async XLA Ops:
  7.2 51.6 %all-gather.4.cloned.1.call-start = ((), (), s32[]{:S(2)}) async-start(), calls=%async_computation.3 | async-start | bytes 5222400 | tf_op jit(solution)/shard_map/all_gather | solution.py:116
Sparse Core Ops, SparseCore 0:
  10.1 48.5 all-gather.3

commit v8 on v5

--- a/solution.py
+++ b/solution.py
@@ -1,3 +1,4 @@
+import functools
 import math
 import jax
 import jax.numpy as jnp
@@ -11,11 +12,13 @@
 DP = ("z", "xlo")
 MP = ("xhi", "y", "core")
 GROUP = ("y", "core")
+OWNERS = ("xlo", "xhi", "z")
 ROW = ("xlo", "xhi")
 BF16 = jnp.bfloat16
 F32 = jnp.float32
 ROOT = math.sqrt(2.0 / math.pi)
 CUBE = 0.044715
+TURN_FLOPS = 1 << 34
 
 
 def gelu_parts(v):
@@ -53,10 +56,21 @@
         ref[...] += term
 
 
-def first_kernel(core_ref, own_ref, far_ref, weights_ref, turned_ref, *sums):
+def turn_kernel(arrived_ref, turned_ref, *, pairs, cols, deep):
+    own, width = arrived_ref.shape[1] // 2, arrived_ref.shape[2]
+    for n in range(2):
+        for h in range(cols):
+            blocks = [
+                arrived_ref[(k % pairs * cols + h) * deep + k // pairs, n * own : (n + 1) * own, :]
+                for k in range(deep * pairs)
+            ]
+            rows = slice((n * cols + h) * width, (n * cols + h + 1) * width)
+            turned_ref[rows, :] = jnp.concatenate(blocks, axis=0).T
+
+
+def first_kernel(core_ref, own_ref, far_ref, turned_ref, *sums):
     @pl.when(pl.program_id(0) == 0)
     def _():
-        turned_ref[...] = weights_ref[...].T
         for ref in sums:
             ref[...] = jnp.zeros_like(ref)
 
@@ -87,7 +101,7 @@
 def run_images(kernel, core, own, far, weights, sums, outs):
     pieces, seq, part = own.shape
     last = pieces // 2 - 1
-    hid, d = outs[-1].shape if sums == () else sums[0].shape
+    hid, d = outs[0].shape if sums == () else sums[0].shape
     block = (2, seq, part)
 
     def whole(a):
@@ -115,7 +129,7 @@
     )(core, own, far, weights, *sums)
 
 
-def round_the_ring(own, weights):
+def round_the_ring(own):
     n, cores = lax.axis_size("y"), lax.axis_size("core")
 
     def turned(step):
@@ -133,11 +147,24 @@
     for _ in range(n // 2 - 1):
         up.append(lax.ppermute(up[-1], GROUP, turned(1)))
         down.append(lax.ppermute(down[-1], GROUP, turned(-1)))
-    up[3], down[3], weights = lax.optimization_barrier((up[3], down[3], weights))
     opposite = [lax.ppermute(up[3][:1], GROUP, turned(1)), lax.ppermute(down[3][1:], GROUP, turned(-1))]
     early = jnp.concatenate([up[1], down[1], up[2], down[2], own])
     late = jnp.concatenate([up[3], down[3], *opposite])
-    return (early, swap(early)), (late, swap(late)), weights
+    return (early, swap(early)), (late, swap(late))
+
+
+def update_kernel(pieces_ref, w_in_ref, w_out_ref, prec_in_ref, prec_out_ref, *outs, scale):
+    total = pieces_ref[0].astype(F32)
+    for k in range(1, pieces_ref.shape[0]):
+        total += pieces_ref[k].astype(F32)
+    width = w_in_ref.shape[1]
+    for n, (w_ref, prec_ref) in enumerate(((w_in_ref, prec_in_ref), (w_out_ref, prec_out_ref))):
+        grad = total[:, 2 * n * width : (2 * n + 1) * width]
+        square = total[:, (2 * n + 1) * width : (2 * n + 2) * width]
+        prec = 0.6 * prec_ref[...] + 0.4 * square * scale
+        w = w_ref[...].astype(F32)
+        outs[n][...] = prec
+        outs[2 + n][...] = w - 1.0 * (grad * scale + 0.1 * w) / (prec + 0.1)
 
 
 def per_device(inputs, cotangent, w_in, w_out, prec_in, prec_out):
@@ -145,33 +172,30 @@
     cols, pairs, deep = (lax.axis_size(a) for a in ("xhi", "xlo", "z"))
     dp = deep * pairs
     hid = cols * h_own
-    both = jnp.concatenate([w_in, w_out.T], axis=1)
-    both = jnp.broadcast_to(both[None], (pairs * cols, *both.shape))
-    both = lax.all_to_all(both, ROW, 0, 0, tiled=True).reshape(pairs, cols, d_own, 2, h_own)
-    both = both.transpose(0, 2, 3, 1, 4).reshape(pairs, d_own, 2 * hid)
-    weights = lax.all_to_all(jnp.broadcast_to(both[None], (deep, *both.shape)), "z", 0, 0, tiled=True)
-    weights = weights.reshape(dp * d_own, 2 * hid)
-    early, late, weights = round_the_ring(jnp.stack([inputs, cotangent]), weights)
+    both = jnp.concatenate([w_in, w_out.T], axis=0)
+    both = jnp.broadcast_to(both[None], (cols * dp, *both.shape))
+    arrived = lax.all_to_all(both, OWNERS, 0, 0, tiled=True)
+    turned = pl.pallas_call(
+        functools.partial(turn_kernel, pairs=pairs, cols=cols, deep=deep),
+        out_shape=jax.ShapeDtypeStruct((2 * hid, dp * d_own), BF16),
+        cost_estimate=pl.CostEstimate(flops=TURN_FLOPS, bytes_accessed=4 * arrived.size, transcendentals=0),
+    )(arrived)
+    early, late = round_the_ring(jnp.stack([inputs, cotangent]))
     core = lax.axis_index("core").reshape(1).astype(jnp.int32)
-    turned = jax.ShapeDtypeStruct((2 * hid, dp * d_own), BF16)
     partial = [jax.ShapeDtypeStruct((hid, dp * d_own), F32)] * 4
     packed = jax.ShapeDtypeStruct((pairs, cols, deep, d_own, 4 * h_own), BF16)
-    turned, *partial = run_images(first_kernel, core, *early, weights, (), [turned, *partial])
+    partial = run_images(first_kernel, core, *early, turned, (), partial)
     (pieces,) = run_images(last_kernel, core, *late, turned, tuple(partial), [packed])
     pieces = pieces.reshape(pairs * cols, deep, d_own, 4 * h_own)
     pieces = lax.all_to_all(pieces, ROW, 0, 0, tiled=True)
     pieces = sum(pieces[k].astype(F32) for k in range(cols * pairs)).astype(BF16)
     pieces = lax.all_to_all(pieces, "z", 0, 0, tiled=True)
-    total = jnp.sum(pieces.astype(F32), axis=0)
-    sum_in, sq_in, sum_out, sq_out = jnp.split(total, 4, axis=1)
-    scale = 1.0 / (lax.axis_size("y") * cols * dp)
-    new_prec_in = 0.6 * prec_in + 0.4 * sq_in * scale
-    new_prec_out = 0.6 * prec_out + 0.4 * sq_out.T * scale
-    w_in_own = w_in.astype(F32)
-    w_out_own = w_out.astype(F32)
-    new_w_in = w_in_own - 1.0 * (sum_in * scale + 0.1 * w_in_own) / (new_prec_in + 0.1)
-    new_w_out = w_out_own - 1.0 * (sum_out.T * scale + 0.1 * w_out_own) / (new_prec_out + 0.1)
-    return (new_prec_in, new_prec_out, new_w_in, new_w_out)
+    images = lax.axis_size("y") * cols * dp
+    new_prec_in, new_prec_out, new_w_in, new_w_out = pl.pallas_call(
+        functools.partial(update_kernel, scale=1.0 / images),
+        out_shape=[jax.ShapeDtypeStruct((d_own, h_own), F32)] * 4,
+    )(pieces, w_in, w_out.T, prec_in, prec_out.T)
+    return (new_prec_in, new_prec_out.T, new_w_in, new_w_out.T)
 
 
 def solution(mesh):

time: 122 us -> 117 us (0.959)
  the two profiles are of different devices: /device:TPU:56 before, /device:TPU:24 now
where the time goes in v8:
time: 117 us; the launch traced here: 116 us
  starting transfers between devices  45.8 us (39%)
  blocking collectives  39.6 us (34%)
  waiting for transfers between devices  13.6 us (12%)
  Pallas kernels  11.9 us (10%)
  local copies, waits for them, and re-layouts  2.47 us (2%)
  other arithmetic  1.91 us (2%)
    all_to_all x1, blocking collectives, per_device(): pieces = lax.all_to_all(pieces, ROW, 0, 0, tiled=True)  20.9 us
    all_to_all x1, blocking collectives, per_device(): pieces = lax.all_to_all(pieces, 'z', 0, 0, tiled=True)  18.7 us
    ppermute x3, starting transfers between devices, round_the_ring(): up.append(lax.ppermute(up[-1], GROUP, turned(1)))  15.4 us
    all_to_all x1, starting transfers between devices, per_device(): arrived = lax.all_to_all(both, OWNERS, 0, 0, tiled=True)  13.3 us
    pallas_call x2, Pallas kernels, run_images(): pl.pallas_call(kernel, grid=(last + 1,), in_specs=[pl.BlockSpec(memory_sp...  7.88 us
    ppermute x3, waiting for transfers between devices, round_the_ring(): up.append(lax.ppermute(up[-1], GROUP, turned(1)))  7.3 us
    ppermute x3, starting transfers between devices, round_the_ring(): down.append(lax.ppermute(down[-1], GROUP, turned(-1)))  5.76 us
    ppermute x1, starting transfers between devices, round_the_ring(): lax.ppermute(up[3][:1], GROUP, turned(1))  5.6 us
  transfers between devices with their start and end apart: 11, of which 4 were waited for; matrix products, arithmetic and copies ran while one was open for 2% of the time, Pallas kernels for 6%

profile of v8, /device:TPU:24, one launch (start us, length us, event | category | flops | bytes accessed | tf_op | source)
XLA Modules:
  0.0 116.2 jit_solution(14189942109562993538)
XLA Ops:
  0.6 1.0 pad_maximum_fusion
  1.7 4.7 %collective-permute-start = (bf16[2,197,384]{2,1,0:T(8,128)(2,1)S(1)}, bf16[2,197,384]{2,1,0:T(8,128)(2,1)S(1)}, u32[]{:S(2)}, u32[]{:S(2)}) collective-permute-start(bf16[2,197,384]{2,1,0:T(8,128)(2,1)S(1)} %pad_maximum_fusion), channel_id=1, source_target_pairs={{0,2},{1,15},{2,4},{3,1},{4,6},{5,3},{6,8},{7,5},{8,10},{9,7},{10,... | collective-permute-start | bytes 907784 | tf_op jit(solution)/shard_map/ppermute | solution.py:148
  6.4 1.9 %collective-permute-start.3 = (bf16[2,197,384]{2,1,0:T(8,128)(2,1)S(1)}, bf16[2,197,384]{2,1,0:T(8,128)(2,1)S(1)}, u32[]{:S(2)}, u32[]{:S(2)}) collective-permute-start(bf16[2,197,384]{2,1,0:T(8,128)(2,1)S(1)} %pad_maximum_fusion), channel_id=1, source_target_pairs={{0,14},{1,3},{2,0},{3,5},{4,2},{5,7},{6,4},{7,9},{8,6},{9,11},{10,... | collective-permute-start | bytes 907784 | tf_op jit(solution)/shard_map/ppermute | solution.py:149
  8.3 4.8 %collective-permute-done = bf16[2,197,384]{2,1,0:T(8,128)(2,1)S(1)} collective-permute-done((bf16[2,197,384]{2,1,0:T(8,128)(2,1)S(1)}, bf16[2,197,384]{2,1,0:T(8,128)(2,1)S(1)}, u32[]{:S(2)}, u32[]{:S(2)}) %collective-permute-start) | collective-permute-done | bytes 302624 | tf_op jit(solution)/shard_map/ppermute | solution.py:148
  13.1 5.6 %collective-permute-start.1 = (bf16[2,197,384]{2,1,0:T(8,128)(2,1)S(1)}, bf16[2,197,384]{2,1,0:T(8,128)(2,1)S(1)}, u32[]{:S(2)}, u32[]{:S(2)}) collective-permute-start(bf16[2,197,384]{2,1,0:T(8,128)(2,1)S(1)} %collective-permute-done), channel_id=1, source_target_pairs={{0,2},{1,15},{2,4},{3,1},{4,6},{5,3},{6,8},{7,5},{8,10},{9,7},{10,... | collective-permute-start | bytes 907784 | tf_op jit(solution)/shard_map/ppermute | solution.py:148
  18.7 0.0 collective-permute-done.3
  18.7 1.9 %collective-permute-start.4 = (bf16[2,197,384]{2,1,0:T(8,128)(2,1)S(1)}, bf16[2,197,384]{2,1,0:T(8,128)(2,1)S(1)}, u32[]{:S(2)}, u32[]{:S(2)}) collective-permute-start(bf16[2,197,384]{2,1,0:T(8,128)(2,1)S(1)} %collective-permute-done.3), channel_id=1, source_target_pairs={{0,14},{1,3},{2,0},{3,5},{4,2},{5,7},{6,4},{7,9},{8,6},{9,11},{10,... | collective-permute-start | bytes 907784 | tf_op jit(solution)/shard_map/ppermute | solution.py:149
  20.6 0.7 pad_maximum_fusion.1
  21.3 1.0 broadcast_in_dim.2
  22.3 13.3 %all-to-all-start = ((bf16[32,96,96]{2,1,0:T(8,128)(2,1)}), bf16[32,96,96]{2,1,0:T(8,128)(2,1)}, u32[]{:S(2)}, u32[]{:S(2)}) async-start(bf16[32,96,96]{2,1,0:T(8,128)(2,1)} %broadcast_in_dim.2), calls=%async_computation | async-start | bytes 1572864 | tf_op jit(solution)/shard_map/all_to_all | solution.py:177
  35.6 0.0 copy-start.1
  35.6 0.0 copy-start.2
  35.7 0.1 constant_dynamic-update-slice_fusion.8
  35.7 0.0 collective-permute-done.1
  35.7 5.1 %collective-permute-start.2 = (bf16[2,197,384]{2,1,0:T(8,128)(2,1)S(1)}, bf16[2,197,384]{2,1,0:T(8,128)(2,1)S(1)}, u32[]{:S(2)}, u32[]{:S(2)}) collective-permute-start(bf16[2,197,384]{2,1,0:T(8,128)(2,1)S(1)} %collective-permute-done.1), channel_id=1, source_target_pairs={{0,2},{1,15},{2,4},{3,1},{4,6},{5,3},{6,8},{7,5},{8,10},{9,7},{10,... | collective-permute-start | bytes 907784 | tf_op jit(solution)/shard_map/ppermute | solution.py:148
  40.9 0.0 collective-permute-done.4
  40.9 1.9 %collective-permute-start.5 = (bf16[2,197,384]{2,1,0:T(8,128)(2,1)S(1)}, bf16[2,197,384]{2,1,0:T(8,128)(2,1)S(1)}, u32[]{:S(2)}, u32[]{:S(2)}) collective-permute-start(bf16[2,197,384]{2,1,0:T(8,128)(2,1)S(1)} %collective-permute-done.4), channel_id=1, source_target_pairs={{0,14},{1,3},{2,0},{3,5},{4,2},{5,7},{6,4},{7,9},{8,6},{9,11},{10,... | collective-permute-start | bytes 907784 | tf_op jit(solution)/shard_map/ppermute | solution.py:149
  42.8 0.1 constant_dynamic-update-slice_fusion.7
  42.9 0.1 constant_dynamic-update-slice_fusion.6
  42.9 0.0 copy-done.1
  43.0 0.0 copy-done.2
  43.0 1.9 %collective-permute-start.9 = (bf16[10,197,384]{2,1,0:T(8,128)(2,1)S(1)}, bf16[10,197,384]{2,1,0:T(8,128)(2,1)}, u32[]{:S(2)}, u32[]{:S(2)}) collective-permute-start(bf16[10,197,384]{2,1,0:T(8,128)(2,1)S(1)} %constant_dynamic-update-slice_fusion.4.own_ref), channel_id=1, source_target_pairs={{0,1},{1,0},{2,3},{3,2},{4,5},{5,4},{6,7},{7,6},{8,9},{9,8},{10,11... | collective-permute-start | bytes 4538888 | tf_op jit(solution)/shard_map/ppermute | solution.py:144
  45.0 2.5 %collective-permute-done.2 = bf16[2,197,384]{2,1,0:T(8,128)(2,1)S(1)} collective-permute-done((bf16[2,197,384]{2,1,0:T(8,128)(2,1)S(1)}, bf16[2,197,384]{2,1,0:T(8,128)(2,1)S(1)}, u32[]{:S(2)}, u32[]{:S(2)}) %collective-permute-start.2) | collective-permute-done | bytes 302624 | tf_op jit(solution)/shard_map/ppermute | solution.py:148
  47.5 5.6 %collective-permute-start.6 = (bf16[1,197,384]{2,1,0:T(8,128)(2,1)S(1)}, bf16[1,197,384]{2,1,0:T(8,128)(2,1)S(1)}, u32[]{:S(2)}, u32[]{:S(2)}) collective-permute-start(bf16[1,197,384]{2,1,0:T(8,128)(2,1)S(1)} %slice.24), channel_id=1, source_target_pairs={{0,2},{1,15},{2,4},{3,1},{4,6},{5,3},{6,8},{7,5},{8,10},{9,7},{10,... | collective-permute-start | bytes 453896 | tf_op jit(solution)/shard_map/ppermute | solution.py:150
  53.1 0.0 collective-permute-done.5
  53.1 1.9 %collective-permute-start.7 = (bf16[1,197,384]{2,1,0:T(8,128)(2,1)S(1)}, bf16[1,197,384]{2,1,0:T(8,128)(2,1)S(1)}, u32[]{:S(2)}, u32[]{:S(2)}) collective-permute-start(bf16[1,197,384]{2,1,0:T(8,128)(2,1)S(1)} %slice.25), channel_id=1, source_target_pairs={{0,14},{1,3},{2,0},{3,5},{4,2},{5,7},{6,4},{7,9},{8,6},{9,11},{10,... | collective-permute-start | bytes 453896 | tf_op jit(solution)/shard_map/ppermute | solution.py:150
  55.1 0.1 constant_dynamic-update-slice_fusion.2
  55.2 0.8 collective-permute-done.6
  56.0 5.5 %collective-permute-done.7 = bf16[1,197,384]{2,1,0:T(8,128)(2,1)S(1)} collective-permute-done((bf16[1,197,384]{2,1,0:T(8,128)(2,1)S(1)}, bf16[1,197,384]{2,1,0:T(8,128)(2,1)S(1)}, u32[]{:S(2)}, u32[]{:S(2)}) %collective-permute-start.7) | collective-permute-done | bytes 151328 | tf_op jit(solution)/shard_map/ppermute | solution.py:150
  61.5 1.9 %collective-permute-start.8 = (bf16[6,197,384]{2,1,0:T(8,128)(2,1)S(1)}, bf16[6,197,384]{2,1,0:T(8,128)(2,1)S(1)}, u32[]{:S(2)}, u32[]{:S(2)}) collective-permute-start(bf16[6,197,384]{2,1,0:T(8,128)(2,1)S(1)} %constant_dynamic-update-slice_fusion.own_ref), channel_id=1, source_target_pairs={{0,1},{1,0},{2,3},{3,2},{4,5},{5,4},{6,7},{7,6},{8,9},{9,8},{10,11... | collective-permute-start | bytes 2723336 | tf_op jit(solution)/shard_map/ppermute | solution.py:144
  63.4 0.0 all-to-all-done.arrived_ref
  63.4 2.2 %shard_map.93.turned_ref = bf16[384,768]{1,0:T(8,128)(2,1)} custom-call(bf16[32,96,96]{2,1,0:T(8,128)(2,1)} %all-to-all-done.arrived_ref), custom_call_target="tpu_custom_call" | custom-call | flops 17179869184 | bytes 1179648 | tf_op jit(solution)/shard_map/pallas_call | solution.py:178
  65.6 0.0 collective-permute-done.9.far_ref
  65.6 0.0 copy-start
  65.6 1.1 copy-done
  66.7 5.2 %shard_map.94 = (f32[192,768]{1,0:T(8,128)S(1)}, f32[192,768]{1,0:T(8,128)S(1)}, f32[192,768]{1,0:T(8,128)S(1)}, f32[192,768]{1,0:T(8,128)S(1)}) custom-call(s32[1]{0:T(128)} %bitcast.core_ref, bf16[10,197,384]{2,1,0:T(8,128)(2,1)S(1)} %constant_dynamic-update-slice_fusion.4.own_ref, bf16[10,197,384]{2,1,0:T(8,128)(2,1)} %collective-permute-done.9.far_ref, ...), custom_call_target="tpu_custom_call" | custom-call | flops 1161953280 | bytes 3025920 | tf_op jit(solution)/shard_map/pallas_call | solution.py:110
  71.9 0.0 collective-permute-done.8.far_ref
  71.9 2.7 %shard_map.95 = bf16[2,2,8,48,384]{4,3,2,1,0:T(8,128)(2,1)S(1)} custom-call(s32[1]{0:T(128)} %bitcast.core_ref, bf16[6,197,384]{2,1,0:T(8,128)(2,1)S(1)} %constant_dynamic-update-slice_fusion.own_ref, bf16[6,197,384]{2,1,0:T(8,128)(2,1)S(1)} %collective-permute-done.8.far_ref, bf16[384,768]{1,0:T(8,128)(2,1)S(1)} %copy-done, ...), custom_call_target="tpu_custom_call" | custom-call | flops 697171968 | bytes 1815552 | tf_op jit(solution)/shard_map/pallas_call | solution.py:110
  74.6 20.9 %all_to_all.15 = bf16[4,8,48,384]{3,2,1,0:T(8,128)(2,1)S(1)} all-to-all(bf16[4,8,48,384]{3,2,1,0:T(8,128)(2,1)S(1)} %bitcast.12), channel_id=1, replica_groups=mesh['z'=8,'xlo'=2,'xhi'=2,'y'=8,'core'=2] {'xlo','xhi'}, dimensions={0} | all-to-all | bytes 2359296 | tf_op jit(solution)/shard_map/all_to_all | solution.py:190
  95.5 0.1 fusion
  95.7 18.7 %all_to_all.16.pieces_ref = bf16[8,48,384]{2,1,0:T(8,128)(2,1)} all-to-all(bf16[8,48,384]{2,1,0:T(8,128)(2,1)S(1)} %fusion), channel_id=1, replica_groups=mesh['z'=8,'xlo'=2,'xhi'=2,'y'=8,'core'=2] {'z'}, dimensions={0} | all-to-all | bytes 589824 | tf_op jit(solution)/shard_map/all_to_all | solution.py:192
  114.4 1.8 %shard_map.96 = (f32[48,96]{1,0:T(8,128)}, f32[48,96]{1,0:T(8,128)}, f32[48,96]{1,0:T(8,128)}, f32[48,96]{1,0:T(8,128)}) custom-call(bf16[8,48,384]{2,1,0:T(8,128)(2,1)} %all_to_all.16.pieces_ref, bf16[48,96]{1,0:T(8,128)(2,1)} %w_in_ref.1, bf16[48,96]{1,0:T(8,128)(2,1)} %bitcast.16, f32[48,96]{1,0:T(8,128)} %prec_in_ref.1, f32[48,96]{1,0:T(8,128)} %bitcast.17), custom_call_target="tpu_custom_call" | custom-call | tf_op jit(solution)/shard_map/pallas_call | solution.py:194
  (8 shorter events, 0.2 us)
Async XLA Ops:
  1.7 11.4 %collective-permute-start = (bf16[2,197,384]{2,1,0:T(8,128)(2,1)S(1)}, bf16[2,197,384]{2,1,0:T(8,128)(2,1)S(1)}, u32[]{:S(2)}, u32[]{:S(2)}) collective-permute-start(bf16[2,197,384]{2,1,0:T(8,128)(2,1)S(1)} %pad_maximum_fusion), channel_id=1, source_target_pairs={{0,2},{1,15},{2,4},{3,1},{4,6},{5,3},{6,8},{7,5},{8,10},{9,7},{10,... | collective-permute-start | bytes 907784 | tf_op jit(solution)/shard_map/ppermute | solution.py:148
  6.4 12.3 %collective-permute-start.3 = (bf16[2,197,384]{2,1,0:T(8,128)(2,1)S(1)}, bf16[2,197,384]{2,1,0:T(8,128)(2,1)S(1)}, u32[]{:S(2)}, u32[]{:S(2)}) collective-permute-start(bf16[2,197,384]{2,1,0:T(8,128)(2,1)S(1)} %pad_maximum_fusion), channel_id=1, source_target_pairs={{0,14},{1,3},{2,0},{3,5},{4,2},{5,7},{6,4},{7,9},{8,6},{9,11},{10,... | collective-permute-start | bytes 907784 | tf_op jit(solution)/shard_map/ppermute | solution.py:149
  13.1 22.7 %collective-permute-start.1 = (bf16[2,197,384]{2,1,0:T(8,128)(2,1)S(1)}, bf16[2,197,384]{2,1,0:T(8,128)(2,1)S(1)}, u32[]{:S(2)}, u32[]{:S(2)}) collective-permute-start(bf16[2,197,384]{2,1,0:T(8,128)(2,1)S(1)} %collective-permute-done), channel_id=1, source_target_pairs={{0,2},{1,15},{2,4},{3,1},{4,6},{5,3},{6,8},{7,5},{8,10},{9,7},{10,... | collective-permute-start | bytes 907784 | tf_op jit(solution)/shard_map/ppermute | solution.py:148
  18.7 22.2 %collective-permute-start.4 = (bf16[2,197,384]{2,1,0:T(8,128)(2,1)S(1)}, bf16[2,197,384]{2,1,0:T(8,128)(2,1)S(1)}, u32[]{:S(2)}, u32[]{:S(2)}) collective-permute-start(bf16[2,197,384]{2,1,0:T(8,128)(2,1)S(1)} %collective-permute-done.3), channel_id=1, source_target_pairs={{0,14},{1,3},{2,0},{3,5},{4,2},{5,7},{6,4},{7,9},{8,6},{9,11},{10,... | collective-permute-start | bytes 907784 | tf_op jit(solution)/shard_map/ppermute | solution.py:149
  22.3 41.1 %all-to-all-start = ((bf16[32,96,96]{2,1,0:T(8,128)(2,1)}), bf16[32,96,96]{2,1,0:T(8,128)(2,1)}, u32[]{:S(2)}, u32[]{:S(2)}) async-start(bf16[32,96,96]{2,1,0:T(8,128)(2,1)} %broadcast_in_dim.2), calls=%async_computation | async-start | bytes 1572864 | tf_op jit(solution)/shard_map/all_to_all | solution.py:177
  35.6 7.3 %copy-start.1 = (bf16[197,384]{1,0:T(8,128)(2,1)S(1)}, bf16[197,384]{1,0:T(8,128)(2,1)}, u32[]{:S(2)}) copy-start(bf16[197,384]{1,0:T(8,128)(2,1)} %param.6) | copy-start | bytes 453892
  35.6 7.4 %copy-start.2 = (bf16[197,384]{1,0:T(8,128)(2,1)S(1)}, bf16[197,384]{1,0:T(8,128)(2,1)}, u32[]{:S(2)}) copy-start(bf16[197,384]{1,0:T(8,128)(2,1)} %param.7) | copy-start | bytes 453892
  35.7 11.7 %collective-permute-start.2 = (bf16[2,197,384]{2,1,0:T(8,128)(2,1)S(1)}, bf16[2,197,384]{2,1,0:T(8,128)(2,1)S(1)}, u32[]{:S(2)}, u32[]{:S(2)}) collective-permute-start(bf16[2,197,384]{2,1,0:T(8,128)(2,1)S(1)} %collective-permute-done.1), channel_id=1, source_target_pairs={{0,2},{1,15},{2,4},{3,1},{4,6},{5,3},{6,8},{7,5},{8,10},{9,7},{10,... | collective-permute-start | bytes 907784 | tf_op jit(solution)/shard_map/ppermute | solution.py:148
  40.9 12.2 %collective-permute-start.5 = (bf16[2,197,384]{2,1,0:T(8,128)(2,1)S(1)}, bf16[2,197,384]{2,1,0:T(8,128)(2,1)S(1)}, u32[]{:S(2)}, u32[]{:S(2)}) collective-permute-start(bf16[2,197,384]{2,1,0:T(8,128)(2,1)S(1)} %collective-permute-done.4), channel_id=1, source_target_pairs={{0,14},{1,3},{2,0},{3,5},{4,2},{5,7},{6,4},{7,9},{8,6},{9,11},{10,... | collective-permute-start | bytes 907784 | tf_op jit(solution)/shard_map/ppermute | solution.py:149
  43.0 22.6 %collective-permute-start.9 = (bf16[10,197,384]{2,1,0:T(8,128)(2,1)S(1)}, bf16[10,197,384]{2,1,0:T(8,128)(2,1)}, u32[]{:S(2)}, u32[]{:S(2)}) collective-permute-start(bf16[10,197,384]{2,1,0:T(8,128)(2,1)S(1)} %constant_dynamic-update-slice_fusion.4.own_ref), channel_id=1, source_target_pairs={{0,1},{1,0},{2,3},{3,2},{4,5},{5,4},{6,7},{7,6},{8,9},{9,8},{10,11... | collective-permute-start | bytes 4538888 | tf_op jit(solution)/shard_map/ppermute | solution.py:144
  47.5 8.5 %collective-permute-start.6 = (bf16[1,197,384]{2,1,0:T(8,128)(2,1)S(1)}, bf16[1,197,384]{2,1,0:T(8,128)(2,1)S(1)}, u32[]{:S(2)}, u32[]{:S(2)}) collective-permute-start(bf16[1,197,384]{2,1,0:T(8,128)(2,1)S(1)} %slice.24), channel_id=1, source_target_pairs={{0,2},{1,15},{2,4},{3,1},{4,6},{5,3},{6,8},{7,5},{8,10},{9,7},{10,... | collective-permute-start | bytes 453896 | tf_op jit(solution)/shard_map/ppermute | solution.py:150
  53.1 8.3 %collective-permute-start.7 = (bf16[1,197,384]{2,1,0:T(8,128)(2,1)S(1)}, bf16[1,197,384]{2,1,0:T(8,128)(2,1)S(1)}, u32[]{:S(2)}, u32[]{:S(2)}) collective-permute-start(bf16[1,197,384]{2,1,0:T(8,128)(2,1)S(1)} %slice.25), channel_id=1, source_target_pairs={{0,14},{1,3},{2,0},{3,5},{4,2},{5,7},{6,4},{7,9},{8,6},{9,11},{10,... | collective-permute-start | bytes 453896 | tf_op jit(solution)/shard_map/ppermute | solution.py:150
  61.5 10.4 %collective-permute-start.8 = (bf16[6,197,384]{2,1,0:T(8,128)(2,1)S(1)}, bf16[6,197,384]{2,1,0:T(8,128)(2,1)S(1)}, u32[]{:S(2)}, u32[]{:S(2)}) collective-permute-start(bf16[6,197,384]{2,1,0:T(8,128)(2,1)S(1)} %constant_dynamic-update-slice_fusion.own_ref), channel_id=1, source_target_pairs={{0,1},{1,0},{2,3},{3,2},{4,5},{5,4},{6,7},{7,6},{8,9},{9,8},{10,11... | collective-permute-start | bytes 2723336 | tf_op jit(solution)/shard_map/ppermute | solution.py:144
  65.6 1.1 copy-start

commit v9 on v8

--- a/solution.py
+++ b/solution.py
@@ -29,31 +29,33 @@
     return v * half, slope
 
 
-def image_grads(core_ref, own_ref, far_ref, turned_ref):
+def summed(core_ref, own_ref, far_ref, turned_ref):
+    first = core_ref[0] == 0
+    hid = turned_ref.shape[0] // 2
+    last = own_ref.shape[0] // 2 - 1
+
     def dot(a, b, dims):
         return lax.dot_general(a, b, (dims, ((), ())), preferred_element_type=F32)
 
-    first = core_ref[0] == 0
-    hid = turned_ref.shape[0] // 2
-
-    def whole(k):
-        own, far = own_ref[k], far_ref[k]
+    def whole(n, k):
+        own = own_ref[2 * n + k]
+        far = far_ref[2 * (n ^ 1 if n < last else n) + k]
         return jnp.concatenate(
             [jnp.where(first, own, far), jnp.where(first, far, own)], axis=1
         )
 
-    x, c = whole(0), whole(1)
-    pre = dot(turned_ref[:hid], x, ((1,), (1,)))
-    back = dot(turned_ref[hid:], c, ((1,), (1,)))
-    act, slope = gelu_parts(pre)
-    act = act.astype(BF16)
-    delta = (back * slope).astype(BF16)
-    return dot(delta, x, ((1,), (0,))), dot(act, c, ((1,), (0,)))
-
-
-def add_image(sums, g_in, g_out):
-    for ref, term in zip(sums, (g_in, g_in * g_in, g_out, g_out * g_out)):
-        ref[...] += term
+    sums = None
+    for n in range(last + 1):
+        x, c = whole(n, 0), whole(n, 1)
+        pre = dot(turned_ref[:hid], x, ((1,), (1,)))
+        back = dot(turned_ref[hid:], c, ((1,), (1,)))
+        act, slope = gelu_parts(pre)
+        act = act.astype(BF16)
+        delta = (back * slope).astype(BF16)
+        g_in, g_out = dot(delta, x, ((1,), (0,))), dot(act, c, ((1,), (0,)))
+        terms = (g_in, g_in * g_in, g_out, g_out * g_out)
+        sums = terms if sums is None else tuple(s + t for s, t in zip(sums, terms))
+    return sums
 
 
 def turn_kernel(arrived_ref, turned_ref, *, pairs, cols, deep):
@@ -69,67 +71,41 @@
 
 
 def first_kernel(core_ref, own_ref, far_ref, turned_ref, *sums):
-    @pl.when(pl.program_id(0) == 0)
-    def _():
-        for ref in sums:
-            ref[...] = jnp.zeros_like(ref)
-
-    add_image(sums, *image_grads(core_ref, own_ref, far_ref, turned_ref))
+    for ref, term in zip(sums, summed(core_ref, own_ref, far_ref, turned_ref)):
+        ref[...] = term
 
 
-def last_kernel(core_ref, own_ref, far_ref, turned_ref, s0, s1, s2, s3, out_ref, *sums):
-    step = pl.program_id(0)
-
-    @pl.when(step == 0)
-    def _():
-        for ref, start in zip(sums, (s0, s1, s2, s3)):
-            ref[...] = start[...]
-
-    add_image(sums, *image_grads(core_ref, own_ref, far_ref, turned_ref))
-
-    @pl.when(step == pl.num_programs(0) - 1)
-    def _():
-        pairs, cols, deep, rows, packed = out_ref.shape
-        width = packed // 4
-        for h in range(cols):
-            part = slice(h * width, (h + 1) * width)
-            turned = jnp.concatenate([r[part, :] for r in sums], axis=0).T.astype(BF16)
-            for k in range(deep * pairs):
-                out_ref[k % pairs, h, k // pairs] = turned[k * rows : (k + 1) * rows]
+def last_kernel(core_ref, own_ref, far_ref, turned_ref, s0, s1, s2, s3, out_ref):
+    sums = summed(core_ref, own_ref, far_ref, turned_ref)
+    sums = [ref[...] + term for ref, term in zip((s0, s1, s2, s3), sums)]
+    pairs, cols, deep, rows, packed = out_ref.shape
+    width = packed // 4
+    for h in range(cols):
+        part = slice(h * width, (h + 1) * width)
+        turned = jnp.concatenate([s[part, :] for s in sums], axis=0).T.astype(BF16)
+        for k in range(deep * pairs):
+            out_ref[k % pairs, h, k // pairs] = turned[k * rows : (k + 1) * rows]
 
 
-def run_images(kernel, core, own, far, weights, sums, outs):
+def run_images(kernel, core, own, far, turned, sums, outs):
     pieces, seq, part = own.shape
-    last = pieces // 2 - 1
-    hid, d = outs[0].shape if sums == () else sums[0].shape
-    block = (2, seq, part)
-
-    def whole(a):
-        return pl.BlockSpec(a.shape, lambda i: (0,) * len(a.shape))
-
+    rows, d = turned.shape
+    vmem = pl.BlockSpec(memory_space=pltpu.VMEM)
     return pl.pallas_call(
         kernel,
-        grid=(last + 1,),
-        in_specs=[
-            pl.BlockSpec(memory_space=pltpu.SMEM),
-            pl.BlockSpec(block, lambda i: (i, 0, 0)),
-            pl.BlockSpec(block, lambda i: (jnp.where(i < last, i ^ 1, i), 0, 0)),
-            whole(weights),
-        ]
-        + [whole(a) for a in sums],
-        out_specs=[whole(a) for a in outs],
+        in_specs=[pl.BlockSpec(memory_space=pltpu.SMEM)] + [vmem] * (3 + len(sums)),
+        out_specs=[vmem] * len(outs),
         out_shape=outs,
-        scratch_shapes=[pltpu.VMEM(a.shape, a.dtype) for a in sums],
-        compiler_params=pltpu.CompilerParams(vmem_limit_bytes=40 << 20),
+        compiler_params=pltpu.CompilerParams(vmem_limit_bytes=24 << 20),
         cost_estimate=pl.CostEstimate(
-            flops=pieces * 4 * seq * hid * d,
+            flops=pieces * 2 * seq * rows * d,
             bytes_accessed=pieces * 4 * seq * part,
-            transcendentals=pieces * seq * hid // 2,
+            transcendentals=pieces * seq * rows // 4,
         ),
-    )(core, own, far, weights, *sums)
+    )(core, own, far, turned, *sums)
 
 
-def round_the_ring(own):
+def round_the_ring(own, turned_weights):
     n, cores = lax.axis_size("y"), lax.axis_size("core")
 
     def turned(step):
@@ -148,9 +124,10 @@
         up.append(lax.ppermute(up[-1], GROUP, turned(1)))
         down.append(lax.ppermute(down[-1], GROUP, turned(-1)))
     opposite = [lax.ppermute(up[3][:1], GROUP, turned(1)), lax.ppermute(down[3][1:], GROUP, turned(-1))]
+    *opposite, turned_weights = lax.optimization_barrier((*opposite, turned_weights))
     early = jnp.concatenate([up[1], down[1], up[2], down[2], own])
     late = jnp.concatenate([up[3], down[3], *opposite])
-    return (early, swap(early)), (late, swap(late))
+    return (early, swap(early)), (late, swap(late)), turned_weights
 
 
 def update_kernel(pieces_ref, w_in_ref, w_out_ref, prec_in_ref, prec_out_ref, *outs, scale):
@@ -178,9 +155,10 @@
     turned = pl.pallas_call(
         functools.partial(turn_kernel, pairs=pairs, cols=cols, deep=deep),
         out_shape=jax.ShapeDtypeStruct((2 * hid, dp * d_own), BF16),
+
         cost_estimate=pl.CostEstimate(flops=TURN_FLOPS, bytes_accessed=4 * arrived.size, transcendentals=0),
     )(arrived)
-    early, late = round_the_ring(jnp.stack([inputs, cotangent]))
+    early, late, turned = round_the_ring(jnp.stack([inputs, cotangent]), turned)
     core = lax.axis_index("core").reshape(1).astype(jnp.int32)
     partial = [jax.ShapeDtypeStruct((hid, dp * d_own), F32)] * 4
     packed = jax.ShapeDtypeStruct((pairs, cols, deep, d_own, 4 * h_own), BF16)
@@ -194,6 +172,7 @@
     new_prec_in, new_prec_out, new_w_in, new_w_out = pl.pallas_call(
         functools.partial(update_kernel, scale=1.0 / images),
         out_shape=[jax.ShapeDtypeStruct((d_own, h_own), F32)] * 4,
+        compiler_params=pltpu.CompilerParams(vmem_limit_bytes=4 << 20),
     )(pieces, w_in, w_out.T, prec_in, prec_out.T)
     return (new_prec_in, new_prec_out.T, new_w_in, new_w_out.T)
 

time: 117 us -> 116 us (level)
  local copies, waits for them, and re-layouts: 2.47 us -> 6.59 us
  waiting for transfers between devices: 13.6 us -> 10.7 us
  Pallas kernels: 11.9 us -> 10 us
    ppermute x1, waiting for transfers between devices: 5.45 us -> 3.5 us  [round_the_ring(): lax.ppermute(down[3][1:], GROUP, turned(-1))]
    unnamed x14 -> x24, local copies, waits for them, and re-layouts: 1.4 us -> 3.29 us
  transfers between devices with their start and end apart: 11 -> 11, of which waited for: 4 -> 3; matrix products, arithmetic and copies ran while one was open for 2% -> 5% of each run, Pallas kernels for 6% -> 6%
where the time goes in v9:
time: 116 us
  starting transfers between devices  45.8 us (39%)
  blocking collectives  39.5 us (34%)
  waiting for transfers between devices  10.7 us (9%)
  Pallas kernels  10 us (9%)
  local copies, waits for them, and re-layouts  6.59 us (6%)
  other arithmetic  1.91 us (2%)
    all_to_all x1, blocking collectives, per_device(): pieces = lax.all_to_all(pieces, ROW, 0, 0, tiled=True)  21 us
    all_to_all x1, blocking collectives, per_device(): pieces = lax.all_to_all(pieces, 'z', 0, 0, tiled=True)  18.6 us
    ppermute x3, starting transfers between devices, round_the_ring(): up.append(lax.ppermute(up[-1], GROUP, turned(1)))  15.5 us
    all_to_all x1, starting transfers between devices, per_device(): arrived = lax.all_to_all(both, OWNERS, 0, 0, tiled=True)  13.2 us
    ppermute x3, waiting for transfers between devices, round_the_ring(): up.append(lax.ppermute(up[-1], GROUP, turned(1)))  7.19 us
    pallas_call x2, Pallas kernels, run_images(): pl.pallas_call(kernel, in_specs=[pl.BlockSpec(memory_space=pltpu.SMEM)] +...  6.97 us
    ppermute x3, starting transfers between devices, round_the_ring(): down.append(lax.ppermute(down[-1], GROUP, turned(-1)))  5.76 us
    ppermute x1, starting transfers between devices, round_the_ring(): lax.ppermute(up[3][:1], GROUP, turned(1))  5.59 us
  transfers between devices with their start and end apart: 11, of which 3 were waited for; matrix products, arithmetic and copies ran while one was open for 5% of the time, Pallas kernels for 6%

profile of v9, /device:TPU:24, one launch (start us, length us, event | category | flops | bytes accessed | tf_op | source)
XLA Modules:
  0.0 115.5 jit_solution(2993467523861915076)
XLA Ops:
  0.6 1.0 pad_maximum_fusion
  1.7 4.7 %collective-permute-start = (bf16[2,197,384]{2,1,0:T(8,128)(2,1)S(1)}, bf16[2,197,384]{2,1,0:T(8,128)(2,1)}, u32[]{:S(2)}, u32[]{:S(2)}) collective-permute-start(bf16[2,197,384]{2,1,0:T(8,128)(2,1)S(1)} %pad_maximum_fusion), channel_id=1, source_target_pairs={{0,2},{1,15},{2,4},{3,1},{4,6},{5,3},{6,8},{7,5},{8,10},{9,7},{10,... | collective-permute-start | bytes 907784 | tf_op jit(solution)/shard_map/ppermute | solution.py:124
  6.4 1.9 %collective-permute-start.3 = (bf16[2,197,384]{2,1,0:T(8,128)(2,1)S(1)}, bf16[2,197,384]{2,1,0:T(8,128)(2,1)S(1)}, u32[]{:S(2)}, u32[]{:S(2)}) collective-permute-start(bf16[2,197,384]{2,1,0:T(8,128)(2,1)S(1)} %pad_maximum_fusion), channel_id=1, source_target_pairs={{0,14},{1,3},{2,0},{3,5},{4,2},{5,7},{6,4},{7,9},{8,6},{9,11},{10,... | collective-permute-start | bytes 907784 | tf_op jit(solution)/shard_map/ppermute | solution.py:125
  8.3 4.8 %collective-permute-done = bf16[2,197,384]{2,1,0:T(8,128)(2,1)} collective-permute-done((bf16[2,197,384]{2,1,0:T(8,128)(2,1)S(1)}, bf16[2,197,384]{2,1,0:T(8,128)(2,1)}, u32[]{:S(2)}, u32[]{:S(2)}) %collective-permute-start) | collective-permute-done | bytes 302624 | tf_op jit(solution)/shard_map/ppermute | solution.py:124
  13.1 5.7 %collective-permute-start.1 = (bf16[2,197,384]{2,1,0:T(8,128)(2,1)}, bf16[2,197,384]{2,1,0:T(8,128)(2,1)S(1)}, u32[]{:S(2)}, u32[]{:S(2)}) collective-permute-start(bf16[2,197,384]{2,1,0:T(8,128)(2,1)} %collective-permute-done), channel_id=1, source_target_pairs={{0,2},{1,15},{2,4},{3,1},{4,6},{5,3},{6,8},{7,5},{8,10},{9,7},{10,... | collective-permute-start | bytes 907784 | tf_op jit(solution)/shard_map/ppermute | solution.py:124
  18.8 0.0 collective-permute-done.3
  18.8 1.9 %collective-permute-start.4 = (bf16[2,197,384]{2,1,0:T(8,128)(2,1)S(1)}, bf16[2,197,384]{2,1,0:T(8,128)(2,1)S(1)}, u32[]{:S(2)}, u32[]{:S(2)}) collective-permute-start(bf16[2,197,384]{2,1,0:T(8,128)(2,1)S(1)} %collective-permute-done.3), channel_id=1, source_target_pairs={{0,14},{1,3},{2,0},{3,5},{4,2},{5,7},{6,4},{7,9},{8,6},{9,11},{10,... | collective-permute-start | bytes 907784 | tf_op jit(solution)/shard_map/ppermute | solution.py:125
  20.7 0.7 pad_maximum_fusion.1
  21.4 1.0 broadcast_in_dim.2
  22.4 13.2 %all-to-all-start = ((bf16[32,96,96]{2,1,0:T(8,128)(2,1)}), bf16[32,96,96]{2,1,0:T(8,128)(2,1)S(1)}, u32[]{:S(2)}, u32[]{:S(2)}) async-start(bf16[32,96,96]{2,1,0:T(8,128)(2,1)} %broadcast_in_dim.2), calls=%async_computation | async-start | bytes 1572864 | tf_op jit(solution)/shard_map/all_to_all | solution.py:154
  35.6 0.0 copy-start.6
  35.6 0.0 copy-start.7
  35.6 1.0 constant_dynamic-update-slice_fusion.9
  36.7 0.1 constant_dynamic-update-slice_fusion.8
  36.7 0.0 collective-permute-done.1
  36.7 5.1 %collective-permute-start.2 = (bf16[2,197,384]{2,1,0:T(8,128)(2,1)S(1)}, bf16[2,197,384]{2,1,0:T(8,128)(2,1)S(1)}, u32[]{:S(2)}, u32[]{:S(2)}) collective-permute-start(bf16[2,197,384]{2,1,0:T(8,128)(2,1)S(1)} %collective-permute-done.1), channel_id=1, source_target_pairs={{0,2},{1,15},{2,4},{3,1},{4,6},{5,3},{6,8},{7,5},{8,10},{9,7},{10,... | collective-permute-start | bytes 907784 | tf_op jit(solution)/shard_map/ppermute | solution.py:124
  41.9 0.0 collective-permute-done.4
  41.9 1.9 %collective-permute-start.5 = (bf16[2,197,384]{2,1,0:T(8,128)(2,1)S(1)}, bf16[2,197,384]{2,1,0:T(8,128)(2,1)S(1)}, u32[]{:S(2)}, u32[]{:S(2)}) collective-permute-start(bf16[2,197,384]{2,1,0:T(8,128)(2,1)S(1)} %collective-permute-done.4), channel_id=1, source_target_pairs={{0,14},{1,3},{2,0},{3,5},{4,2},{5,7},{6,4},{7,9},{8,6},{9,11},{10,... | collective-permute-start | bytes 907784 | tf_op jit(solution)/shard_map/ppermute | solution.py:125
  43.8 0.1 constant_dynamic-update-slice_fusion.7
  43.9 0.1 constant_dynamic-update-slice_fusion.6
  43.9 0.0 copy-done.6
  44.0 0.0 copy-done.7
  44.0 1.9 %collective-permute-start.9 = (bf16[10,197,384]{2,1,0:T(8,128)(2,1)S(1)}, bf16[10,197,384]{2,1,0:T(8,128)(2,1)}, u32[]{:S(2)}, u32[]{:S(2)}) collective-permute-start(bf16[10,197,384]{2,1,0:T(8,128)(2,1)S(1)} %constant_dynamic-update-slice_fusion.4.own_ref), channel_id=1, source_target_pairs={{0,1},{1,0},{2,3},{3,2},{4,5},{5,4},{6,7},{7,6},{8,9},{9,8},{10,11... | collective-permute-start | bytes 4538888 | tf_op jit(solution)/shard_map/ppermute | solution.py:120
  45.9 2.4 %collective-permute-done.2 = bf16[2,197,384]{2,1,0:T(8,128)(2,1)S(1)} collective-permute-done((bf16[2,197,384]{2,1,0:T(8,128)(2,1)S(1)}, bf16[2,197,384]{2,1,0:T(8,128)(2,1)S(1)}, u32[]{:S(2)}, u32[]{:S(2)}) %collective-permute-start.2) | collective-permute-done | bytes 302624 | tf_op jit(solution)/shard_map/ppermute | solution.py:124
  48.4 0.7 slice.24
  49.0 5.6 %collective-permute-start.6 = (bf16[1,197,384]{2,1,0:T(8,128)(2,1)}, bf16[1,197,384]{2,1,0:T(8,128)(2,1)S(1)}, u32[]{:S(2)}, u32[]{:S(2)}) collective-permute-start(bf16[1,197,384]{2,1,0:T(8,128)(2,1)} %slice.24), channel_id=1, source_target_pairs={{0,2},{1,15},{2,4},{3,1},{4,6},{5,3},{6,8},{7,5},{8,10},{9,7},{10,... | collective-permute-start | bytes 453896 | tf_op jit(solution)/shard_map/ppermute | solution.py:126
  54.6 0.0 collective-permute-done.5
  54.6 0.7 slice.25
  55.3 1.9 %collective-permute-start.7 = (bf16[1,197,384]{2,1,0:T(8,128)(2,1)}, bf16[1,197,384]{2,1,0:T(8,128)(2,1)}, u32[]{:S(2)}, u32[]{:S(2)}) collective-permute-start(bf16[1,197,384]{2,1,0:T(8,128)(2,1)} %slice.25), channel_id=1, source_target_pairs={{0,14},{1,3},{2,0},{3,5},{4,2},{5,7},{6,4},{7,9},{8,6},{9,11},{10,... | collective-permute-start | bytes 453896 | tf_op jit(solution)/shard_map/ppermute | solution.py:126
  57.3 0.1 constant_dynamic-update-slice_fusion.2
  57.3 0.0 all-to-all-done.arrived_ref
  57.4 0.0 copy-start.5
  57.4 0.9 copy-done.5
  58.2 2.2 %shard_map.93.turned_ref = bf16[384,768]{1,0:T(8,128)(2,1)} custom-call(bf16[32,96,96]{2,1,0:T(8,128)(2,1)} %copy-done.5), custom_call_target="tpu_custom_call" | custom-call | flops 17179869184 | bytes 1179648 | tf_op jit(solution)/shard_map/pallas_call | solution.py:155
  60.4 0.0 collective-permute-done.6
  60.4 3.5 %collective-permute-done.7 = bf16[1,197,384]{2,1,0:T(8,128)(2,1)} collective-permute-done((bf16[1,197,384]{2,1,0:T(8,128)(2,1)}, bf16[1,197,384]{2,1,0:T(8,128)(2,1)}, u32[]{:S(2)}, u32[]{:S(2)}) %collective-permute-start.7) | collective-permute-done | bytes 151328 | tf_op jit(solution)/shard_map/ppermute | solution.py:126
  64.0 0.9 constant_dynamic-update-slice_fusion.own_ref
  64.9 1.9 %collective-permute-start.8 = (bf16[6,197,384]{2,1,0:T(8,128)(2,1)S(1)}, bf16[6,197,384]{2,1,0:T(8,128)(2,1)S(1)}, u32[]{:S(2)}, u32[]{:S(2)}) collective-permute-start(bf16[6,197,384]{2,1,0:T(8,128)(2,1)S(1)} %constant_dynamic-update-slice_fusion.own_ref), channel_id=1, source_target_pairs={{0,1},{1,0},{2,3},{3,2},{4,5},{5,4},{6,7},{7,6},{8,9},{9,8},{10,11... | collective-permute-start | bytes 2723336 | tf_op jit(solution)/shard_map/ppermute | solution.py:120
  66.8 0.0 collective-permute-done.9.far_ref
  66.9 1.1 copy-done
  67.9 4.5 %shard_map.94 = (f32[192,768]{1,0:T(8,128)S(1)}, f32[192,768]{1,0:T(8,128)S(1)}, f32[192,768]{1,0:T(8,128)S(1)}, f32[192,768]{1,0:T(8,128)S(1)}) custom-call(s32[1]{0:T(128)} %bitcast.core_ref, bf16[10,197,384]{2,1,0:T(8,128)(2,1)S(1)} %constant_dynamic-update-slice_fusion.4.own_ref, bf16[10,197,384]{2,1,0:T(8,128)(2,1)} %collective-permute-done.9.far_ref, ...), custom_call_target="tpu_custom_call" | custom-call | flops 1161953280 | bytes 3025920 | tf_op jit(solution)/shard_map/pallas_call | solution.py:94
  72.5 0.0 collective-permute-done.8.far_ref
  72.5 2.4 %shard_map.95 = bf16[2,2,8,48,384]{4,3,2,1,0:T(8,128)(2,1)S(1)} custom-call(s32[1]{0:T(128)} %bitcast.core_ref, bf16[6,197,384]{2,1,0:T(8,128)(2,1)S(1)} %constant_dynamic-update-slice_fusion.own_ref, bf16[6,197,384]{2,1,0:T(8,128)(2,1)S(1)} %collective-permute-done.8.far_ref, bf16[384,768]{1,0:T(8,128)(2,1)S(1)} %copy-done, ...), custom_call_target="tpu_custom_call" | custom-call | flops 697171968 | bytes 1815552 | tf_op jit(solution)/shard_map/pallas_call | solution.py:94
  74.9 21.0 %all_to_all.15 = bf16[4,8,48,384]{3,2,1,0:T(8,128)(2,1)S(1)} all-to-all(bf16[4,8,48,384]{3,2,1,0:T(8,128)(2,1)S(1)} %bitcast.12), channel_id=1, replica_groups=mesh['z'=8,'xlo'=2,'xhi'=2,'y'=8,'core'=2] {'xlo','xhi'}, dimensions={0} | all-to-all | bytes 2359296 | tf_op jit(solution)/shard_map/all_to_all | solution.py:168
  95.9 0.2 fusion
  96.1 18.6 %all_to_all.16.pieces_ref = bf16[8,48,384]{2,1,0:T(8,128)(2,1)S(1)} all-to-all(bf16[8,48,384]{2,1,0:T(8,128)(2,1)S(1)} %fusion), channel_id=1, replica_groups=mesh['z'=8,'xlo'=2,'xhi'=2,'y'=8,'core'=2] {'z'}, dimensions={0} | all-to-all | bytes 589824 | tf_op jit(solution)/shard_map/all_to_all | solution.py:170
  114.6 0.0 copy-done.2
  114.7 0.8 shard_map.96
  (12 shorter events, 0.1 us)
Async XLA Ops:
  1.7 11.4 %collective-permute-start = (bf16[2,197,384]{2,1,0:T(8,128)(2,1)S(1)}, bf16[2,197,384]{2,1,0:T(8,128)(2,1)}, u32[]{:S(2)}, u32[]{:S(2)}) collective-permute-start(bf16[2,197,384]{2,1,0:T(8,128)(2,1)S(1)} %pad_maximum_fusion), channel_id=1, source_target_pairs={{0,2},{1,15},{2,4},{3,1},{4,6},{5,3},{6,8},{7,5},{8,10},{9,7},{10,... | collective-permute-start | bytes 907784 | tf_op jit(solution)/shard_map/ppermute | solution.py:124
  6.4 12.4 %collective-permute-start.3 = (bf16[2,197,384]{2,1,0:T(8,128)(2,1)S(1)}, bf16[2,197,384]{2,1,0:T(8,128)(2,1)S(1)}, u32[]{:S(2)}, u32[]{:S(2)}) collective-permute-start(bf16[2,197,384]{2,1,0:T(8,128)(2,1)S(1)} %pad_maximum_fusion), channel_id=1, source_target_pairs={{0,14},{1,3},{2,0},{3,5},{4,2},{5,7},{6,4},{7,9},{8,6},{9,11},{10,... | collective-permute-start | bytes 907784 | tf_op jit(solution)/shard_map/ppermute | solution.py:125
  13.1 23.7 %collective-permute-start.1 = (bf16[2,197,384]{2,1,0:T(8,128)(2,1)}, bf16[2,197,384]{2,1,0:T(8,128)(2,1)S(1)}, u32[]{:S(2)}, u32[]{:S(2)}) collective-permute-start(bf16[2,197,384]{2,1,0:T(8,128)(2,1)} %collective-permute-done), channel_id=1, source_target_pairs={{0,2},{1,15},{2,4},{3,1},{4,6},{5,3},{6,8},{7,5},{8,10},{9,7},{10,... | collective-permute-start | bytes 907784 | tf_op jit(solution)/shard_map/ppermute | solution.py:124
  18.8 23.1 %collective-permute-start.4 = (bf16[2,197,384]{2,1,0:T(8,128)(2,1)S(1)}, bf16[2,197,384]{2,1,0:T(8,128)(2,1)S(1)}, u32[]{:S(2)}, u32[]{:S(2)}) collective-permute-start(bf16[2,197,384]{2,1,0:T(8,128)(2,1)S(1)} %collective-permute-done.3), channel_id=1, source_target_pairs={{0,14},{1,3},{2,0},{3,5},{4,2},{5,7},{6,4},{7,9},{8,6},{9,11},{10,... | collective-permute-start | bytes 907784 | tf_op jit(solution)/shard_map/ppermute | solution.py:125
  22.4 34.9 %all-to-all-start = ((bf16[32,96,96]{2,1,0:T(8,128)(2,1)}), bf16[32,96,96]{2,1,0:T(8,128)(2,1)S(1)}, u32[]{:S(2)}, u32[]{:S(2)}) async-start(bf16[32,96,96]{2,1,0:T(8,128)(2,1)} %broadcast_in_dim.2), calls=%async_computation | async-start | bytes 1572864 | tf_op jit(solution)/shard_map/all_to_all | solution.py:154
  35.6 8.3 %copy-start.6 = (bf16[197,384]{1,0:T(8,128)(2,1)S(1)}, bf16[197,384]{1,0:T(8,128)(2,1)}, u32[]{:S(2)}) copy-start(bf16[197,384]{1,0:T(8,128)(2,1)} %param.6) | copy-start | bytes 453892
  35.6 8.4 %copy-start.7 = (bf16[197,384]{1,0:T(8,128)(2,1)S(1)}, bf16[197,384]{1,0:T(8,128)(2,1)}, u32[]{:S(2)}) copy-start(bf16[197,384]{1,0:T(8,128)(2,1)} %param.7) | copy-start | bytes 453892
  36.7 11.6 %collective-permute-start.2 = (bf16[2,197,384]{2,1,0:T(8,128)(2,1)S(1)}, bf16[2,197,384]{2,1,0:T(8,128)(2,1)S(1)}, u32[]{:S(2)}, u32[]{:S(2)}) collective-permute-start(bf16[2,197,384]{2,1,0:T(8,128)(2,1)S(1)} %collective-permute-done.1), channel_id=1, source_target_pairs={{0,2},{1,15},{2,4},{3,1},{4,6},{5,3},{6,8},{7,5},{8,10},{9,7},{10,... | collective-permute-start | bytes 907784 | tf_op jit(solution)/shard_map/ppermute | solution.py:124
  41.9 12.8 %collective-permute-start.5 = (bf16[2,197,384]{2,1,0:T(8,128)(2,1)S(1)}, bf16[2,197,384]{2,1,0:T(8,128)(2,1)S(1)}, u32[]{:S(2)}, u32[]{:S(2)}) collective-permute-start(bf16[2,197,384]{2,1,0:T(8,128)(2,1)S(1)} %collective-permute-done.4), channel_id=1, source_target_pairs={{0,14},{1,3},{2,0},{3,5},{4,2},{5,7},{6,4},{7,9},{8,6},{9,11},{10,... | collective-permute-start | bytes 907784 | tf_op jit(solution)/shard_map/ppermute | solution.py:125
  44.0 22.8 %collective-permute-start.9 = (bf16[10,197,384]{2,1,0:T(8,128)(2,1)S(1)}, bf16[10,197,384]{2,1,0:T(8,128)(2,1)}, u32[]{:S(2)}, u32[]{:S(2)}) collective-permute-start(bf16[10,197,384]{2,1,0:T(8,128)(2,1)S(1)} %constant_dynamic-update-slice_fusion.4.own_ref), channel_id=1, source_target_pairs={{0,1},{1,0},{2,3},{3,2},{4,5},{5,4},{6,7},{7,6},{8,9},{9,8},{10,11... | collective-permute-start | bytes 4538888 | tf_op jit(solution)/shard_map/ppermute | solution.py:120
  49.0 11.4 %collective-permute-start.6 = (bf16[1,197,384]{2,1,0:T(8,128)(2,1)}, bf16[1,197,384]{2,1,0:T(8,128)(2,1)S(1)}, u32[]{:S(2)}, u32[]{:S(2)}) collective-permute-start(bf16[1,197,384]{2,1,0:T(8,128)(2,1)} %slice.24), channel_id=1, source_target_pairs={{0,2},{1,15},{2,4},{3,1},{4,6},{5,3},{6,8},{7,5},{8,10},{9,7},{10,... | collective-permute-start | bytes 453896 | tf_op jit(solution)/shard_map/ppermute | solution.py:126
  55.3 8.6 %collective-permute-start.7 = (bf16[1,197,384]{2,1,0:T(8,128)(2,1)}, bf16[1,197,384]{2,1,0:T(8,128)(2,1)}, u32[]{:S(2)}, u32[]{:S(2)}) collective-permute-start(bf16[1,197,384]{2,1,0:T(8,128)(2,1)} %slice.25), channel_id=1, source_target_pairs={{0,14},{1,3},{2,0},{3,5},{4,2},{5,7},{6,4},{7,9},{8,6},{9,11},{10,... | collective-permute-start | bytes 453896 | tf_op jit(solution)/shard_map/ppermute | solution.py:126
  57.4 0.9 copy-start.5
  64.9 7.5 %collective-permute-start.8 = (bf16[6,197,384]{2,1,0:T(8,128)(2,1)S(1)}, bf16[6,197,384]{2,1,0:T(8,128)(2,1)S(1)}, u32[]{:S(2)}, u32[]{:S(2)}) collective-permute-start(bf16[6,197,384]{2,1,0:T(8,128)(2,1)S(1)} %constant_dynamic-update-slice_fusion.own_ref), channel_id=1, source_target_pairs={{0,1},{1,0},{2,3},{3,2},{4,5},{5,4},{6,7},{7,6},{8,9},{9,8},{10,11... | collective-permute-start | bytes 2723336 | tf_op jit(solution)/shard_map/ppermute | solution.py:120
  66.9 1.1 copy-start
  95.9 18.8 %copy-start.1 = (bf16[96,48]{0,1:T(8,128)(2,1)S(1)}, bf16[96,48]{0,1:T(8,128)(2,1)}, u32[]{:S(2)}) copy-start(bf16[96,48]{0,1:T(8,128)(2,1)} %param.9) | copy-start | bytes 27652
  95.9 18.8 %copy-start.2 = (bf16[48,96]{1,0:T(8,128)(2,1)S(1)}, bf16[48,96]{1,0:T(8,128)(2,1)}, u32[]{:S(2)}) copy-start(bf16[48,96]{1,0:T(8,128)(2,1)} %w_in_ref.1) | copy-start | bytes 27652
  95.9 18.8 %copy-start.3 = (f32[48,96]{1,0:T(8,128)S(1)}, f32[48,96]{1,0:T(8,128)}, u32[]{:S(2)}) copy-start(f32[48,96]{1,0:T(8,128)} %prec_in_ref.1) | copy-start | bytes 55300
  95.9 18.8 %copy-start.4 = (f32[96,48]{0,1:T(8,128)S(1)}, f32[96,48]{0,1:T(8,128)}, u32[]{:S(2)}) copy-start(f32[96,48]{0,1:T(8,128)} %param.11) | copy-start | bytes 55300

commit v10 on v9

--- a/solution.py
+++ b/solution.py
@@ -124,7 +124,7 @@
         up.append(lax.ppermute(up[-1], GROUP, turned(1)))
         down.append(lax.ppermute(down[-1], GROUP, turned(-1)))
     opposite = [lax.ppermute(up[3][:1], GROUP, turned(1)), lax.ppermute(down[3][1:], GROUP, turned(-1))]
-    *opposite, turned_weights = lax.optimization_barrier((*opposite, turned_weights))
+
     early = jnp.concatenate([up[1], down[1], up[2], down[2], own])
     late = jnp.concatenate([up[3], down[3], *opposite])
     return (early, swap(early)), (late, swap(late)), turned_weights

time: 116 us -> 115 us (level)
  local copies, waits for them, and re-layouts: 6.59 us -> 2.48 us
  waiting for transfers between devices: 10.7 us -> 13.6 us
    ppermute x1, waiting for transfers between devices: 3.5 us -> 5.45 us  [round_the_ring(): lax.ppermute(down[3][1:], GROUP, turned(-1))]
    unnamed x24 -> x22, local copies, waits for them, and re-layouts: 3.29 us -> 1.41 us
  transfers between devices with their start and end apart: 11 -> 11, of which waited for: 3 -> 4; matrix products, arithmetic and copies ran while one was open for 5% -> 2% of each run, Pallas kernels for 6% -> 6%
where the time goes in v10:
time: 115 us; the launch traced here: 114 us
  starting transfers between devices  45.8 us (40%)
  blocking collectives  39.5 us (34%)
  waiting for transfers between devices  13.6 us (12%)
  Pallas kernels  10 us (9%)
  local copies, waits for them, and re-layouts  2.48 us (2%)
  other arithmetic  1.91 us (2%)
    all_to_all x1, blocking collectives, per_device(): pieces = lax.all_to_all(pieces, ROW, 0, 0, tiled=True)  20.9 us
    all_to_all x1, blocking collectives, per_device(): pieces = lax.all_to_all(pieces, 'z', 0, 0, tiled=True)  18.6 us
    ppermute x3, starting transfers between devices, round_the_ring(): up.append(lax.ppermute(up[-1], GROUP, turned(1)))  15.4 us
    all_to_all x1, starting transfers between devices, per_device(): arrived = lax.all_to_all(both, OWNERS, 0, 0, tiled=True)  13.3 us
    ppermute x3, waiting for transfers between devices, round_the_ring(): up.append(lax.ppermute(up[-1], GROUP, turned(1)))  7.3 us
    pallas_call x2, Pallas kernels, run_images(): pl.pallas_call(kernel, in_specs=[pl.BlockSpec(memory_space=pltpu.SMEM)] +...  6.98 us
    ppermute x3, starting transfers between devices, round_the_ring(): down.append(lax.ppermute(down[-1], GROUP, turned(-1)))  5.76 us
    ppermute x1, starting transfers between devices, round_the_ring(): lax.ppermute(up[3][:1], GROUP, turned(1))  5.6 us
  transfers between devices with their start and end apart: 11, of which 4 were waited for; matrix products, arithmetic and copies ran while one was open for 2% of the time, Pallas kernels for 6%

profile of v10, /device:TPU:24, one launch (start us, length us, event | category | flops | bytes accessed | tf_op | source)
XLA Modules:
  0.0 114.2 jit_solution(13939183093649141)
XLA Ops:
  0.6 1.0 pad_maximum_fusion
  1.7 4.7 %collective-permute-start = (bf16[2,197,384]{2,1,0:T(8,128)(2,1)S(1)}, bf16[2,197,384]{2,1,0:T(8,128)(2,1)S(1)}, u32[]{:S(2)}, u32[]{:S(2)}) collective-permute-start(bf16[2,197,384]{2,1,0:T(8,128)(2,1)S(1)} %pad_maximum_fusion), channel_id=1, source_target_pairs={{0,2},{1,15},{2,4},{3,1},{4,6},{5,3},{6,8},{7,5},{8,10},{9,7},{10,... | collective-permute-start | bytes 907784 | tf_op jit(solution)/shard_map/ppermute | solution.py:124
  6.4 1.9 %collective-permute-start.3 = (bf16[2,197,384]{2,1,0:T(8,128)(2,1)S(1)}, bf16[2,197,384]{2,1,0:T(8,128)(2,1)S(1)}, u32[]{:S(2)}, u32[]{:S(2)}) collective-permute-start(bf16[2,197,384]{2,1,0:T(8,128)(2,1)S(1)} %pad_maximum_fusion), channel_id=1, source_target_pairs={{0,14},{1,3},{2,0},{3,5},{4,2},{5,7},{6,4},{7,9},{8,6},{9,11},{10,... | collective-permute-start | bytes 907784 | tf_op jit(solution)/shard_map/ppermute | solution.py:125
  8.3 4.8 %collective-permute-done = bf16[2,197,384]{2,1,0:T(8,128)(2,1)S(1)} collective-permute-done((bf16[2,197,384]{2,1,0:T(8,128)(2,1)S(1)}, bf16[2,197,384]{2,1,0:T(8,128)(2,1)S(1)}, u32[]{:S(2)}, u32[]{:S(2)}) %collective-permute-start) | collective-permute-done | bytes 302624 | tf_op jit(solution)/shard_map/ppermute | solution.py:124
  13.1 5.6 %collective-permute-start.1 = (bf16[2,197,384]{2,1,0:T(8,128)(2,1)S(1)}, bf16[2,197,384]{2,1,0:T(8,128)(2,1)S(1)}, u32[]{:S(2)}, u32[]{:S(2)}) collective-permute-start(bf16[2,197,384]{2,1,0:T(8,128)(2,1)S(1)} %collective-permute-done), channel_id=1, source_target_pairs={{0,2},{1,15},{2,4},{3,1},{4,6},{5,3},{6,8},{7,5},{8,10},{9,7},{10,... | collective-permute-start | bytes 907784 | tf_op jit(solution)/shard_map/ppermute | solution.py:124
  18.7 0.0 collective-permute-done.3
  18.7 1.9 %collective-permute-start.4 = (bf16[2,197,384]{2,1,0:T(8,128)(2,1)S(1)}, bf16[2,197,384]{2,1,0:T(8,128)(2,1)S(1)}, u32[]{:S(2)}, u32[]{:S(2)}) collective-permute-start(bf16[2,197,384]{2,1,0:T(8,128)(2,1)S(1)} %collective-permute-done.3), channel_id=1, source_target_pairs={{0,14},{1,3},{2,0},{3,5},{4,2},{5,7},{6,4},{7,9},{8,6},{9,11},{10,... | collective-permute-start | bytes 907784 | tf_op jit(solution)/shard_map/ppermute | solution.py:125
  20.6 0.7 pad_maximum_fusion.1
  21.3 1.0 broadcast_in_dim.2
  22.3 13.3 %all-to-all-start = ((bf16[32,96,96]{2,1,0:T(8,128)(2,1)}), bf16[32,96,96]{2,1,0:T(8,128)(2,1)}, u32[]{:S(2)}, u32[]{:S(2)}) async-start(bf16[32,96,96]{2,1,0:T(8,128)(2,1)} %broadcast_in_dim.2), calls=%async_computation | async-start | bytes 1572864 | tf_op jit(solution)/shard_map/all_to_all | solution.py:154
  35.6 0.0 copy-start.5
  35.6 0.0 copy-start.6
  35.7 0.1 constant_dynamic-update-slice_fusion.8
  35.7 0.0 collective-permute-done.1
  35.7 5.1 %collective-permute-start.2 = (bf16[2,197,384]{2,1,0:T(8,128)(2,1)S(1)}, bf16[2,197,384]{2,1,0:T(8,128)(2,1)S(1)}, u32[]{:S(2)}, u32[]{:S(2)}) collective-permute-start(bf16[2,197,384]{2,1,0:T(8,128)(2,1)S(1)} %collective-permute-done.1), channel_id=1, source_target_pairs={{0,2},{1,15},{2,4},{3,1},{4,6},{5,3},{6,8},{7,5},{8,10},{9,7},{10,... | collective-permute-start | bytes 907784 | tf_op jit(solution)/shard_map/ppermute | solution.py:124
  40.9 0.0 collective-permute-done.4
  40.9 1.9 %collective-permute-start.5 = (bf16[2,197,384]{2,1,0:T(8,128)(2,1)S(1)}, bf16[2,197,384]{2,1,0:T(8,128)(2,1)S(1)}, u32[]{:S(2)}, u32[]{:S(2)}) collective-permute-start(bf16[2,197,384]{2,1,0:T(8,128)(2,1)S(1)} %collective-permute-done.4), channel_id=1, source_target_pairs={{0,14},{1,3},{2,0},{3,5},{4,2},{5,7},{6,4},{7,9},{8,6},{9,11},{10,... | collective-permute-start | bytes 907784 | tf_op jit(solution)/shard_map/ppermute | solution.py:125
  42.8 0.1 constant_dynamic-update-slice_fusion.7
  42.9 0.1 constant_dynamic-update-slice_fusion.6
  42.9 0.0 copy-done.5
  43.0 0.0 copy-done.6
  43.0 1.9 %collective-permute-start.9 = (bf16[10,197,384]{2,1,0:T(8,128)(2,1)S(1)}, bf16[10,197,384]{2,1,0:T(8,128)(2,1)}, u32[]{:S(2)}, u32[]{:S(2)}) collective-permute-start(bf16[10,197,384]{2,1,0:T(8,128)(2,1)S(1)} %constant_dynamic-update-slice_fusion.4.own_ref), channel_id=1, source_target_pairs={{0,1},{1,0},{2,3},{3,2},{4,5},{5,4},{6,7},{7,6},{8,9},{9,8},{10,11... | collective-permute-start | bytes 4538888 | tf_op jit(solution)/shard_map/ppermute | solution.py:120
  45.0 2.5 %collective-permute-done.2 = bf16[2,197,384]{2,1,0:T(8,128)(2,1)S(1)} collective-permute-done((bf16[2,197,384]{2,1,0:T(8,128)(2,1)S(1)}, bf16[2,197,384]{2,1,0:T(8,128)(2,1)S(1)}, u32[]{:S(2)}, u32[]{:S(2)}) %collective-permute-start.2) | collective-permute-done | bytes 302624 | tf_op jit(solution)/shard_map/ppermute | solution.py:124
  47.5 5.6 %collective-permute-start.6 = (bf16[1,197,384]{2,1,0:T(8,128)(2,1)S(1)}, bf16[1,197,384]{2,1,0:T(8,128)(2,1)S(1)}, u32[]{:S(2)}, u32[]{:S(2)}) collective-permute-start(bf16[1,197,384]{2,1,0:T(8,128)(2,1)S(1)} %slice.24), channel_id=1, source_target_pairs={{0,2},{1,15},{2,4},{3,1},{4,6},{5,3},{6,8},{7,5},{8,10},{9,7},{10,... | collective-permute-start | bytes 453896 | tf_op jit(solution)/shard_map/ppermute | solution.py:126
  53.1 0.0 collective-permute-done.5
  53.1 1.9 %collective-permute-start.7 = (bf16[1,197,384]{2,1,0:T(8,128)(2,1)S(1)}, bf16[1,197,384]{2,1,0:T(8,128)(2,1)S(1)}, u32[]{:S(2)}, u32[]{:S(2)}) collective-permute-start(bf16[1,197,384]{2,1,0:T(8,128)(2,1)S(1)} %slice.25), channel_id=1, source_target_pairs={{0,14},{1,3},{2,0},{3,5},{4,2},{5,7},{6,4},{7,9},{8,6},{9,11},{10,... | collective-permute-start | bytes 453896 | tf_op jit(solution)/shard_map/ppermute | solution.py:126
  55.1 0.1 constant_dynamic-update-slice_fusion.2
  55.2 0.8 collective-permute-done.6
  56.0 5.5 %collective-permute-done.7 = bf16[1,197,384]{2,1,0:T(8,128)(2,1)S(1)} collective-permute-done((bf16[1,197,384]{2,1,0:T(8,128)(2,1)S(1)}, bf16[1,197,384]{2,1,0:T(8,128)(2,1)S(1)}, u32[]{:S(2)}, u32[]{:S(2)}) %collective-permute-start.7) | collective-permute-done | bytes 151328 | tf_op jit(solution)/shard_map/ppermute | solution.py:126
  61.5 1.9 %collective-permute-start.8 = (bf16[6,197,384]{2,1,0:T(8,128)(2,1)S(1)}, bf16[6,197,384]{2,1,0:T(8,128)(2,1)S(1)}, u32[]{:S(2)}, u32[]{:S(2)}) collective-permute-start(bf16[6,197,384]{2,1,0:T(8,128)(2,1)S(1)} %constant_dynamic-update-slice_fusion.own_ref), channel_id=1, source_target_pairs={{0,1},{1,0},{2,3},{3,2},{4,5},{5,4},{6,7},{7,6},{8,9},{9,8},{10,11... | collective-permute-start | bytes 2723336 | tf_op jit(solution)/shard_map/ppermute | solution.py:120
  63.4 0.0 all-to-all-done.arrived_ref
  63.4 2.2 %shard_map.93.turned_ref = bf16[384,768]{1,0:T(8,128)(2,1)} custom-call(bf16[32,96,96]{2,1,0:T(8,128)(2,1)} %all-to-all-done.arrived_ref), custom_call_target="tpu_custom_call" | custom-call | flops 17179869184 | bytes 1179648 | tf_op jit(solution)/shard_map/pallas_call | solution.py:155
  65.6 0.0 collective-permute-done.9.far_ref
  65.6 0.0 copy-start
  65.6 1.1 copy-done
  66.7 4.5 %shard_map.94 = (f32[192,768]{1,0:T(8,128)S(1)}, f32[192,768]{1,0:T(8,128)S(1)}, f32[192,768]{1,0:T(8,128)S(1)}, f32[192,768]{1,0:T(8,128)S(1)}) custom-call(s32[1]{0:T(128)} %bitcast.core_ref, bf16[10,197,384]{2,1,0:T(8,128)(2,1)S(1)} %constant_dynamic-update-slice_fusion.4.own_ref, bf16[10,197,384]{2,1,0:T(8,128)(2,1)} %collective-permute-done.9.far_ref, ...), custom_call_target="tpu_custom_call" | custom-call | flops 1161953280 | bytes 3025920 | tf_op jit(solution)/shard_map/pallas_call | solution.py:94
  71.2 0.0 collective-permute-done.8.far_ref
  71.3 2.4 %shard_map.95 = bf16[2,2,8,48,384]{4,3,2,1,0:T(8,128)(2,1)S(1)} custom-call(s32[1]{0:T(128)} %bitcast.core_ref, bf16[6,197,384]{2,1,0:T(8,128)(2,1)S(1)} %constant_dynamic-update-slice_fusion.own_ref, bf16[6,197,384]{2,1,0:T(8,128)(2,1)S(1)} %collective-permute-done.8.far_ref, bf16[384,768]{1,0:T(8,128)(2,1)S(1)} %copy-done, ...), custom_call_target="tpu_custom_call" | custom-call | flops 697171968 | bytes 1815552 | tf_op jit(solution)/shard_map/pallas_call | solution.py:94
  73.7 20.9 %all_to_all.15 = bf16[4,8,48,384]{3,2,1,0:T(8,128)(2,1)S(1)} all-to-all(bf16[4,8,48,384]{3,2,1,0:T(8,128)(2,1)S(1)} %bitcast.12), channel_id=1, replica_groups=mesh['z'=8,'xlo'=2,'xhi'=2,'y'=8,'core'=2] {'xlo','xhi'}, dimensions={0} | all-to-all | bytes 2359296 | tf_op jit(solution)/shard_map/all_to_all | solution.py:168
  94.6 0.0 copy-start.1
  94.6 0.0 copy-start.2
  94.6 0.2 fusion
  94.8 18.6 %all_to_all.16.pieces_ref = bf16[8,48,384]{2,1,0:T(8,128)(2,1)S(1)} all-to-all(bf16[8,48,384]{2,1,0:T(8,128)(2,1)S(1)} %fusion), channel_id=1, replica_groups=mesh['z'=8,'xlo'=2,'xhi'=2,'y'=8,'core'=2] {'z'}, dimensions={0} | all-to-all | bytes 589824 | tf_op jit(solution)/shard_map/all_to_all | solution.py:170
  113.4 0.0 copy-done.1
  113.4 0.0 copy-done.2
  113.4 0.0 copy-done.3
  113.4 0.0 copy-done.4
  113.4 0.8 shard_map.96
  (10 shorter events, 0.2 us)
Async XLA Ops:
  1.7 11.4 %collective-permute-start = (bf16[2,197,384]{2,1,0:T(8,128)(2,1)S(1)}, bf16[2,197,384]{2,1,0:T(8,128)(2,1)S(1)}, u32[]{:S(2)}, u32[]{:S(2)}) collective-permute-start(bf16[2,197,384]{2,1,0:T(8,128)(2,1)S(1)} %pad_maximum_fusion), channel_id=1, source_target_pairs={{0,2},{1,15},{2,4},{3,1},{4,6},{5,3},{6,8},{7,5},{8,10},{9,7},{10,... | collective-permute-start | bytes 907784 | tf_op jit(solution)/shard_map/ppermute | solution.py:124
  6.4 12.3 %collective-permute-start.3 = (bf16[2,197,384]{2,1,0:T(8,128)(2,1)S(1)}, bf16[2,197,384]{2,1,0:T(8,128)(2,1)S(1)}, u32[]{:S(2)}, u32[]{:S(2)}) collective-permute-start(bf16[2,197,384]{2,1,0:T(8,128)(2,1)S(1)} %pad_maximum_fusion), channel_id=1, source_target_pairs={{0,14},{1,3},{2,0},{3,5},{4,2},{5,7},{6,4},{7,9},{8,6},{9,11},{10,... | collective-permute-start | bytes 907784 | tf_op jit(solution)/shard_map/ppermute | solution.py:125
  13.1 22.7 %collective-permute-start.1 = (bf16[2,197,384]{2,1,0:T(8,128)(2,1)S(1)}, bf16[2,197,384]{2,1,0:T(8,128)(2,1)S(1)}, u32[]{:S(2)}, u32[]{:S(2)}) collective-permute-start(bf16[2,197,384]{2,1,0:T(8,128)(2,1)S(1)} %collective-permute-done), channel_id=1, source_target_pairs={{0,2},{1,15},{2,4},{3,1},{4,6},{5,3},{6,8},{7,5},{8,10},{9,7},{10,... | collective-permute-start | bytes 907784 | tf_op jit(solution)/shard_map/ppermute | solution.py:124
  18.7 22.2 %collective-permute-start.4 = (bf16[2,197,384]{2,1,0:T(8,128)(2,1)S(1)}, bf16[2,197,384]{2,1,0:T(8,128)(2,1)S(1)}, u32[]{:S(2)}, u32[]{:S(2)}) collective-permute-start(bf16[2,197,384]{2,1,0:T(8,128)(2,1)S(1)} %collective-permute-done.3), channel_id=1, source_target_pairs={{0,14},{1,3},{2,0},{3,5},{4,2},{5,7},{6,4},{7,9},{8,6},{9,11},{10,... | collective-permute-start | bytes 907784 | tf_op jit(solution)/shard_map/ppermute | solution.py:125
  22.3 41.1 %all-to-all-start = ((bf16[32,96,96]{2,1,0:T(8,128)(2,1)}), bf16[32,96,96]{2,1,0:T(8,128)(2,1)}, u32[]{:S(2)}, u32[]{:S(2)}) async-start(bf16[32,96,96]{2,1,0:T(8,128)(2,1)} %broadcast_in_dim.2), calls=%async_computation | async-start | bytes 1572864 | tf_op jit(solution)/shard_map/all_to_all | solution.py:154
  35.6 7.3 %copy-start.5 = (bf16[197,384]{1,0:T(8,128)(2,1)S(1)}, bf16[197,384]{1,0:T(8,128)(2,1)}, u32[]{:S(2)}) copy-start(bf16[197,384]{1,0:T(8,128)(2,1)} %param.6) | copy-start | bytes 453892
  35.6 7.4 %copy-start.6 = (bf16[197,384]{1,0:T(8,128)(2,1)S(1)}, bf16[197,384]{1,0:T(8,128)(2,1)}, u32[]{:S(2)}) copy-start(bf16[197,384]{1,0:T(8,128)(2,1)} %param.7) | copy-start | bytes 453892
  35.7 11.7 %collective-permute-start.2 = (bf16[2,197,384]{2,1,0:T(8,128)(2,1)S(1)}, bf16[2,197,384]{2,1,0:T(8,128)(2,1)S(1)}, u32[]{:S(2)}, u32[]{:S(2)}) collective-permute-start(bf16[2,197,384]{2,1,0:T(8,128)(2,1)S(1)} %collective-permute-done.1), channel_id=1, source_target_pairs={{0,2},{1,15},{2,4},{3,1},{4,6},{5,3},{6,8},{7,5},{8,10},{9,7},{10,... | collective-permute-start | bytes 907784 | tf_op jit(solution)/shard_map/ppermute | solution.py:124
  40.9 12.2 %collective-permute-start.5 = (bf16[2,197,384]{2,1,0:T(8,128)(2,1)S(1)}, bf16[2,197,384]{2,1,0:T(8,128)(2,1)S(1)}, u32[]{:S(2)}, u32[]{:S(2)}) collective-permute-start(bf16[2,197,384]{2,1,0:T(8,128)(2,1)S(1)} %collective-permute-done.4), channel_id=1, source_target_pairs={{0,14},{1,3},{2,0},{3,5},{4,2},{5,7},{6,4},{7,9},{8,6},{9,11},{10,... | collective-permute-start | bytes 907784 | tf_op jit(solution)/shard_map/ppermute | solution.py:125
  43.0 22.6 %collective-permute-start.9 = (bf16[10,197,384]{2,1,0:T(8,128)(2,1)S(1)}, bf16[10,197,384]{2,1,0:T(8,128)(2,1)}, u32[]{:S(2)}, u32[]{:S(2)}) collective-permute-start(bf16[10,197,384]{2,1,0:T(8,128)(2,1)S(1)} %constant_dynamic-update-slice_fusion.4.own_ref), channel_id=1, source_target_pairs={{0,1},{1,0},{2,3},{3,2},{4,5},{5,4},{6,7},{7,6},{8,9},{9,8},{10,11... | collective-permute-start | bytes 4538888 | tf_op jit(solution)/shard_map/ppermute | solution.py:120
  47.5 8.5 %collective-permute-start.6 = (bf16[1,197,384]{2,1,0:T(8,128)(2,1)S(1)}, bf16[1,197,384]{2,1,0:T(8,128)(2,1)S(1)}, u32[]{:S(2)}, u32[]{:S(2)}) collective-permute-start(bf16[1,197,384]{2,1,0:T(8,128)(2,1)S(1)} %slice.24), channel_id=1, source_target_pairs={{0,2},{1,15},{2,4},{3,1},{4,6},{5,3},{6,8},{7,5},{8,10},{9,7},{10,... | collective-permute-start | bytes 453896 | tf_op jit(solution)/shard_map/ppermute | solution.py:126
  53.1 8.3 %collective-permute-start.7 = (bf16[1,197,384]{2,1,0:T(8,128)(2,1)S(1)}, bf16[1,197,384]{2,1,0:T(8,128)(2,1)S(1)}, u32[]{:S(2)}, u32[]{:S(2)}) collective-permute-start(bf16[1,197,384]{2,1,0:T(8,128)(2,1)S(1)} %slice.25), channel_id=1, source_target_pairs={{0,14},{1,3},{2,0},{3,5},{4,2},{5,7},{6,4},{7,9},{8,6},{9,11},{10,... | collective-permute-start | bytes 453896 | tf_op jit(solution)/shard_map/ppermute | solution.py:126
  61.5 9.8 %collective-permute-start.8 = (bf16[6,197,384]{2,1,0:T(8,128)(2,1)S(1)}, bf16[6,197,384]{2,1,0:T(8,128)(2,1)S(1)}, u32[]{:S(2)}, u32[]{:S(2)}) collective-permute-start(bf16[6,197,384]{2,1,0:T(8,128)(2,1)S(1)} %constant_dynamic-update-slice_fusion.own_ref), channel_id=1, source_target_pairs={{0,1},{1,0},{2,3},{3,2},{4,5},{5,4},{6,7},{7,6},{8,9},{9,8},{10,11... | collective-permute-start | bytes 2723336 | tf_op jit(solution)/shard_map/ppermute | solution.py:120
  65.6 1.1 copy-start
  94.6 18.8 %copy-start.1 = (bf16[96,48]{0,1:T(8,128)(2,1)S(1)}, bf16[96,48]{0,1:T(8,128)(2,1)}, u32[]{:S(2)}) copy-start(bf16[96,48]{0,1:T(8,128)(2,1)} %param.9) | copy-start | bytes 27652
  94.6 18.8 %copy-start.2 = (bf16[48,96]{1,0:T(8,128)(2,1)S(1)}, bf16[48,96]{1,0:T(8,128)(2,1)}, u32[]{:S(2)}) copy-start(bf16[48,96]{1,0:T(8,128)(2,1)} %w_in_ref.1) | copy-start | bytes 27652
  94.6 18.8 %copy-start.3 = (f32[48,96]{1,0:T(8,128)S(1)}, f32[48,96]{1,0:T(8,128)}, u32[]{:S(2)}) copy-start(f32[48,96]{1,0:T(8,128)} %prec_in_ref.1) | copy-start | bytes 55300
  94.6 18.8 %copy-start.4 = (f32[96,48]{0,1:T(8,128)S(1)}, f32[96,48]{0,1:T(8,128)}, u32[]{:S(2)}) copy-start(f32[96,48]{0,1:T(8,128)} %param.11) | copy-start | bytes 55300

commit v11 on v10

--- a/solution.py
+++ b/solution.py
@@ -123,9 +123,12 @@
     for _ in range(n // 2 - 1):
         up.append(lax.ppermute(up[-1], GROUP, turned(1)))
         down.append(lax.ppermute(down[-1], GROUP, turned(-1)))
+    early = jnp.concatenate([up[1], down[1], up[2], down[2], own])
+    up[3], down[3], turned_weights, early = lax.optimization_barrier(
+        (up[3], down[3], turned_weights, early)
+    )
     opposite = [lax.ppermute(up[3][:1], GROUP, turned(1)), lax.ppermute(down[3][1:], GROUP, turned(-1))]
 
-    early = jnp.concatenate([up[1], down[1], up[2], down[2], own])
     late = jnp.concatenate([up[3], down[3], *opposite])
     return (early, swap(early)), (late, swap(late)), turned_weights
 
@@ -156,6 +159,7 @@
         functools.partial(turn_kernel, pairs=pairs, cols=cols, deep=deep),
         out_shape=jax.ShapeDtypeStruct((2 * hid, dp * d_own), BF16),
 
+        compiler_params=pltpu.CompilerParams(vmem_limit_bytes=8 << 20),
         cost_estimate=pl.CostEstimate(flops=TURN_FLOPS, bytes_accessed=4 * arrived.size, transcendentals=0),
     )(arrived)
     early, late, turned = round_the_ring(jnp.stack([inputs, cotangent]), turned)

time: 115 us -> 115 us (level)
  the two profiles are of different devices: /device:TPU:24 before, /device:TPU:56 now
where the time goes in v11:
time: 115 us; the launch traced here: 114 us
  starting transfers between devices  44.9 us (39%)
  blocking collectives  39.5 us (34%)
  waiting for transfers between devices  13.1 us (11%)
  Pallas kernels  8.62 us (7%)
  local copies, waits for them, and re-layouts  5.55 us (5%)
  other arithmetic  1.91 us (2%)
    all_to_all x1, blocking collectives, per_device(): pieces = lax.all_to_all(pieces, ROW, 0, 0, tiled=True)  21 us
    all_to_all x1, blocking collectives, per_device(): pieces = lax.all_to_all(pieces, 'z', 0, 0, tiled=True)  18.6 us
    ppermute x3, starting transfers between devices, round_the_ring(): up.append(lax.ppermute(up[-1], GROUP, turned(1)))  15.9 us
    all_to_all x1, starting transfers between devices, per_device(): arrived = lax.all_to_all(both, OWNERS, 0, 0, tiled=True)  11.2 us
    pallas_call x2, Pallas kernels, run_images(): pl.pallas_call(kernel, in_specs=[pl.BlockSpec(memory_space=pltpu.SMEM)] +...  7.52 us
    ppermute x3, starting transfers between devices, round_the_ring(): down.append(lax.ppermute(down[-1], GROUP, turned(-1)))  7.34 us
    ppermute x3, waiting for transfers between devices, round_the_ring(): down.append(lax.ppermute(down[-1], GROUP, turned(-1)))  6.78 us
    ppermute x1, waiting for transfers between devices, round_the_ring(): lax.ppermute(down[3][1:], GROUP, turned(-1))  5.64 us
  transfers between devices with their start and end apart: 11, of which 4 were waited for; matrix products, arithmetic and copies ran while one was open for 5% of the time, Pallas kernels for 5%

profile of v11, /device:TPU:56, one launch (start us, length us, event | category | flops | bytes accessed | tf_op | source)
XLA Modules:
  0.0 114.4 jit_solution(4556074693209374832)
XLA Ops:
  0.6 1.0 pad_maximum_fusion
  1.7 3.3 %collective-permute-start.3 = (bf16[2,197,384]{2,1,0:T(8,128)(2,1)S(1)}, bf16[2,197,384]{2,1,0:T(8,128)(2,1)S(1)}, u32[]{:S(2)}, u32[]{:S(2)}) collective-permute-start(bf16[2,197,384]{2,1,0:T(8,128)(2,1)S(1)} %pad_maximum_fusion), channel_id=1, source_target_pairs={{0,14},{1,3},{2,0},{3,5},{4,2},{5,7},{6,4},{7,9},{8,6},{9,11},{10,... | collective-permute-start | bytes 907784 | tf_op jit(solution)/shard_map/ppermute | solution.py:125
  4.9 5.7 %collective-permute-start = (bf16[2,197,384]{2,1,0:T(8,128)(2,1)S(1)}, bf16[2,197,384]{2,1,0:T(8,128)(2,1)S(1)}, u32[]{:S(2)}, u32[]{:S(2)}) collective-permute-start(bf16[2,197,384]{2,1,0:T(8,128)(2,1)S(1)} %pad_maximum_fusion), channel_id=1, source_target_pairs={{0,2},{1,15},{2,4},{3,1},{4,6},{5,3},{6,8},{7,5},{8,10},{9,7},{10,... | collective-permute-start | bytes 907784 | tf_op jit(solution)/shard_map/ppermute | solution.py:124
  10.6 0.7 pad_maximum_fusion.1
  11.4 1.0 broadcast_in_dim.2
  12.4 11.2 %all-to-all-start = ((bf16[32,96,96]{2,1,0:T(8,128)(2,1)}), bf16[32,96,96]{2,1,0:T(8,128)(2,1)S(1)}, u32[]{:S(2)}, u32[]{:S(2)}) async-start(bf16[32,96,96]{2,1,0:T(8,128)(2,1)} %broadcast_in_dim.2), calls=%async_computation | async-start | bytes 1572864 | tf_op jit(solution)/shard_map/all_to_all | solution.py:157
  23.6 0.0 copy-start.4
  23.6 0.0 copy-start.5
  23.6 0.0 collective-permute-done.3
  23.7 2.2 %collective-permute-start.4 = (bf16[2,197,384]{2,1,0:T(8,128)(2,1)S(1)}, bf16[2,197,384]{2,1,0:T(8,128)(2,1)S(1)}, u32[]{:S(2)}, u32[]{:S(2)}) collective-permute-start(bf16[2,197,384]{2,1,0:T(8,128)(2,1)S(1)} %collective-permute-done.3), channel_id=1, source_target_pairs={{0,14},{1,3},{2,0},{3,5},{4,2},{5,7},{6,4},{7,9},{8,6},{9,11},{10,... | collective-permute-start | bytes 907784 | tf_op jit(solution)/shard_map/ppermute | solution.py:125
  25.8 0.0 collective-permute-done
  25.9 5.0 %collective-permute-start.1 = (bf16[2,197,384]{2,1,0:T(8,128)(2,1)S(1)}, bf16[2,197,384]{2,1,0:T(8,128)(2,1)S(1)}, u32[]{:S(2)}, u32[]{:S(2)}) collective-permute-start(bf16[2,197,384]{2,1,0:T(8,128)(2,1)S(1)} %collective-permute-done), channel_id=1, source_target_pairs={{0,2},{1,15},{2,4},{3,1},{4,6},{5,3},{6,8},{7,5},{8,10},{9,7},{10,... | collective-permute-start | bytes 907784 | tf_op jit(solution)/shard_map/ppermute | solution.py:124
  30.9 0.7 constant_dynamic-update-slice_fusion.5
  31.6 0.8 constant_dynamic-update-slice_fusion.4
  32.4 4.6 %collective-permute-done.4 = bf16[2,197,384]{2,1,0:T(8,128)(2,1)S(1)} collective-permute-done((bf16[2,197,384]{2,1,0:T(8,128)(2,1)S(1)}, bf16[2,197,384]{2,1,0:T(8,128)(2,1)S(1)}, u32[]{:S(2)}, u32[]{:S(2)}) %collective-permute-start.4) | collective-permute-done | bytes 302624 | tf_op jit(solution)/shard_map/ppermute | solution.py:125
  37.0 1.9 %collective-permute-start.5 = (bf16[2,197,384]{2,1,0:T(8,128)(2,1)S(1)}, bf16[2,197,384]{2,1,0:T(8,128)(2,1)S(1)}, u32[]{:S(2)}, u32[]{:S(2)}) collective-permute-start(bf16[2,197,384]{2,1,0:T(8,128)(2,1)S(1)} %collective-permute-done.4), channel_id=1, source_target_pairs={{0,14},{1,3},{2,0},{3,5},{4,2},{5,7},{6,4},{7,9},{8,6},{9,11},{10,... | collective-permute-start | bytes 907784 | tf_op jit(solution)/shard_map/ppermute | solution.py:125
  38.9 0.0 collective-permute-done.1
  38.9 5.1 %collective-permute-start.2 = (bf16[2,197,384]{2,1,0:T(8,128)(2,1)S(1)}, bf16[2,197,384]{2,1,0:T(8,128)(2,1)S(1)}, u32[]{:S(2)}, u32[]{:S(2)}) collective-permute-start(bf16[2,197,384]{2,1,0:T(8,128)(2,1)S(1)} %collective-permute-done.1), channel_id=1, source_target_pairs={{0,2},{1,15},{2,4},{3,1},{4,6},{5,3},{6,8},{7,5},{8,10},{9,7},{10,... | collective-permute-start | bytes 907784 | tf_op jit(solution)/shard_map/ppermute | solution.py:124
  44.1 0.8 constant_dynamic-update-slice_fusion.3
  44.8 0.8 constant_dynamic-update-slice_fusion.2
  45.6 0.0 copy-done.4
  45.6 0.7 constant_dynamic-update-slice_fusion.1
  46.3 0.0 copy-done.5
  46.3 0.7 constant_dynamic-update-slice_fusion.own_ref
  47.0 0.0 all-to-all-done.arrived_ref
  47.0 0.2 shard_map.93.turned_ref
  47.2 2.1 %collective-permute-done.5 = bf16[2,197,384]{2,1,0:T(8,128)(2,1)S(1)} collective-permute-done((bf16[2,197,384]{2,1,0:T(8,128)(2,1)S(1)}, bf16[2,197,384]{2,1,0:T(8,128)(2,1)S(1)}, u32[]{:S(2)}, u32[]{:S(2)}) %collective-permute-start.5) | collective-permute-done | bytes 302624 | tf_op jit(solution)/shard_map/ppermute | solution.py:125
  49.4 0.0 collective-permute-done.2
  49.4 1.9 %collective-permute-start.9 = (bf16[10,197,384]{2,1,0:T(8,128)(2,1)}, bf16[10,197,384]{2,1,0:T(8,128)(2,1)}, u32[]{:S(2)}, u32[]{:S(2)}) collective-permute-start(bf16[10,197,384]{2,1,0:T(8,128)(2,1)} %constant_dynamic-update-slice_fusion.own_ref), channel_id=1, source_target_pairs={{0,1},{1,0},{2,3},{3,2},{4,5},{5,4},{6,7},{7,6},{8,9},{9,8},{10,11... | collective-permute-start | bytes 4538888 | tf_op jit(solution)/shard_map/ppermute | solution.py:120
  51.3 4.7 %collective-permute-start.6 = (bf16[1,197,384]{2,1,0:T(8,128)(2,1)S(1)}, bf16[1,197,384]{2,1,0:T(8,128)(2,1)S(1)}, u32[]{:S(2)}, u32[]{:S(2)}) collective-permute-start(bf16[1,197,384]{2,1,0:T(8,128)(2,1)S(1)} %slice.18), channel_id=1, source_target_pairs={{0,2},{1,15},{2,4},{3,1},{4,6},{5,3},{6,8},{7,5},{8,10},{9,7},{10,... | collective-permute-start | bytes 453896 | tf_op jit(solution)/shard_map/ppermute | solution.py:130
  56.0 1.9 %collective-permute-start.7 = (bf16[1,197,384]{2,1,0:T(8,128)(2,1)S(1)}, bf16[1,197,384]{2,1,0:T(8,128)(2,1)S(1)}, u32[]{:S(2)}, u32[]{:S(2)}) collective-permute-start(bf16[1,197,384]{2,1,0:T(8,128)(2,1)S(1)} %slice.19), channel_id=1, source_target_pairs={{0,14},{1,3},{2,0},{3,5},{4,2},{5,7},{6,4},{7,9},{8,6},{9,11},{10,... | collective-permute-start | bytes 453896 | tf_op jit(solution)/shard_map/ppermute | solution.py:130
  58.0 0.1 constant_dynamic-update-slice_fusion.8
  58.0 0.7 collective-permute-done.6
  58.7 5.6 %collective-permute-done.7 = bf16[1,197,384]{2,1,0:T(8,128)(2,1)S(1)} collective-permute-done((bf16[1,197,384]{2,1,0:T(8,128)(2,1)S(1)}, bf16[1,197,384]{2,1,0:T(8,128)(2,1)S(1)}, u32[]{:S(2)}, u32[]{:S(2)}) %collective-permute-start.7) | collective-permute-done | bytes 151328 | tf_op jit(solution)/shard_map/ppermute | solution.py:130
  64.4 1.9 %collective-permute-start.8 = (bf16[6,197,384]{2,1,0:T(8,128)(2,1)S(1)}, bf16[6,197,384]{2,1,0:T(8,128)(2,1)S(1)}, u32[]{:S(2)}, u32[]{:S(2)}) collective-permute-start(bf16[6,197,384]{2,1,0:T(8,128)(2,1)S(1)} %constant_dynamic-update-slice_fusion.6.own_ref), channel_id=1, source_target_pairs={{0,1},{1,0},{2,3},{3,2},{4,5},{5,4},{6,7},{7,6},{8,9},{9,8},{10,11... | collective-permute-start | bytes 2723336 | tf_op jit(solution)/shard_map/ppermute | solution.py:120
  66.3 0.0 collective-permute-done.9.far_ref
  66.3 5.0 %shard_map.94 = (f32[192,768]{1,0:T(8,128)S(1)}, f32[192,768]{1,0:T(8,128)S(1)}, f32[192,768]{1,0:T(8,128)S(1)}, f32[192,768]{1,0:T(8,128)S(1)}) custom-call(s32[1]{0:T(128)} %bitcast.core_ref, bf16[10,197,384]{2,1,0:T(8,128)(2,1)} %constant_dynamic-update-slice_fusion.own_ref, bf16[10,197,384]{2,1,0:T(8,128)(2,1)} %collective-permute-done.9.far_ref, ...), custom_call_target="tpu_custom_call" | custom-call | flops 1161953280 | bytes 3025920 | tf_op jit(solution)/shard_map/pallas_call | solution.py:94
  71.3 0.0 collective-permute-done.8.far_ref
  71.3 2.5 %shard_map.95 = bf16[2,2,8,48,384]{4,3,2,1,0:T(8,128)(2,1)S(1)} custom-call(s32[1]{0:T(128)} %bitcast.core_ref, bf16[6,197,384]{2,1,0:T(8,128)(2,1)S(1)} %constant_dynamic-update-slice_fusion.6.own_ref, bf16[6,197,384]{2,1,0:T(8,128)(2,1)S(1)} %collective-permute-done.8.far_ref, bf16[384,768]{1,0:T(8,128)(2,1)S(1)} %shard_map.93.turned_ref, ...), custom_call_target="tpu_custom_call" | custom-call | flops 697171968 | bytes 1815552 | tf_op jit(solution)/shard_map/pallas_call | solution.py:94
  73.9 21.0 %all_to_all.15 = bf16[4,8,48,384]{3,2,1,0:T(8,128)(2,1)S(1)} all-to-all(bf16[4,8,48,384]{3,2,1,0:T(8,128)(2,1)S(1)} %bitcast.12), channel_id=1, replica_groups=mesh['z'=8,'xlo'=2,'xhi'=2,'y'=8,'core'=2] {'xlo','xhi'}, dimensions={0} | all-to-all | bytes 2359296 | tf_op jit(solution)/shard_map/all_to_all | solution.py:172
  94.8 0.0 copy-start
  94.8 0.2 fusion
  95.0 18.6 %all_to_all.16.pieces_ref = bf16[8,48,384]{2,1,0:T(8,128)(2,1)S(1)} all-to-all(bf16[8,48,384]{2,1,0:T(8,128)(2,1)S(1)} %fusion), channel_id=1, replica_groups=mesh['z'=8,'xlo'=2,'xhi'=2,'y'=8,'core'=2] {'z'}, dimensions={0} | all-to-all | bytes 589824 | tf_op jit(solution)/shard_map/all_to_all | solution.py:174
  113.6 0.0 copy-done
  113.6 0.0 copy-done.1
  113.6 0.0 copy-done.2
  113.6 0.0 copy-done.3
  113.6 0.8 shard_map.96
  (8 shorter events, 0.1 us)
Async XLA Ops:
  1.7 22.0 %collective-permute-start.3 = (bf16[2,197,384]{2,1,0:T(8,128)(2,1)S(1)}, bf16[2,197,384]{2,1,0:T(8,128)(2,1)S(1)}, u32[]{:S(2)}, u32[]{:S(2)}) collective-permute-start(bf16[2,197,384]{2,1,0:T(8,128)(2,1)S(1)} %pad_maximum_fusion), channel_id=1, source_target_pairs={{0,14},{1,3},{2,0},{3,5},{4,2},{5,7},{6,4},{7,9},{8,6},{9,11},{10,... | collective-permute-start | bytes 907784 | tf_op jit(solution)/shard_map/ppermute | solution.py:125
  4.9 20.9 %collective-permute-start = (bf16[2,197,384]{2,1,0:T(8,128)(2,1)S(1)}, bf16[2,197,384]{2,1,0:T(8,128)(2,1)S(1)}, u32[]{:S(2)}, u32[]{:S(2)}) collective-permute-start(bf16[2,197,384]{2,1,0:T(8,128)(2,1)S(1)} %pad_maximum_fusion), channel_id=1, source_target_pairs={{0,2},{1,15},{2,4},{3,1},{4,6},{5,3},{6,8},{7,5},{8,10},{9,7},{10,... | collective-permute-start | bytes 907784 | tf_op jit(solution)/shard_map/ppermute | solution.py:124
  12.4 34.6 %all-to-all-start = ((bf16[32,96,96]{2,1,0:T(8,128)(2,1)}), bf16[32,96,96]{2,1,0:T(8,128)(2,1)S(1)}, u32[]{:S(2)}, u32[]{:S(2)}) async-start(bf16[32,96,96]{2,1,0:T(8,128)(2,1)} %broadcast_in_dim.2), calls=%async_computation | async-start | bytes 1572864 | tf_op jit(solution)/shard_map/all_to_all | solution.py:157
  23.6 22.0 %copy-start.4 = (bf16[197,384]{1,0:T(8,128)(2,1)S(1)}, bf16[197,384]{1,0:T(8,128)(2,1)}, u32[]{:S(2)}) copy-start(bf16[197,384]{1,0:T(8,128)(2,1)} %param.6) | copy-start | bytes 453892
  23.6 22.6 %copy-start.5 = (bf16[197,384]{1,0:T(8,128)(2,1)S(1)}, bf16[197,384]{1,0:T(8,128)(2,1)}, u32[]{:S(2)}) copy-start(bf16[197,384]{1,0:T(8,128)(2,1)} %param.7) | copy-start | bytes 453892
  23.7 13.3 %collective-permute-start.4 = (bf16[2,197,384]{2,1,0:T(8,128)(2,1)S(1)}, bf16[2,197,384]{2,1,0:T(8,128)(2,1)S(1)}, u32[]{:S(2)}, u32[]{:S(2)}) collective-permute-start(bf16[2,197,384]{2,1,0:T(8,128)(2,1)S(1)} %collective-permute-done.3), channel_id=1, source_target_pairs={{0,14},{1,3},{2,0},{3,5},{4,2},{5,7},{6,4},{7,9},{8,6},{9,11},{10,... | collective-permute-start | bytes 907784 | tf_op jit(solution)/shard_map/ppermute | solution.py:125
  25.9 13.1 %collective-permute-start.1 = (bf16[2,197,384]{2,1,0:T(8,128)(2,1)S(1)}, bf16[2,197,384]{2,1,0:T(8,128)(2,1)S(1)}, u32[]{:S(2)}, u32[]{:S(2)}) collective-permute-start(bf16[2,197,384]{2,1,0:T(8,128)(2,1)S(1)} %collective-permute-done), channel_id=1, source_target_pairs={{0,2},{1,15},{2,4},{3,1},{4,6},{5,3},{6,8},{7,5},{8,10},{9,7},{10,... | collective-permute-start | bytes 907784 | tf_op jit(solution)/shard_map/ppermute | solution.py:124
  37.0 12.3 %collective-permute-start.5 = (bf16[2,197,384]{2,1,0:T(8,128)(2,1)S(1)}, bf16[2,197,384]{2,1,0:T(8,128)(2,1)S(1)}, u32[]{:S(2)}, u32[]{:S(2)}) collective-permute-start(bf16[2,197,384]{2,1,0:T(8,128)(2,1)S(1)} %collective-permute-done.4), channel_id=1, source_target_pairs={{0,14},{1,3},{2,0},{3,5},{4,2},{5,7},{6,4},{7,9},{8,6},{9,11},{10,... | collective-permute-start | bytes 907784 | tf_op jit(solution)/shard_map/ppermute | solution.py:125
  38.9 10.4 %collective-permute-start.2 = (bf16[2,197,384]{2,1,0:T(8,128)(2,1)S(1)}, bf16[2,197,384]{2,1,0:T(8,128)(2,1)S(1)}, u32[]{:S(2)}, u32[]{:S(2)}) collective-permute-start(bf16[2,197,384]{2,1,0:T(8,128)(2,1)S(1)} %collective-permute-done.1), channel_id=1, source_target_pairs={{0,2},{1,15},{2,4},{3,1},{4,6},{5,3},{6,8},{7,5},{8,10},{9,7},{10,... | collective-permute-start | bytes 907784 | tf_op jit(solution)/shard_map/ppermute | solution.py:124
  49.4 17.0 %collective-permute-start.9 = (bf16[10,197,384]{2,1,0:T(8,128)(2,1)}, bf16[10,197,384]{2,1,0:T(8,128)(2,1)}, u32[]{:S(2)}, u32[]{:S(2)}) collective-permute-start(bf16[10,197,384]{2,1,0:T(8,128)(2,1)} %constant_dynamic-update-slice_fusion.own_ref), channel_id=1, source_target_pairs={{0,1},{1,0},{2,3},{3,2},{4,5},{5,4},{6,7},{7,6},{8,9},{9,8},{10,11... | collective-permute-start | bytes 4538888 | tf_op jit(solution)/shard_map/ppermute | solution.py:120
  51.3 7.4 %collective-permute-start.6 = (bf16[1,197,384]{2,1,0:T(8,128)(2,1)S(1)}, bf16[1,197,384]{2,1,0:T(8,128)(2,1)S(1)}, u32[]{:S(2)}, u32[]{:S(2)}) collective-permute-start(bf16[1,197,384]{2,1,0:T(8,128)(2,1)S(1)} %slice.18), channel_id=1, source_target_pairs={{0,2},{1,15},{2,4},{3,1},{4,6},{5,3},{6,8},{7,5},{8,10},{9,7},{10,... | collective-permute-start | bytes 453896 | tf_op jit(solution)/shard_map/ppermute | solution.py:130
  56.0 8.3 %collective-permute-start.7 = (bf16[1,197,384]{2,1,0:T(8,128)(2,1)S(1)}, bf16[1,197,384]{2,1,0:T(8,128)(2,1)S(1)}, u32[]{:S(2)}, u32[]{:S(2)}) collective-permute-start(bf16[1,197,384]{2,1,0:T(8,128)(2,1)S(1)} %slice.19), channel_id=1, source_target_pairs={{0,14},{1,3},{2,0},{3,5},{4,2},{5,7},{6,4},{7,9},{8,6},{9,11},{10,... | collective-permute-start | bytes 453896 | tf_op jit(solution)/shard_map/ppermute | solution.py:130
  64.4 6.9 %collective-permute-start.8 = (bf16[6,197,384]{2,1,0:T(8,128)(2,1)S(1)}, bf16[6,197,384]{2,1,0:T(8,128)(2,1)S(1)}, u32[]{:S(2)}, u32[]{:S(2)}) collective-permute-start(bf16[6,197,384]{2,1,0:T(8,128)(2,1)S(1)} %constant_dynamic-update-slice_fusion.6.own_ref), channel_id=1, source_target_pairs={{0,1},{1,0},{2,3},{3,2},{4,5},{5,4},{6,7},{7,6},{8,9},{9,8},{10,11... | collective-permute-start | bytes 2723336 | tf_op jit(solution)/shard_map/ppermute | solution.py:120
  94.8 18.7 %copy-start = (bf16[96,48]{0,1:T(8,128)(2,1)S(1)}, bf16[96,48]{0,1:T(8,128)(2,1)}, u32[]{:S(2)}) copy-start(bf16[96,48]{0,1:T(8,128)(2,1)} %param.9) | copy-start | bytes 27652
  94.8 18.7 %copy-start.1 = (bf16[48,96]{1,0:T(8,128)(2,1)S(1)}, bf16[48,96]{1,0:T(8,128)(2,1)}, u32[]{:S(2)}) copy-start(bf16[48,96]{1,0:T(8,128)(2,1)} %w_in_ref.1) | copy-start | bytes 27652
  94.8 18.7 %copy-start.2 = (f32[48,96]{1,0:T(8,128)S(1)}, f32[48,96]{1,0:T(8,128)}, u32[]{:S(2)}) copy-start(f32[48,96]{1,0:T(8,128)} %prec_in_ref.1) | copy-start | bytes 55300
  94.8 18.7 %copy-start.3 = (f32[96,48]{0,1:T(8,128)S(1)}, f32[96,48]{0,1:T(8,128)}, u32[]{:S(2)}) copy-start(f32[96,48]{0,1:T(8,128)} %param.11) | copy-start | bytes 55300

commit v12 on v10

--- a/solution.py
+++ b/solution.py
@@ -70,7 +70,8 @@
             turned_ref[rows, :] = jnp.concatenate(blocks, axis=0).T
 
 
-def first_kernel(core_ref, own_ref, far_ref, turned_ref, *sums):
+def first_kernel(core_ref, own_ref, far_ref, arrived_ref, turned_ref, *sums, pairs, cols, deep):
+    turn_kernel(arrived_ref, turned_ref, pairs=pairs, cols=cols, deep=deep)
     for ref, term in zip(sums, summed(core_ref, own_ref, far_ref, turned_ref)):
         ref[...] = term
 
@@ -89,7 +90,7 @@
 
 def run_images(kernel, core, own, far, turned, sums, outs):
     pieces, seq, part = own.shape
-    rows, d = turned.shape
+    rows, d = (outs[0] if sums == () else turned).shape
     vmem = pl.BlockSpec(memory_space=pltpu.VMEM)
     return pl.pallas_call(
         kernel,
@@ -126,6 +127,7 @@
     opposite = [lax.ppermute(up[3][:1], GROUP, turned(1)), lax.ppermute(down[3][1:], GROUP, turned(-1))]
 
     early = jnp.concatenate([up[1], down[1], up[2], down[2], own])
+    *opposite, turned_weights = lax.optimization_barrier((*opposite, turned_weights))
     late = jnp.concatenate([up[3], down[3], *opposite])
     return (early, swap(early)), (late, swap(late)), turned_weights
 
@@ -152,17 +154,13 @@
     both = jnp.concatenate([w_in, w_out.T], axis=0)
     both = jnp.broadcast_to(both[None], (cols * dp, *both.shape))
     arrived = lax.all_to_all(both, OWNERS, 0, 0, tiled=True)
-    turned = pl.pallas_call(
-        functools.partial(turn_kernel, pairs=pairs, cols=cols, deep=deep),
-        out_shape=jax.ShapeDtypeStruct((2 * hid, dp * d_own), BF16),
-
-        cost_estimate=pl.CostEstimate(flops=TURN_FLOPS, bytes_accessed=4 * arrived.size, transcendentals=0),
-    )(arrived)
-    early, late, turned = round_the_ring(jnp.stack([inputs, cotangent]), turned)
+    early, late, arrived = round_the_ring(jnp.stack([inputs, cotangent]), arrived)
     core = lax.axis_index("core").reshape(1).astype(jnp.int32)
     partial = [jax.ShapeDtypeStruct((hid, dp * d_own), F32)] * 4
     packed = jax.ShapeDtypeStruct((pairs, cols, deep, d_own, 4 * h_own), BF16)
-    partial = run_images(first_kernel, core, *early, turned, (), partial)
+    turned = jax.ShapeDtypeStruct((2 * hid, dp * d_own), BF16)
+    first = functools.partial(first_kernel, pairs=pairs, cols=cols, deep=deep)
+    turned, *partial = run_images(first, core, *early, arrived, (), [turned, *partial])
     (pieces,) = run_images(last_kernel, core, *late, turned, tuple(partial), [packed])
     pieces = pieces.reshape(pairs * cols, deep, d_own, 4 * h_own)
     pieces = lax.all_to_all(pieces, ROW, 0, 0, tiled=True)

time: 115 us -> 113 us (0.983)
  local copies, waits for them, and re-layouts: 2.48 us -> 5.56 us
  waiting for transfers between devices: 13.6 us -> 11.1 us
  Pallas kernels: 10 us -> 8.3 us
    ppermute x3, waiting for transfers between devices: 7.3 us -> 4.78 us  [round_the_ring(): up.append(lax.ppermute(up[-1], GROUP, turned(1)))]
    unnamed x22 -> x20, local copies, waits for them, and re-layouts: 1.41 us -> 3.82 us
    pallas_call x1 -> x0, Pallas kernels: 2.22 us -> none  [per_device(): pl.pallas_call(functools.partial(turn_kernel, pairs=pairs, cols=cols, dee...]
  transfers between devices with their start and end apart: 11 -> 11, of which waited for: 4 -> 3; matrix products, arithmetic and copies ran while one was open for 2% -> 6% of each run, Pallas kernels for 6% -> 4%
where the time goes in v12:
time: 113 us
  starting transfers between devices  45.5 us (40%)
  blocking collectives  39.5 us (35%)
  waiting for transfers between devices  11.1 us (10%)
  Pallas kernels  8.3 us (7%)
  local copies, waits for them, and re-layouts  5.56 us (5%)
  other arithmetic  1.91 us (2%)
    all_to_all x1, blocking collectives, per_device(): pieces = lax.all_to_all(pieces, ROW, 0, 0, tiled=True)  21 us
    all_to_all x1, blocking collectives, per_device(): pieces = lax.all_to_all(pieces, 'z', 0, 0, tiled=True)  18.6 us
    ppermute x3, starting transfers between devices, round_the_ring(): up.append(lax.ppermute(up[-1], GROUP, turned(1)))  15.4 us
    all_to_all x1, starting transfers between devices, per_device(): arrived = lax.all_to_all(both, OWNERS, 0, 0, tiled=True)  13.2 us
    pallas_call x2, Pallas kernels, run_images(): pl.pallas_call(kernel, in_specs=[pl.BlockSpec(memory_space=pltpu.SMEM)] +...  7.45 us
    ppermute x3, starting transfers between devices, round_the_ring(): down.append(lax.ppermute(down[-1], GROUP, turned(-1)))  5.76 us
    ppermute x1, starting transfers between devices, round_the_ring(): lax.ppermute(up[3][:1], GROUP, turned(1))  5.45 us
    ppermute x1, waiting for transfers between devices, round_the_ring(): lax.ppermute(down[3][1:], GROUP, turned(-1))  5.2 us
  transfers between devices with their start and end apart: 11, of which 3 were waited for; matrix products, arithmetic and copies ran while one was open for 6% of the time, Pallas kernels for 4%

profile of v12, /device:TPU:24, one launch (start us, length us, event | category | flops | bytes accessed | tf_op | source)
XLA Modules:
  0.0 112.8 jit_solution(4676846585114226871)
XLA Ops:
  0.6 1.0 pad_maximum_fusion
  1.7 4.7 %collective-permute-start = (bf16[2,197,384]{2,1,0:T(8,128)(2,1)S(1)}, bf16[2,197,384]{2,1,0:T(8,128)(2,1)S(1)}, u32[]{:S(2)}, u32[]{:S(2)}) collective-permute-start(bf16[2,197,384]{2,1,0:T(8,128)(2,1)S(1)} %pad_maximum_fusion), channel_id=1, source_target_pairs={{0,2},{1,15},{2,4},{3,1},{4,6},{5,3},{6,8},{7,5},{8,10},{9,7},{10,... | collective-permute-start | bytes 907784 | tf_op jit(solution)/shard_map/ppermute | solution.py:125
  6.4 1.9 %collective-permute-start.3 = (bf16[2,197,384]{2,1,0:T(8,128)(2,1)S(1)}, bf16[2,197,384]{2,1,0:T(8,128)(2,1)S(1)}, u32[]{:S(2)}, u32[]{:S(2)}) collective-permute-start(bf16[2,197,384]{2,1,0:T(8,128)(2,1)S(1)} %pad_maximum_fusion), channel_id=1, source_target_pairs={{0,14},{1,3},{2,0},{3,5},{4,2},{5,7},{6,4},{7,9},{8,6},{9,11},{10,... | collective-permute-start | bytes 907784 | tf_op jit(solution)/shard_map/ppermute | solution.py:126
  8.3 4.8 %collective-permute-done = bf16[2,197,384]{2,1,0:T(8,128)(2,1)S(1)} collective-permute-done((bf16[2,197,384]{2,1,0:T(8,128)(2,1)S(1)}, bf16[2,197,384]{2,1,0:T(8,128)(2,1)S(1)}, u32[]{:S(2)}, u32[]{:S(2)}) %collective-permute-start) | collective-permute-done | bytes 302624 | tf_op jit(solution)/shard_map/ppermute | solution.py:125
  13.1 5.6 %collective-permute-start.1 = (bf16[2,197,384]{2,1,0:T(8,128)(2,1)S(1)}, bf16[2,197,384]{2,1,0:T(8,128)(2,1)S(1)}, u32[]{:S(2)}, u32[]{:S(2)}) collective-permute-start(bf16[2,197,384]{2,1,0:T(8,128)(2,1)S(1)} %collective-permute-done), channel_id=1, source_target_pairs={{0,2},{1,15},{2,4},{3,1},{4,6},{5,3},{6,8},{7,5},{8,10},{9,7},{10,... | collective-permute-start | bytes 907784 | tf_op jit(solution)/shard_map/ppermute | solution.py:125
  18.7 0.0 collective-permute-done.3
  18.7 1.9 %collective-permute-start.4 = (bf16[2,197,384]{2,1,0:T(8,128)(2,1)S(1)}, bf16[2,197,384]{2,1,0:T(8,128)(2,1)S(1)}, u32[]{:S(2)}, u32[]{:S(2)}) collective-permute-start(bf16[2,197,384]{2,1,0:T(8,128)(2,1)S(1)} %collective-permute-done.3), channel_id=1, source_target_pairs={{0,14},{1,3},{2,0},{3,5},{4,2},{5,7},{6,4},{7,9},{8,6},{9,11},{10,... | collective-permute-start | bytes 907784 | tf_op jit(solution)/shard_map/ppermute | solution.py:126
  20.6 0.7 pad_maximum_fusion.1
  21.3 1.0 broadcast_in_dim.2
  22.3 13.2 %all-to-all-start = ((bf16[32,96,96]{2,1,0:T(8,128)(2,1)}), bf16[32,96,96]{2,1,0:T(8,128)(2,1)S(1)}, u32[]{:S(2)}, u32[]{:S(2)}) async-start(bf16[32,96,96]{2,1,0:T(8,128)(2,1)} %broadcast_in_dim.2), calls=%async_computation | async-start | bytes 1572864 | tf_op jit(solution)/shard_map/all_to_all | solution.py:156
  35.5 0.0 copy-start.4
  35.5 0.0 copy-start.5
  35.5 0.7 constant_dynamic-update-slice_fusion.9
  36.3 0.8 constant_dynamic-update-slice_fusion.8
  37.0 0.0 collective-permute-done.1
  37.0 5.1 %collective-permute-start.2 = (bf16[2,197,384]{2,1,0:T(8,128)(2,1)S(1)}, bf16[2,197,384]{2,1,0:T(8,128)(2,1)S(1)}, u32[]{:S(2)}, u32[]{:S(2)}) collective-permute-start(bf16[2,197,384]{2,1,0:T(8,128)(2,1)S(1)} %collective-permute-done.1), channel_id=1, source_target_pairs={{0,2},{1,15},{2,4},{3,1},{4,6},{5,3},{6,8},{7,5},{8,10},{9,7},{10,... | collective-permute-start | bytes 907784 | tf_op jit(solution)/shard_map/ppermute | solution.py:125
  42.1 0.0 collective-permute-done.4
  42.2 1.9 %collective-permute-start.5 = (bf16[2,197,384]{2,1,0:T(8,128)(2,1)S(1)}, bf16[2,197,384]{2,1,0:T(8,128)(2,1)S(1)}, u32[]{:S(2)}, u32[]{:S(2)}) collective-permute-start(bf16[2,197,384]{2,1,0:T(8,128)(2,1)S(1)} %collective-permute-done.4), channel_id=1, source_target_pairs={{0,14},{1,3},{2,0},{3,5},{4,2},{5,7},{6,4},{7,9},{8,6},{9,11},{10,... | collective-permute-start | bytes 907784 | tf_op jit(solution)/shard_map/ppermute | solution.py:126
  44.1 0.8 constant_dynamic-update-slice_fusion.7
  44.8 0.8 constant_dynamic-update-slice_fusion.6
  45.6 0.0 copy-done.4
  45.6 0.7 constant_dynamic-update-slice_fusion.5
  46.3 0.0 copy-done.5
  46.3 0.7 constant_dynamic-update-slice_fusion.4.own_ref
  47.0 1.9 %collective-permute-start.9 = (bf16[10,197,384]{2,1,0:T(8,128)(2,1)}, bf16[10,197,384]{2,1,0:T(8,128)(2,1)}, u32[]{:S(2)}, u32[]{:S(2)}) collective-permute-start(bf16[10,197,384]{2,1,0:T(8,128)(2,1)} %constant_dynamic-update-slice_fusion.4.own_ref), channel_id=1, source_target_pairs={{0,1},{1,0},{2,3},{3,2},{4,5},{5,4},{6,7},{7,6},{8,9},{9,8},{10,11... | collective-permute-start | bytes 4538888 | tf_op jit(solution)/shard_map/ppermute | solution.py:121
  48.9 0.0 collective-permute-done.2
  48.9 5.4 %collective-permute-start.6 = (bf16[1,197,384]{2,1,0:T(8,128)(2,1)S(1)}, bf16[1,197,384]{2,1,0:T(8,128)(2,1)S(1)}, u32[]{:S(2)}, u32[]{:S(2)}) collective-permute-start(bf16[1,197,384]{2,1,0:T(8,128)(2,1)S(1)} %slice.24), channel_id=1, source_target_pairs={{0,2},{1,15},{2,4},{3,1},{4,6},{5,3},{6,8},{7,5},{8,10},{9,7},{10,... | collective-permute-start | bytes 453896 | tf_op jit(solution)/shard_map/ppermute | solution.py:127
  54.4 0.0 collective-permute-done.5
  54.4 1.9 %collective-permute-start.7 = (bf16[1,197,384]{2,1,0:T(8,128)(2,1)S(1)}, bf16[1,197,384]{2,1,0:T(8,128)(2,1)S(1)}, u32[]{:S(2)}, u32[]{:S(2)}) collective-permute-start(bf16[1,197,384]{2,1,0:T(8,128)(2,1)S(1)} %slice.25), channel_id=1, source_target_pairs={{0,14},{1,3},{2,0},{3,5},{4,2},{5,7},{6,4},{7,9},{8,6},{9,11},{10,... | collective-permute-start | bytes 453896 | tf_op jit(solution)/shard_map/ppermute | solution.py:127
  56.4 0.1 constant_dynamic-update-slice_fusion.2
  56.4 1.1 collective-permute-done.6
  57.5 5.2 %collective-permute-done.7 = bf16[1,197,384]{2,1,0:T(8,128)(2,1)S(1)} collective-permute-done((bf16[1,197,384]{2,1,0:T(8,128)(2,1)S(1)}, bf16[1,197,384]{2,1,0:T(8,128)(2,1)S(1)}, u32[]{:S(2)}, u32[]{:S(2)}) %collective-permute-start.7) | collective-permute-done | bytes 151328 | tf_op jit(solution)/shard_map/ppermute | solution.py:127
  62.7 0.0 all-to-all-done.arrived_ref
  62.8 1.9 %collective-permute-start.8 = (bf16[6,197,384]{2,1,0:T(8,128)(2,1)S(1)}, bf16[6,197,384]{2,1,0:T(8,128)(2,1)S(1)}, u32[]{:S(2)}, u32[]{:S(2)}) collective-permute-start(bf16[6,197,384]{2,1,0:T(8,128)(2,1)S(1)} %constant_dynamic-update-slice_fusion.own_ref), channel_id=1, source_target_pairs={{0,1},{1,0},{2,3},{3,2},{4,5},{5,4},{6,7},{7,6},{8,9},{9,8},{10,11... | collective-permute-start | bytes 2723336 | tf_op jit(solution)/shard_map/ppermute | solution.py:121
  64.7 0.0 collective-permute-done.9.far_ref
  64.7 5.0 %shard_map.93 = (bf16[384,768]{1,0:T(8,128)(2,1)S(1)}, f32[192,768]{1,0:T(8,128)S(1)}, f32[192,768]{1,0:T(8,128)S(1)}, f32[192,768]{1,0:T(8,128)S(1)}, f32[192,768]{1,0:T(8,128)S(1)}) custom-call(s32[1]{0:T(128)} %bitcast.core_ref, bf16[10,197,384]{2,1,0:T(8,128)(2,1)} %constant_dynamic-update-slice_fusion.4.own_ref, ...), custom_call_target="tpu_custom_call" | custom-call | flops 1161953280 | bytes 3025920 | tf_op jit(solution)/shard_map/pallas_call | solution.py:95
  69.7 0.0 collective-permute-done.8.far_ref
  69.7 2.5 %shard_map.94 = bf16[2,2,8,48,384]{4,3,2,1,0:T(8,128)(2,1)S(1)} custom-call(s32[1]{0:T(128)} %bitcast.core_ref, bf16[6,197,384]{2,1,0:T(8,128)(2,1)S(1)} %constant_dynamic-update-slice_fusion.own_ref, bf16[6,197,384]{2,1,0:T(8,128)(2,1)S(1)} %collective-permute-done.8.far_ref, bf16[384,768]{1,0:T(8,128)(2,1)S(1)} %get-tuple-element.19.turned_ref, ...), custom_call_target="tpu_custom_call" | custom-call | flops 697171968 | bytes 1815552 | tf_op jit(solution)/shard_map/pallas_call | solution.py:95
  72.2 21.0 %all_to_all.15 = bf16[4,8,48,384]{3,2,1,0:T(8,128)(2,1)S(1)} all-to-all(bf16[4,8,48,384]{3,2,1,0:T(8,128)(2,1)S(1)} %bitcast.12), channel_id=1, replica_groups=mesh['z'=8,'xlo'=2,'xhi'=2,'y'=8,'core'=2] {'xlo','xhi'}, dimensions={0} | all-to-all | bytes 2359296 | tf_op jit(solution)/shard_map/all_to_all | solution.py:166
  93.2 0.0 copy-start
  93.2 0.0 copy-start.1
  93.2 0.2 fusion
  93.3 18.6 %all_to_all.16.pieces_ref = bf16[8,48,384]{2,1,0:T(8,128)(2,1)S(1)} all-to-all(bf16[8,48,384]{2,1,0:T(8,128)(2,1)S(1)} %fusion), channel_id=1, replica_groups=mesh['z'=8,'xlo'=2,'xhi'=2,'y'=8,'core'=2] {'z'}, dimensions={0} | all-to-all | bytes 589824 | tf_op jit(solution)/shard_map/all_to_all | solution.py:168
  111.9 0.0 copy-done
  111.9 0.0 copy-done.1
  111.9 0.0 copy-done.2
  111.9 0.0 copy-done.3
  111.9 0.8 shard_map.95
  (7 shorter events, 0.1 us)
Async XLA Ops:
  1.7 11.4 %collective-permute-start = (bf16[2,197,384]{2,1,0:T(8,128)(2,1)S(1)}, bf16[2,197,384]{2,1,0:T(8,128)(2,1)S(1)}, u32[]{:S(2)}, u32[]{:S(2)}) collective-permute-start(bf16[2,197,384]{2,1,0:T(8,128)(2,1)S(1)} %pad_maximum_fusion), channel_id=1, source_target_pairs={{0,2},{1,15},{2,4},{3,1},{4,6},{5,3},{6,8},{7,5},{8,10},{9,7},{10,... | collective-permute-start | bytes 907784 | tf_op jit(solution)/shard_map/ppermute | solution.py:125
  6.4 12.3 %collective-permute-start.3 = (bf16[2,197,384]{2,1,0:T(8,128)(2,1)S(1)}, bf16[2,197,384]{2,1,0:T(8,128)(2,1)S(1)}, u32[]{:S(2)}, u32[]{:S(2)}) collective-permute-start(bf16[2,197,384]{2,1,0:T(8,128)(2,1)S(1)} %pad_maximum_fusion), channel_id=1, source_target_pairs={{0,14},{1,3},{2,0},{3,5},{4,2},{5,7},{6,4},{7,9},{8,6},{9,11},{10,... | collective-permute-start | bytes 907784 | tf_op jit(solution)/shard_map/ppermute | solution.py:126
  13.1 24.0 %collective-permute-start.1 = (bf16[2,197,384]{2,1,0:T(8,128)(2,1)S(1)}, bf16[2,197,384]{2,1,0:T(8,128)(2,1)S(1)}, u32[]{:S(2)}, u32[]{:S(2)}) collective-permute-start(bf16[2,197,384]{2,1,0:T(8,128)(2,1)S(1)} %collective-permute-done), channel_id=1, source_target_pairs={{0,2},{1,15},{2,4},{3,1},{4,6},{5,3},{6,8},{7,5},{8,10},{9,7},{10,... | collective-permute-start | bytes 907784 | tf_op jit(solution)/shard_map/ppermute | solution.py:125
  18.7 23.5 %collective-permute-start.4 = (bf16[2,197,384]{2,1,0:T(8,128)(2,1)S(1)}, bf16[2,197,384]{2,1,0:T(8,128)(2,1)S(1)}, u32[]{:S(2)}, u32[]{:S(2)}) collective-permute-start(bf16[2,197,384]{2,1,0:T(8,128)(2,1)S(1)} %collective-permute-done.3), channel_id=1, source_target_pairs={{0,14},{1,3},{2,0},{3,5},{4,2},{5,7},{6,4},{7,9},{8,6},{9,11},{10,... | collective-permute-start | bytes 907784 | tf_op jit(solution)/shard_map/ppermute | solution.py:126
  22.3 40.4 %all-to-all-start = ((bf16[32,96,96]{2,1,0:T(8,128)(2,1)}), bf16[32,96,96]{2,1,0:T(8,128)(2,1)S(1)}, u32[]{:S(2)}, u32[]{:S(2)}) async-start(bf16[32,96,96]{2,1,0:T(8,128)(2,1)} %broadcast_in_dim.2), calls=%async_computation | async-start | bytes 1572864 | tf_op jit(solution)/shard_map/all_to_all | solution.py:156
  35.5 10.1 %copy-start.4 = (bf16[197,384]{1,0:T(8,128)(2,1)S(1)}, bf16[197,384]{1,0:T(8,128)(2,1)}, u32[]{:S(2)}) copy-start(bf16[197,384]{1,0:T(8,128)(2,1)} %param.6) | copy-start | bytes 453892
  35.5 10.8 %copy-start.5 = (bf16[197,384]{1,0:T(8,128)(2,1)S(1)}, bf16[197,384]{1,0:T(8,128)(2,1)}, u32[]{:S(2)}) copy-start(bf16[197,384]{1,0:T(8,128)(2,1)} %param.7) | copy-start | bytes 453892
  37.0 11.9 %collective-permute-start.2 = (bf16[2,197,384]{2,1,0:T(8,128)(2,1)S(1)}, bf16[2,197,384]{2,1,0:T(8,128)(2,1)S(1)}, u32[]{:S(2)}, u32[]{:S(2)}) collective-permute-start(bf16[2,197,384]{2,1,0:T(8,128)(2,1)S(1)} %collective-permute-done.1), channel_id=1, source_target_pairs={{0,2},{1,15},{2,4},{3,1},{4,6},{5,3},{6,8},{7,5},{8,10},{9,7},{10,... | collective-permute-start | bytes 907784 | tf_op jit(solution)/shard_map/ppermute | solution.py:125
  42.2 12.2 %collective-permute-start.5 = (bf16[2,197,384]{2,1,0:T(8,128)(2,1)S(1)}, bf16[2,197,384]{2,1,0:T(8,128)(2,1)S(1)}, u32[]{:S(2)}, u32[]{:S(2)}) collective-permute-start(bf16[2,197,384]{2,1,0:T(8,128)(2,1)S(1)} %collective-permute-done.4), channel_id=1, source_target_pairs={{0,14},{1,3},{2,0},{3,5},{4,2},{5,7},{6,4},{7,9},{8,6},{9,11},{10,... | collective-permute-start | bytes 907784 | tf_op jit(solution)/shard_map/ppermute | solution.py:126
  47.0 17.8 %collective-permute-start.9 = (bf16[10,197,384]{2,1,0:T(8,128)(2,1)}, bf16[10,197,384]{2,1,0:T(8,128)(2,1)}, u32[]{:S(2)}, u32[]{:S(2)}) collective-permute-start(bf16[10,197,384]{2,1,0:T(8,128)(2,1)} %constant_dynamic-update-slice_fusion.4.own_ref), channel_id=1, source_target_pairs={{0,1},{1,0},{2,3},{3,2},{4,5},{5,4},{6,7},{7,6},{8,9},{9,8},{10,11... | collective-permute-start | bytes 4538888 | tf_op jit(solution)/shard_map/ppermute | solution.py:121
  48.9 8.6 %collective-permute-start.6 = (bf16[1,197,384]{2,1,0:T(8,128)(2,1)S(1)}, bf16[1,197,384]{2,1,0:T(8,128)(2,1)S(1)}, u32[]{:S(2)}, u32[]{:S(2)}) collective-permute-start(bf16[1,197,384]{2,1,0:T(8,128)(2,1)S(1)} %slice.24), channel_id=1, source_target_pairs={{0,2},{1,15},{2,4},{3,1},{4,6},{5,3},{6,8},{7,5},{8,10},{9,7},{10,... | collective-permute-start | bytes 453896 | tf_op jit(solution)/shard_map/ppermute | solution.py:127
  54.4 8.3 %collective-permute-start.7 = (bf16[1,197,384]{2,1,0:T(8,128)(2,1)S(1)}, bf16[1,197,384]{2,1,0:T(8,128)(2,1)S(1)}, u32[]{:S(2)}, u32[]{:S(2)}) collective-permute-start(bf16[1,197,384]{2,1,0:T(8,128)(2,1)S(1)} %slice.25), channel_id=1, source_target_pairs={{0,14},{1,3},{2,0},{3,5},{4,2},{5,7},{6,4},{7,9},{8,6},{9,11},{10,... | collective-permute-start | bytes 453896 | tf_op jit(solution)/shard_map/ppermute | solution.py:127
  62.8 6.9 %collective-permute-start.8 = (bf16[6,197,384]{2,1,0:T(8,128)(2,1)S(1)}, bf16[6,197,384]{2,1,0:T(8,128)(2,1)S(1)}, u32[]{:S(2)}, u32[]{:S(2)}) collective-permute-start(bf16[6,197,384]{2,1,0:T(8,128)(2,1)S(1)} %constant_dynamic-update-slice_fusion.own_ref), channel_id=1, source_target_pairs={{0,1},{1,0},{2,3},{3,2},{4,5},{5,4},{6,7},{7,6},{8,9},{9,8},{10,11... | collective-permute-start | bytes 2723336 | tf_op jit(solution)/shard_map/ppermute | solution.py:121
  93.2 18.8 %copy-start = (bf16[96,48]{0,1:T(8,128)(2,1)S(1)}, bf16[96,48]{0,1:T(8,128)(2,1)}, u32[]{:S(2)}) copy-start(bf16[96,48]{0,1:T(8,128)(2,1)} %param.9) | copy-start | bytes 27652
  93.2 18.8 %copy-start.1 = (bf16[48,96]{1,0:T(8,128)(2,1)S(1)}, bf16[48,96]{1,0:T(8,128)(2,1)}, u32[]{:S(2)}) copy-start(bf16[48,96]{1,0:T(8,128)(2,1)} %w_in_ref.1) | copy-start | bytes 27652
  93.2 18.8 %copy-start.2 = (f32[48,96]{1,0:T(8,128)S(1)}, f32[48,96]{1,0:T(8,128)}, u32[]{:S(2)}) copy-start(f32[48,96]{1,0:T(8,128)} %prec_in_ref.1) | copy-start | bytes 55300
  93.2 18.8 %copy-start.3 = (f32[96,48]{0,1:T(8,128)S(1)}, f32[96,48]{0,1:T(8,128)}, u32[]{:S(2)}) copy-start(f32[96,48]{0,1:T(8,128)} %param.11) | copy-start | bytes 55300

commit v13 on v12

--- a/solution.py
+++ b/solution.py
@@ -154,7 +154,7 @@
     both = jnp.concatenate([w_in, w_out.T], axis=0)
     both = jnp.broadcast_to(both[None], (cols * dp, *both.shape))
     arrived = lax.all_to_all(both, OWNERS, 0, 0, tiled=True)
-    early, late, arrived = round_the_ring(jnp.stack([inputs, cotangent]), arrived)
+    early, late, arrived = round_the_ring(lax.optimization_barrier(jnp.stack([inputs, cotangent])), arrived)
     core = lax.axis_index("core").reshape(1).astype(jnp.int32)
     partial = [jax.ShapeDtypeStruct((hid, dp * d_own), F32)] * 4
     packed = jax.ShapeDtypeStruct((pairs, cols, deep, d_own, 4 * h_own), BF16)

time: 113 us -> 113 us (level)
    unnamed x20 -> x15, local copies, waits for them, and re-layouts: 3.82 us -> 3.14 us
  transfers between devices with their start and end apart: 11 -> 11, of which waited for: 3 -> 4; matrix products, arithmetic and copies ran while one was open for 6% -> 5% of each run, Pallas kernels for 4% -> 4%
where the time goes in v13:
time: 113 us
  starting transfers between devices  45.7 us (40%)
  blocking collectives  39.5 us (35%)
  waiting for transfers between devices  11.6 us (10%)
  Pallas kernels  8.29 us (7%)
  local copies, waits for them, and re-layouts  4.93 us (4%)
  other arithmetic  1.91 us (2%)
    all_to_all x1, blocking collectives, per_device(): pieces = lax.all_to_all(pieces, ROW, 0, 0, tiled=True)  21 us
    all_to_all x1, blocking collectives, per_device(): pieces = lax.all_to_all(pieces, 'z', 0, 0, tiled=True)  18.6 us
    ppermute x3, starting transfers between devices, round_the_ring(): up.append(lax.ppermute(up[-1], GROUP, turned(1)))  15.4 us
    all_to_all x1, starting transfers between devices, per_device(): arrived = lax.all_to_all(both, OWNERS, 0, 0, tiled=True)  13.2 us
    pallas_call x2, Pallas kernels, run_images(): pl.pallas_call(kernel, in_specs=[pl.BlockSpec(memory_space=pltpu.SMEM)] +...  7.44 us
    ppermute x3, starting transfers between devices, round_the_ring(): down.append(lax.ppermute(down[-1], GROUP, turned(-1)))  5.76 us
    ppermute x1, starting transfers between devices, round_the_ring(): lax.ppermute(up[3][:1], GROUP, turned(1))  5.6 us
    ppermute x3, waiting for transfers between devices, round_the_ring(): up.append(lax.ppermute(up[-1], GROUP, turned(1)))  5.25 us
  transfers between devices with their start and end apart: 11, of which 4 were waited for; matrix products, arithmetic and copies ran while one was open for 5% of the time, Pallas kernels for 4%

profile of v13, /device:TPU:24, one launch (start us, length us, event | category | flops | bytes accessed | tf_op | source)
XLA Modules:
  0.0 112.8 jit_solution(5524605175323079163)
XLA Ops:
  0.6 1.0 pad_maximum_fusion
  1.7 4.7 %collective-permute-start = (bf16[2,197,384]{2,1,0:T(8,128)(2,1)S(1)}, bf16[2,197,384]{2,1,0:T(8,128)(2,1)S(1)}, u32[]{:S(2)}, u32[]{:S(2)}) collective-permute-start(bf16[2,197,384]{2,1,0:T(8,128)(2,1)S(1)} %pad_maximum_fusion), channel_id=1, source_target_pairs={{0,2},{1,15},{2,4},{3,1},{4,6},{5,3},{6,8},{7,5},{8,10},{9,7},{10,... | collective-permute-start | bytes 907784 | tf_op jit(solution)/shard_map/ppermute | solution.py:125
  6.4 1.9 %collective-permute-start.3 = (bf16[2,197,384]{2,1,0:T(8,128)(2,1)S(1)}, bf16[2,197,384]{2,1,0:T(8,128)(2,1)S(1)}, u32[]{:S(2)}, u32[]{:S(2)}) collective-permute-start(bf16[2,197,384]{2,1,0:T(8,128)(2,1)S(1)} %pad_maximum_fusion), channel_id=1, source_target_pairs={{0,14},{1,3},{2,0},{3,5},{4,2},{5,7},{6,4},{7,9},{8,6},{9,11},{10,... | collective-permute-start | bytes 907784 | tf_op jit(solution)/shard_map/ppermute | solution.py:126
  8.3 4.8 %collective-permute-done = bf16[2,197,384]{2,1,0:T(8,128)(2,1)S(1)} collective-permute-done((bf16[2,197,384]{2,1,0:T(8,128)(2,1)S(1)}, bf16[2,197,384]{2,1,0:T(8,128)(2,1)S(1)}, u32[]{:S(2)}, u32[]{:S(2)}) %collective-permute-start) | collective-permute-done | bytes 302624 | tf_op jit(solution)/shard_map/ppermute | solution.py:125
  13.1 5.6 %collective-permute-start.1 = (bf16[2,197,384]{2,1,0:T(8,128)(2,1)S(1)}, bf16[2,197,384]{2,1,0:T(8,128)(2,1)S(1)}, u32[]{:S(2)}, u32[]{:S(2)}) collective-permute-start(bf16[2,197,384]{2,1,0:T(8,128)(2,1)S(1)} %collective-permute-done), channel_id=1, source_target_pairs={{0,2},{1,15},{2,4},{3,1},{4,6},{5,3},{6,8},{7,5},{8,10},{9,7},{10,... | collective-permute-start | bytes 907784 | tf_op jit(solution)/shard_map/ppermute | solution.py:125
  18.7 0.0 collective-permute-done.3
  18.7 1.9 %collective-permute-start.4 = (bf16[2,197,384]{2,1,0:T(8,128)(2,1)S(1)}, bf16[2,197,384]{2,1,0:T(8,128)(2,1)S(1)}, u32[]{:S(2)}, u32[]{:S(2)}) collective-permute-start(bf16[2,197,384]{2,1,0:T(8,128)(2,1)S(1)} %collective-permute-done.3), channel_id=1, source_target_pairs={{0,14},{1,3},{2,0},{3,5},{4,2},{5,7},{6,4},{7,9},{8,6},{9,11},{10,... | collective-permute-start | bytes 907784 | tf_op jit(solution)/shard_map/ppermute | solution.py:126
  20.6 0.7 pad_maximum_fusion.1
  21.3 1.0 broadcast_in_dim.2
  22.3 13.2 %all-to-all-start = ((bf16[32,96,96]{2,1,0:T(8,128)(2,1)}), bf16[32,96,96]{2,1,0:T(8,128)(2,1)S(1)}, u32[]{:S(2)}, u32[]{:S(2)}) async-start(bf16[32,96,96]{2,1,0:T(8,128)(2,1)} %broadcast_in_dim.2), calls=%async_computation | async-start | bytes 1572864 | tf_op jit(solution)/shard_map/all_to_all | solution.py:156
  35.5 0.7 constant_dynamic-update-slice_fusion.8
  36.2 0.8 constant_dynamic-update-slice_fusion.7
  37.0 0.0 collective-permute-done.1
  37.0 5.1 %collective-permute-start.2 = (bf16[2,197,384]{2,1,0:T(8,128)(2,1)S(1)}, bf16[2,197,384]{2,1,0:T(8,128)(2,1)S(1)}, u32[]{:S(2)}, u32[]{:S(2)}) collective-permute-start(bf16[2,197,384]{2,1,0:T(8,128)(2,1)S(1)} %collective-permute-done.1), channel_id=1, source_target_pairs={{0,2},{1,15},{2,4},{3,1},{4,6},{5,3},{6,8},{7,5},{8,10},{9,7},{10,... | collective-permute-start | bytes 907784 | tf_op jit(solution)/shard_map/ppermute | solution.py:125
  42.1 0.0 collective-permute-done.4
  42.1 1.9 %collective-permute-start.5 = (bf16[2,197,384]{2,1,0:T(8,128)(2,1)S(1)}, bf16[2,197,384]{2,1,0:T(8,128)(2,1)S(1)}, u32[]{:S(2)}, u32[]{:S(2)}) collective-permute-start(bf16[2,197,384]{2,1,0:T(8,128)(2,1)S(1)} %collective-permute-done.4), channel_id=1, source_target_pairs={{0,14},{1,3},{2,0},{3,5},{4,2},{5,7},{6,4},{7,9},{8,6},{9,11},{10,... | collective-permute-start | bytes 907784 | tf_op jit(solution)/shard_map/ppermute | solution.py:126
  44.1 0.7 constant_dynamic-update-slice_fusion.6
  44.8 0.8 constant_dynamic-update-slice_fusion.5
  45.6 0.7 constant_dynamic-update-slice_fusion.4.own_ref
  46.3 1.9 %collective-permute-start.9 = (bf16[10,197,384]{2,1,0:T(8,128)(2,1)}, bf16[10,197,384]{2,1,0:T(8,128)(2,1)}, u32[]{:S(2)}, u32[]{:S(2)}) collective-permute-start(bf16[10,197,384]{2,1,0:T(8,128)(2,1)} %constant_dynamic-update-slice_fusion.4.own_ref), channel_id=1, source_target_pairs={{0,1},{1,0},{2,3},{3,2},{4,5},{5,4},{6,7},{7,6},{8,9},{9,8},{10,11... | collective-permute-start | bytes 4538888 | tf_op jit(solution)/shard_map/ppermute | solution.py:121
  48.2 0.5 collective-permute-done.2
  48.7 5.6 %collective-permute-start.6 = (bf16[1,197,384]{2,1,0:T(8,128)(2,1)S(1)}, bf16[1,197,384]{2,1,0:T(8,128)(2,1)S(1)}, u32[]{:S(2)}, u32[]{:S(2)}) collective-permute-start(bf16[1,197,384]{2,1,0:T(8,128)(2,1)S(1)} %slice.24), channel_id=1, source_target_pairs={{0,2},{1,15},{2,4},{3,1},{4,6},{5,3},{6,8},{7,5},{8,10},{9,7},{10,... | collective-permute-start | bytes 453896 | tf_op jit(solution)/shard_map/ppermute | solution.py:127
  54.4 0.0 collective-permute-done.5
  54.4 1.9 %collective-permute-start.7 = (bf16[1,197,384]{2,1,0:T(8,128)(2,1)S(1)}, bf16[1,197,384]{2,1,0:T(8,128)(2,1)S(1)}, u32[]{:S(2)}, u32[]{:S(2)}) collective-permute-start(bf16[1,197,384]{2,1,0:T(8,128)(2,1)S(1)} %slice.25), channel_id=1, source_target_pairs={{0,14},{1,3},{2,0},{3,5},{4,2},{5,7},{6,4},{7,9},{8,6},{9,11},{10,... | collective-permute-start | bytes 453896 | tf_op jit(solution)/shard_map/ppermute | solution.py:127
  56.4 0.1 constant_dynamic-update-slice_fusion.2
  56.4 1.8 %collective-permute-done.6 = bf16[1,197,384]{2,1,0:T(8,128)(2,1)S(1)} collective-permute-done((bf16[1,197,384]{2,1,0:T(8,128)(2,1)S(1)}, bf16[1,197,384]{2,1,0:T(8,128)(2,1)S(1)}, u32[]{:S(2)}, u32[]{:S(2)}) %collective-permute-start.6) | collective-permute-done | bytes 151328 | tf_op jit(solution)/shard_map/ppermute | solution.py:127
  58.2 4.5 %collective-permute-done.7 = bf16[1,197,384]{2,1,0:T(8,128)(2,1)S(1)} collective-permute-done((bf16[1,197,384]{2,1,0:T(8,128)(2,1)S(1)}, bf16[1,197,384]{2,1,0:T(8,128)(2,1)S(1)}, u32[]{:S(2)}, u32[]{:S(2)}) %collective-permute-start.7) | collective-permute-done | bytes 151328 | tf_op jit(solution)/shard_map/ppermute | solution.py:127
  62.7 0.0 all-to-all-done.arrived_ref
  62.8 1.9 %collective-permute-start.8 = (bf16[6,197,384]{2,1,0:T(8,128)(2,1)S(1)}, bf16[6,197,384]{2,1,0:T(8,128)(2,1)S(1)}, u32[]{:S(2)}, u32[]{:S(2)}) collective-permute-start(bf16[6,197,384]{2,1,0:T(8,128)(2,1)S(1)} %constant_dynamic-update-slice_fusion.own_ref), channel_id=1, source_target_pairs={{0,1},{1,0},{2,3},{3,2},{4,5},{5,4},{6,7},{7,6},{8,9},{9,8},{10,11... | collective-permute-start | bytes 2723336 | tf_op jit(solution)/shard_map/ppermute | solution.py:121
  64.7 0.0 collective-permute-done.9.far_ref
  64.7 5.0 %shard_map.93 = (bf16[384,768]{1,0:T(8,128)(2,1)S(1)}, f32[192,768]{1,0:T(8,128)S(1)}, f32[192,768]{1,0:T(8,128)S(1)}, f32[192,768]{1,0:T(8,128)S(1)}, f32[192,768]{1,0:T(8,128)S(1)}) custom-call(s32[1]{0:T(128)} %bitcast.core_ref, bf16[10,197,384]{2,1,0:T(8,128)(2,1)} %constant_dynamic-update-slice_fusion.4.own_ref, ...), custom_call_target="tpu_custom_call" | custom-call | flops 1161953280 | bytes 3025920 | tf_op jit(solution)/shard_map/pallas_call | solution.py:95
  69.7 0.0 collective-permute-done.8.far_ref
  69.7 2.5 %shard_map.94 = bf16[2,2,8,48,384]{4,3,2,1,0:T(8,128)(2,1)S(1)} custom-call(s32[1]{0:T(128)} %bitcast.core_ref, bf16[6,197,384]{2,1,0:T(8,128)(2,1)S(1)} %constant_dynamic-update-slice_fusion.own_ref, bf16[6,197,384]{2,1,0:T(8,128)(2,1)S(1)} %collective-permute-done.8.far_ref, bf16[384,768]{1,0:T(8,128)(2,1)S(1)} %get-tuple-element.19.turned_ref, ...), custom_call_target="tpu_custom_call" | custom-call | flops 697171968 | bytes 1815552 | tf_op jit(solution)/shard_map/pallas_call | solution.py:95
  72.2 21.0 %all_to_all.15 = bf16[4,8,48,384]{3,2,1,0:T(8,128)(2,1)S(1)} all-to-all(bf16[4,8,48,384]{3,2,1,0:T(8,128)(2,1)S(1)} %bitcast.10), channel_id=1, replica_groups=mesh['z'=8,'xlo'=2,'xhi'=2,'y'=8,'core'=2] {'xlo','xhi'}, dimensions={0} | all-to-all | bytes 2359296 | tf_op jit(solution)/shard_map/all_to_all | solution.py:166
  93.1 0.0 copy-start
  93.1 0.0 copy-start.1
  93.1 0.0 copy-start.2
  93.1 0.0 copy-start.3
  93.1 0.2 fusion
  93.3 18.6 %all_to_all.16.pieces_ref = bf16[8,48,384]{2,1,0:T(8,128)(2,1)S(1)} all-to-all(bf16[8,48,384]{2,1,0:T(8,128)(2,1)S(1)} %fusion), channel_id=1, replica_groups=mesh['z'=8,'xlo'=2,'xhi'=2,'y'=8,'core'=2] {'z'}, dimensions={0} | all-to-all | bytes 589824 | tf_op jit(solution)/shard_map/all_to_all | solution.py:168
  111.9 0.0 copy-done
  111.9 0.0 copy-done.1
  111.9 0.0 copy-done.2
  111.9 0.0 copy-done.3
  111.9 0.8 shard_map.95
  (5 shorter events, 0.1 us)
Async XLA Ops:
  1.7 11.4 %collective-permute-start = (bf16[2,197,384]{2,1,0:T(8,128)(2,1)S(1)}, bf16[2,197,384]{2,1,0:T(8,128)(2,1)S(1)}, u32[]{:S(2)}, u32[]{:S(2)}) collective-permute-start(bf16[2,197,384]{2,1,0:T(8,128)(2,1)S(1)} %pad_maximum_fusion), channel_id=1, source_target_pairs={{0,2},{1,15},{2,4},{3,1},{4,6},{5,3},{6,8},{7,5},{8,10},{9,7},{10,... | collective-permute-start | bytes 907784 | tf_op jit(solution)/shard_map/ppermute | solution.py:125
  6.4 12.3 %collective-permute-start.3 = (bf16[2,197,384]{2,1,0:T(8,128)(2,1)S(1)}, bf16[2,197,384]{2,1,0:T(8,128)(2,1)S(1)}, u32[]{:S(2)}, u32[]{:S(2)}) collective-permute-start(bf16[2,197,384]{2,1,0:T(8,128)(2,1)S(1)} %pad_maximum_fusion), channel_id=1, source_target_pairs={{0,14},{1,3},{2,0},{3,5},{4,2},{5,7},{6,4},{7,9},{8,6},{9,11},{10,... | collective-permute-start | bytes 907784 | tf_op jit(solution)/shard_map/ppermute | solution.py:126
  13.1 23.9 %collective-permute-start.1 = (bf16[2,197,384]{2,1,0:T(8,128)(2,1)S(1)}, bf16[2,197,384]{2,1,0:T(8,128)(2,1)S(1)}, u32[]{:S(2)}, u32[]{:S(2)}) collective-permute-start(bf16[2,197,384]{2,1,0:T(8,128)(2,1)S(1)} %collective-permute-done), channel_id=1, source_target_pairs={{0,2},{1,15},{2,4},{3,1},{4,6},{5,3},{6,8},{7,5},{8,10},{9,7},{10,... | collective-permute-start | bytes 907784 | tf_op jit(solution)/shard_map/ppermute | solution.py:125
  18.7 23.5 %collective-permute-start.4 = (bf16[2,197,384]{2,1,0:T(8,128)(2,1)S(1)}, bf16[2,197,384]{2,1,0:T(8,128)(2,1)S(1)}, u32[]{:S(2)}, u32[]{:S(2)}) collective-permute-start(bf16[2,197,384]{2,1,0:T(8,128)(2,1)S(1)} %collective-permute-done.3), channel_id=1, source_target_pairs={{0,14},{1,3},{2,0},{3,5},{4,2},{5,7},{6,4},{7,9},{8,6},{9,11},{10,... | collective-permute-start | bytes 907784 | tf_op jit(solution)/shard_map/ppermute | solution.py:126
  22.3 40.4 %all-to-all-start = ((bf16[32,96,96]{2,1,0:T(8,128)(2,1)}), bf16[32,96,96]{2,1,0:T(8,128)(2,1)S(1)}, u32[]{:S(2)}, u32[]{:S(2)}) async-start(bf16[32,96,96]{2,1,0:T(8,128)(2,1)} %broadcast_in_dim.2), calls=%async_computation | async-start | bytes 1572864 | tf_op jit(solution)/shard_map/all_to_all | solution.py:156
  37.0 11.7 %collective-permute-start.2 = (bf16[2,197,384]{2,1,0:T(8,128)(2,1)S(1)}, bf16[2,197,384]{2,1,0:T(8,128)(2,1)S(1)}, u32[]{:S(2)}, u32[]{:S(2)}) collective-permute-start(bf16[2,197,384]{2,1,0:T(8,128)(2,1)S(1)} %collective-permute-done.1), channel_id=1, source_target_pairs={{0,2},{1,15},{2,4},{3,1},{4,6},{5,3},{6,8},{7,5},{8,10},{9,7},{10,... | collective-permute-start | bytes 907784 | tf_op jit(solution)/shard_map/ppermute | solution.py:125
  42.1 12.2 %collective-permute-start.5 = (bf16[2,197,384]{2,1,0:T(8,128)(2,1)S(1)}, bf16[2,197,384]{2,1,0:T(8,128)(2,1)S(1)}, u32[]{:S(2)}, u32[]{:S(2)}) collective-permute-start(bf16[2,197,384]{2,1,0:T(8,128)(2,1)S(1)} %collective-permute-done.4), channel_id=1, source_target_pairs={{0,14},{1,3},{2,0},{3,5},{4,2},{5,7},{6,4},{7,9},{8,6},{9,11},{10,... | collective-permute-start | bytes 907784 | tf_op jit(solution)/shard_map/ppermute | solution.py:126
  46.3 18.4 %collective-permute-start.9 = (bf16[10,197,384]{2,1,0:T(8,128)(2,1)}, bf16[10,197,384]{2,1,0:T(8,128)(2,1)}, u32[]{:S(2)}, u32[]{:S(2)}) collective-permute-start(bf16[10,197,384]{2,1,0:T(8,128)(2,1)} %constant_dynamic-update-slice_fusion.4.own_ref), channel_id=1, source_target_pairs={{0,1},{1,0},{2,3},{3,2},{4,5},{5,4},{6,7},{7,6},{8,9},{9,8},{10,11... | collective-permute-start | bytes 4538888 | tf_op jit(solution)/shard_map/ppermute | solution.py:121
  48.7 9.5 %collective-permute-start.6 = (bf16[1,197,384]{2,1,0:T(8,128)(2,1)S(1)}, bf16[1,197,384]{2,1,0:T(8,128)(2,1)S(1)}, u32[]{:S(2)}, u32[]{:S(2)}) collective-permute-start(bf16[1,197,384]{2,1,0:T(8,128)(2,1)S(1)} %slice.24), channel_id=1, source_target_pairs={{0,2},{1,15},{2,4},{3,1},{4,6},{5,3},{6,8},{7,5},{8,10},{9,7},{10,... | collective-permute-start | bytes 453896 | tf_op jit(solution)/shard_map/ppermute | solution.py:127
  54.4 8.3 %collective-permute-start.7 = (bf16[1,197,384]{2,1,0:T(8,128)(2,1)S(1)}, bf16[1,197,384]{2,1,0:T(8,128)(2,1)S(1)}, u32[]{:S(2)}, u32[]{:S(2)}) collective-permute-start(bf16[1,197,384]{2,1,0:T(8,128)(2,1)S(1)} %slice.25), channel_id=1, source_target_pairs={{0,14},{1,3},{2,0},{3,5},{4,2},{5,7},{6,4},{7,9},{8,6},{9,11},{10,... | collective-permute-start | bytes 453896 | tf_op jit(solution)/shard_map/ppermute | solution.py:127
  62.8 6.9 %collective-permute-start.8 = (bf16[6,197,384]{2,1,0:T(8,128)(2,1)S(1)}, bf16[6,197,384]{2,1,0:T(8,128)(2,1)S(1)}, u32[]{:S(2)}, u32[]{:S(2)}) collective-permute-start(bf16[6,197,384]{2,1,0:T(8,128)(2,1)S(1)} %constant_dynamic-update-slice_fusion.own_ref), channel_id=1, source_target_pairs={{0,1},{1,0},{2,3},{3,2},{4,5},{5,4},{6,7},{7,6},{8,9},{9,8},{10,11... | collective-permute-start | bytes 2723336 | tf_op jit(solution)/shard_map/ppermute | solution.py:121
  93.1 18.8 %copy-start = (bf16[96,48]{0,1:T(8,128)(2,1)S(1)}, bf16[96,48]{0,1:T(8,128)(2,1)}, u32[]{:S(2)}) copy-start(bf16[96,48]{0,1:T(8,128)(2,1)} %param.9) | copy-start | bytes 27652
  93.1 18.8 %copy-start.1 = (bf16[48,96]{1,0:T(8,128)(2,1)S(1)}, bf16[48,96]{1,0:T(8,128)(2,1)}, u32[]{:S(2)}) copy-start(bf16[48,96]{1,0:T(8,128)(2,1)} %w_in_ref.1) | copy-start | bytes 27652
  93.1 18.8 %copy-start.2 = (f32[48,96]{1,0:T(8,128)S(1)}, f32[48,96]{1,0:T(8,128)}, u32[]{:S(2)}) copy-start(f32[48,96]{1,0:T(8,128)} %prec_in_ref.1) | copy-start | bytes 55300
  93.1 18.8 %copy-start.3 = (f32[96,48]{0,1:T(8,128)S(1)}, f32[96,48]{0,1:T(8,128)}, u32[]{:S(2)}) copy-start(f32[96,48]{0,1:T(8,128)} %param.11) | copy-start | bytes 55300
